TPU v7x, 32 devices: a whole 2x2x4 slice. The times are simulated.
32 devices in a mesh: mem: 8 (over z, y), lev: 4 (over x, core).
Axes of the slice: x: 2, y: 2, z: 4, core: 2. Of those that a mesh axis runs over, the one named last changes fastest.
Arguments:
- prior_ensemble_stack: float32 [16, 20, 64, 512], P('mem', 'lev'), may hold values from -6 to 6
- vertical_cfl_ratio: float32 [20, 64, 512], P('lev'), may hold values from -0.35 to 0.35
- horizontal_cfl_ratio: float32 [20, 64, 512], P('lev'), may hold values from -0.35 to 0.35
- spreading_coefficient: float32 [20], P('lev'), may hold values from 0.02 to 0.2
- obs_cells: int32 [2, 16], replicated, may hold values from 0 to 32767
- obs_slabs: int32 [2, 16], replicated, may hold values from 0 to 19
- obs_values: float32 [2, 16], replicated, may hold values from -6 to 6
- obs_error: float32 [2, 16], replicated, may hold values from 0.25 to 2
Outputs:
- analysis: float32 [16, 20, 64, 512], P('mem', 'lev')
All inputs are finite; a program needn't handle non-finite values.
Results may differ from a plain program's by a relative error of at most 0.0001.
Values sent between devices are 32-bit elements; how exact they have to be, the bound alone decides.
No kernel may reach another device: no remote copies, remote signals or barrier semaphores. Data moves between devices by JAX's collectives and lax.ppermute only.
A program may use at most 256 MiB of HBM per device.

v0:
```python
import jax
import jax.numpy as jnp
from jax import lax
from jax.sharding import PartitionSpec as P

NX = 512
STEPS = 2
LOC_HALF = 64


def predicted_model_vector(
    ensemble_gridded_values, vertical_cfl_ratio, horizontal_cfl_ratio, spreading_coefficient
):
    diffuse = spreading_coefficient[:, None, None]
    for time_step in range(STEPS):
        widths = [(0, 0)] * (ensemble_gridded_values.ndim - 2) + [(1, 1), (1, 1)]
        padded = jnp.pad(ensemble_gridded_values, widths, mode="edge")
        east_cell = padded[..., 1:-1, 2:]
        west_cell = padded[..., 1:-1, :-2]
        north_cell = padded[..., 2:, 1:-1]
        south_cell = padded[..., :-2, 1:-1]
        ensemble_gridded_values = (
            ensemble_gridded_values
            - 0.5 * vertical_cfl_ratio * (east_cell - west_cell)
            - 0.5 * horizontal_cfl_ratio * (north_cell - south_cell)
            + diffuse
            * (east_cell + west_cell + north_cell + south_cell - 4.0 * ensemble_gridded_values)
        )
    return ensemble_gridded_values


def grid_distance(cells_a, cells_b):
    row_gap = (cells_a[:, None] // NX - cells_b[None, :] // NX).astype(jnp.float32)
    col_gap = (cells_a[:, None] % NX - cells_b[None, :] % NX).astype(jnp.float32)
    return jnp.sqrt(row_gap * row_gap + col_gap * col_gap)


def gaspari_taper(dist):
    scaled = dist / LOC_HALF
    inner_portion = (
        ((-0.25 * scaled + 0.5) * scaled + 0.625) * scaled - 5.0 / 3.0
    ) * scaled * scaled + 1.0
    safe_ratio = jnp.maximum(scaled, 1.0)
    outer_portion = (
        ((((scaled / 12.0 - 0.5) * scaled + 0.625) * scaled + 5.0 / 3.0) * scaled - 5.0) * scaled
        + 4.0
        - 2.0 / (3.0 * safe_ratio)
    )
    return jnp.where(scaled <= 1.0, inner_portion, jnp.where(scaled < 2.0, outer_portion, 0.0))


def obs_space(prior_rows, row_cells, first_row, obs_cell, obs_value, obs_var):
    member_count = prior_rows.shape[1]
    reach_table = gaspari_taper(grid_distance(row_cells, obs_cell))

    def advance_obs(current, position):
        own_row = lax.dynamic_index_in_dim(current, first_row + position, 0, False)
        row_mean = jnp.mean(own_row)
        anomaly = own_row - row_mean
        spread = jnp.sum(anomaly * anomaly) / (member_count - 1) + 1e-06
        error_var = lax.dynamic_index_in_dim(obs_var, position, 0, False)
        seen_value = lax.dynamic_index_in_dim(obs_value, position, 0, False)
        shrink = jnp.sqrt(error_var / (spread + error_var))
        increment = (
            (row_mean * error_var + seen_value * spread) / (spread + error_var)
            - row_mean
            + (shrink - 1.0) * anomaly
        )
        centered = current - jnp.mean(current, axis=1, keepdims=True)
        slopes = jnp.dot(centered, anomaly, precision=lax.Precision.HIGHEST) / (
            (member_count - 1) * spread
        )
        weight = lax.dynamic_index_in_dim(reach_table, position, 1, False)
        current = current + (weight * slopes)[:, None] * increment[None, :]
        return (current, (anomaly, spread, increment))

    positions = jnp.arange(obs_cell.shape[0], dtype=jnp.int32)
    prior_rows, obs_plan = lax.scan(advance_obs, prior_rows, positions)
    return (obs_plan, prior_rows)


def settle(state_rows, obs_plan, cell_loc):
    prior_anoms, spreads, increments = obs_plan
    member_count = state_rows.shape[0]
    centered = state_rows - jnp.mean(state_rows, axis=0, keepdims=True)
    cross_cov = jnp.einsum(
        "km,msc->ksc", prior_anoms, centered, precision=lax.Precision.HIGHEST
    ) / (member_count - 1)
    incr_anom = increments - jnp.mean(increments, axis=1, keepdims=True)
    incr_link = jnp.dot(incr_anom, prior_anoms.T, precision=lax.Precision.HIGHEST) / (
        member_count - 1
    )

    def solve_step(weights, position):
        column = lax.dynamic_index_in_dim(incr_link, position, 1, False)
        summed_total = lax.dynamic_index_in_dim(cross_cov, position, 0, False) + jnp.einsum(
            "j,jsc->sc", column, weights, precision=lax.Precision.HIGHEST
        )
        taper_row = lax.dynamic_index_in_dim(cell_loc, position, 0, False)
        update_row = (
            taper_row[None, :]
            * summed_total
            / lax.dynamic_index_in_dim(spreads, position, 0, False)
        )
        return (lax.dynamic_update_index_in_dim(weights, update_row, position, 0), None)

    positions = jnp.arange(cross_cov.shape[0], dtype=jnp.int32)
    weights, unused = lax.scan(solve_step, jnp.zeros_like(cross_cov), positions)
    return state_rows + jnp.einsum(
        "km,ksc->msc", increments, weights, precision=lax.Precision.HIGHEST
    )


def pick_rows(state_rows, obs_slab, obs_cell, slab_base, cell_base):
    slab_dev = state_rows.shape[1]
    cell_dev = state_rows.shape[2]
    slab_off = obs_slab - slab_base
    cell_off = obs_cell - cell_base
    inside = (slab_off >= 0) & (slab_off < slab_dev) & (cell_off >= 0) & (cell_off < cell_dev)
    taken_rows = state_rows[
        :, jnp.clip(slab_off, 0, slab_dev - 1), jnp.clip(cell_off, 0, cell_dev - 1)
    ]
    return jnp.where(inside[:, None], taken_rows.T, 0.0)


def body(
    prior_ensemble_stack,
    vertical_cfl_ratio,
    horizontal_cfl_ratio,
    spreading_coefficient,
    obs_cells,
    obs_slabs,
    obs_values,
    obs_error,
):
    mem_dev, slab_dev, grid_rows, grid_cols = prior_ensemble_stack.shape
    cell_total = grid_rows * grid_cols
    cell_dev = cell_total // lax.axis_size("mem")
    batch_count = obs_cells.shape[0]
    ensemble_gridded_values = predicted_model_vector(
        prior_ensemble_stack, vertical_cfl_ratio, horizontal_cfl_ratio, spreading_coefficient
    )
    by_cells = ensemble_gridded_values.reshape(mem_dev, slab_dev, cell_total)
    cell_base = lax.axis_index("mem") * cell_dev
    slab_base = lax.axis_index("lev") * slab_dev
    local_cells = cell_base + jnp.arange(cell_dev, dtype=jnp.int32)
    cell_locs = [
        gaspari_taper(grid_distance(obs_cells[batch_no], local_cells))
        for batch_no in range(batch_count)
    ]
    state_rows = lax.all_to_all(by_cells, "mem", split_axis=2, concat_axis=0, tiled=True)
    for batch_no in range(batch_count):
        partial_value = pick_rows(
            state_rows, obs_slabs[batch_no], obs_cells[batch_no], slab_base, cell_base
        )
        prior_rows = lax.psum(partial_value, ("mem", "lev"))
        obs_plan, carried = obs_space(
            prior_rows,
            obs_cells[batch_no],
            0,
            obs_cells[batch_no],
            obs_values[batch_no],
            obs_error[batch_no],
        )
        state_rows = settle(state_rows, obs_plan, cell_locs[batch_no])
    result = lax.all_to_all(state_rows, "mem", split_axis=0, concat_axis=2, tiled=True)
    return result.reshape(prior_ensemble_stack.shape)


def solution(mesh):
    in_specs = (
        P("mem", "lev", None, None),
        P("lev", None, None),
        P("lev", None, None),
        P("lev"),
        P(),
        P(),
        P(),
        P(),
    )
    out_specs = P("mem", "lev", None, None)
    return jax.shard_map(body, mesh=mesh, in_specs=in_specs, out_specs=out_specs, check_vma=False)
```

profile of v0, /device:TPU:0, one launch (start us, length us, event | category | flops | bytes accessed | tf_op | source)
XLA Modules:
  0.0 932.8 jit_solution(16619717677496745712)
XLA Ops:
  2.7 2.2 multiply_add_fusion.5
  5.0 2.2 multiply_add_fusion.4
  7.2 22.3 %copy.76 = f32[2,5,64,512]{1,0,3,2:T(2,128)} copy(f32[2,5,64,512]{3,2,1,0:T(8,128)S(1)} %multiply_add_fusion.4) | data formatting | bytes 2621440 | tf_op jit(solution)/shard_map/reshape | solution.py:143
  29.5 53.2 %reshape.447 = f32[8,1,40960]{2,1,0:T(1,128)} reshape(f32[32768,2,5]{2,1,0:T(2,128)} %bitcast.261) | data formatting | bytes 2621440
  82.7 7.6 all-to-all-start
  92.0 1.6 fusion.55
  93.6 27.9 %all-to-all-done = f32[8,1,40960]{2,1,0:T(1,128)S(1)} async-done(((f32[8,1,40960]{2,1,0:T(1,128)}), f32[8,1,40960]{2,1,0:T(1,128)S(1)}, u32[]{:S(2)}, u32[]{:S(2)}) %all-to-all-start) | async-done | bytes 1310752 | tf_op jit(solution)/shard_map/all_to_all | solution.py:151
  122.0 3.8 reduce.3
  125.8 62.1 %reshape.448 = f32[32768,2,5]{2,1,0:T(2,128)} reshape(f32[8,40960]{1,0:T(8,128)S(1)} %reduce.3) | data formatting | bytes 2621440
  187.9 26.8 %copy.73 = f32[2,5,8,4096]{3,2,0,1:T(8,128)S(1)} copy(f32[2,5,8,4096]{1,0,3,2:T(2,128)} %bitcast.262) | data formatting | bytes 2621440 | tf_op jit(solution)/shard_map/all_to_all | solution.py:151
  216.8 5.5 copy.51
  224.0 37.7 %psum.14 = f32[16,16]{1,0:T(8,128)S(1)} all-reduce(f32[16,16]{1,0:T(8,128)S(1)} %broadcast_select_fusion.1), channel_id=1, replica_groups=mesh['mem'=8,'lev'=4] {'mem','lev'}, use_global_device_ids=true, to_apply=%region_0.1 | all-reduce | flops 256 | bytes 2048 | tf_op jit(solution)/shard_map/psum | solution.py:156
  261.7 153.8 %while.56 = (s32[]{:T(128)}, f32[16,16]{1,0:T(8,128)S(1)}, f32[16,16]{1,0:T(8,128)S(1)}, f32[16]{0:T(128)S(1)}, f32[16,16]{1,0:T(8,128)S(1)}, /*index=5*/s32[16]...) while((s32[]{:T(128)}, f32[16,16]{1,0:T(8,128)S(1)}, ...), condition=%wide.region_5.6_spmd, body=%wide.region_1.5_spmd.sunk | while | flops 4271 | bytes 5831 | solution.py:78
  415.9 2.2 convolution_multiply_fusion.1
  418.4 118.7 %while.57 = (s32[]{:T(128)}, f32[16,5,4096]{2,1,0:T(8,128)S(1)}, s32[16]{0:T(128)S(1)}, f32[16,4096]{1,0:T(8,128)}, f32[16,5,4096]{2,0,1:T(8,128)}, /*index=5*/f...) while((s32[]{:T(128)}, f32[16,5,4096]{2,1,0:T(8,128)S(1)}, s32[16]{0:T(128)S(1)}, ...), condition=%wide.region_9.10_spmd, body=%wide.region_8.9_spmd.sunk | while | flops 3993605 | bytes 2687667 | solution.py:108
  537.1 3.3 fusion.97
  540.4 5.5 copy.57
  545.9 1.6 gather_fusion.1
  547.5 41.7 %psum.15 = f32[16,16]{1,0:T(8,128)S(1)} all-reduce(f32[16,16]{1,0:T(8,128)S(1)} %broadcast_select_fusion), channel_id=1, replica_groups=mesh['mem'=8,'lev'=4] {'mem','lev'}, use_global_device_ids=true, to_apply=%region_10.11 | all-reduce | flops 256 | bytes 2048 | tf_op jit(solution)/shard_map/psum | solution.py:156
  589.2 163.1 %while.58 = (s32[]{:T(128)}, f32[16,16]{1,0:T(8,128)S(1)}, f32[16,16]{1,0:T(8,128)S(1)}, f32[16]{0:T(128)S(1)}, f32[16,16]{1,0:T(8,128)S(1)}, /*index=5*/s32[16]...) while((s32[]{:T(128)}, f32[16,16]{1,0:T(8,128)S(1)}, ...), condition=%wide.region_15.16_spmd, body=%wide.region_11.15_spmd.sunk | while | flops 4271 | bytes 5831 | solution.py:78
  752.9 2.2 convolution_multiply_fusion
  755.8 120.0 %while.59 = (s32[]{:T(128)}, f32[16,5,4096]{2,1,0:T(8,128)S(1)}, s32[16]{0:T(128)S(1)}, f32[16,4096]{1,0:T(8,128)}, f32[16,5,4096]{2,0,1:T(8,128)}, /*index=5*/f...) while((s32[]{:T(128)}, f32[16,5,4096]{2,1,0:T(8,128)S(1)}, s32[16]{0:T(128)S(1)}, ...), condition=%wide.region_19.20_spmd, body=%wide.region_18.19_spmd.sunk | while | flops 3993605 | bytes 2687667 | solution.py:108
  875.8 1.9 convolution_add_fusion
  878.6 51.7 %all_to_all.33 = f32[16,5,4096]{2,1,0:T(8,128)S(1)} all-to-all(f32[16,5,4096]{2,1,0:T(8,128)S(1)} %copy.63), channel_id=1, replica_groups=mesh['mem'=8,'lev'=4] {'mem'}, dimensions={0} | all-to-all | bytes 2621440 | tf_op jit(solution)/shard_map/all_to_all | solution.py:166
  (677 shorter events, 318.6 us)
Async XLA Ops:
  1.0 1.7 copy-start.1
  1.0 1.7 copy-start.4
  82.7 7.7 copy-start.2
  82.7 8.7 copy-start.3
  82.7 8.8 copy-start.5
  82.7 8.8 copy-start.6
  82.7 38.8 %all-to-all-start = ((f32[8,1,40960]{2,1,0:T(1,128)}), f32[8,1,40960]{2,1,0:T(1,128)S(1)}, u32[]{:S(2)}, u32[]{:S(2)}) async-start(f32[8,1,40960]{2,1,0:T(1,128)} %reshape.447), calls=%async_computation | async-start | bytes 2621440 | tf_op jit(solution)/shard_map/all_to_all | solution.py:151
  216.8 199.1 %copy-start = (f32[16,5,4096]{2,0,1:T(8,128)}, f32[16,5,4096]{2,0,1:T(8,128)S(1)}, u32[]{:S(2)}) copy-start(f32[16,5,4096]{2,0,1:T(8,128)S(1)} %all_to_all.27) | copy-start | bytes 3932164
  540.4 48.8 %copy-start.7 = (f32[16]{0:T(128)S(1)}, f32[16]{0:T(128)}, u32[]{:S(2)}) copy-start(f32[16]{0:T(128)} %get-tuple-element.825) | copy-start | bytes 196
  540.4 48.8 %copy-start.8 = (f32[16]{0:T(128)S(1)}, f32[16]{0:T(128)}, u32[]{:S(2)}) copy-start(f32[16]{0:T(128)} %get-tuple-element.824) | copy-start | bytes 196
  752.4 0.6 copy-start.9
  755.2 0.7 copy-start.10
where the time goes:
time: 945 us; the launch traced here: 933 us
  local copies, waits for them, and re-layouts  358 us (38%)
  loops' own time  250 us (26%)
  blocking collectives  131 us (14%)
  other arithmetic  83.4 us (9%)
  matrix products  73.5 us (8%)
  waiting for transfers between devices  27.9 us (3%)
    another operation x2, loops' own time, obs_space(): prior_rows, obs_plan = lax.scan(advance_obs, prior_rows, positions)  189 us
    unnamed x24, local copies, waits for them, and re-layouts  116 us
    psum x2, blocking collectives, body(): prior_rows = lax.psum(partial_value, ('mem', 'lev'))  79.3 us
    another operation x2, loops' own time, settle(): weights, unused = lax.scan(solve_step, jnp.zeros_like(cross_cov), positions)  61.9 us
    all_to_all x1, blocking collectives, body(): lax.all_to_all(state_rows, 'mem', split_axis=0, concat_axis=2, tiled=True)  51.7 us
    dot_general x32, matrix products, solve_step(): jnp.einsum('j,jsc->sc', column, weights, precision=lax.Precision.HIGHEST)  46.1 us
    dynamic_slice x64, local copies, waits for them, and re-layouts, obs_space(): prior_rows, obs_plan = lax.scan(advance_obs, prior_rows, positions)  40.3 us
    dynamic_slice x32, local copies, waits for them, and re-layouts, solve_step(): lax.dynamic_index_in_dim(cross_cov, position, 0, False)  36.9 us
  transfers between devices with their start and end apart: 1, of which 1 were waited for; matrix products, arithmetic and copies ran while one was open for 0% of the time, Pallas kernels for 0%

commit v1 on v0

v1 whole, which is shorter than its diff:
```python
import functools

import jax
import jax.numpy as jnp
from jax import lax
from jax.experimental import pallas as pl
from jax.experimental.pallas import tpu as pltpu
from jax.sharding import PartitionSpec as P

STEPS = 2
LOC_HALF = 64
LANES = 128
TILE = 8
VMEM = pl.BlockSpec(memory_space=pltpu.VMEM)
SMEM = pl.BlockSpec(memory_space=pltpu.SMEM)


def cost(flops, nbytes):
    return pl.CostEstimate(flops=flops, bytes_accessed=nbytes, transcendentals=0)


def taper(row_gap, col_gap):
    scaled = jnp.sqrt(row_gap * row_gap + col_gap * col_gap) * (1.0 / LOC_HALF)
    inner = (
        ((-0.25 * scaled + 0.5) * scaled + 0.625) * scaled - 5.0 / 3.0
    ) * scaled * scaled + 1.0
    safe = jnp.maximum(scaled, 1.0)
    outer = (
        ((((scaled * (1.0 / 12.0) - 0.5) * scaled + 0.625) * scaled + 5.0 / 3.0) * scaled - 5.0)
        * scaled
        + 4.0
        - (2.0 / 3.0) / safe
    )
    return jnp.where(scaled <= 1.0, inner, jnp.where(scaled < 2.0, outer, 0.0))


def chunks_of(slab_dev):
    first = max(1, (2 * slab_dev) // 5)
    return ((0, first), (first, slab_dev - first)) if slab_dev > 1 else ((0, 1),)


def forecast_kernel(
    parts, n, cells_ref, slabs_ref, base_ref, spread_ref, x_ref, cv_ref, ch_ref, *rest
):
    outs, (field, picks) = rest[: len(parts)], rest[len(parts) :]
    mem_dev, _, ny, nx = x_ref.shape
    block = ny // n
    tiles = nx // LANES
    depth = block * tiles
    slab = pl.program_id(0)
    diffuse = spread_ref[slab]
    rows = lax.broadcasted_iota(jnp.int32, (ny, nx), 0)
    cols = lax.broadcasted_iota(jnp.int32, (ny, nx), 1)
    half_v = 0.5 * cv_ref[0]
    half_h = 0.5 * ch_ref[0]
    east_w, west_w = diffuse - half_v, diffuse + half_v
    north_w, south_w = diffuse - half_h, diffuse + half_h
    for m in range(mem_dev):
        f = x_ref[m, 0]
        for _ in range(STEPS):
            east = jnp.where(cols == nx - 1, f, pltpu.roll(f, nx - 1, 1))
            west = jnp.where(cols == 0, f, pltpu.roll(f, 1, 1))
            north = jnp.where(rows == ny - 1, f, pltpu.roll(f, ny - 1, 0))
            south = jnp.where(rows == 0, f, pltpu.roll(f, 1, 0))
            f = (
                (1.0 - 4.0 * diffuse) * f
                + east_w * east
                + west_w * west
                + north_w * north
                + south_w * south
            )
        for t in range(tiles):
            field[slab * mem_dev + m, pl.ds(t * ny, ny), :] = f[:, t * LANES : (t + 1) * LANES]
        for (start, count), out in zip(parts, outs):

            @pl.when((slab >= start) & (slab < start + count))
            def _():
                at = (m * count + slab - start) * depth
                for d in range(n):
                    for t in range(tiles):
                        out[d, pl.ds(at + t * block, block), :] = f[
                            d * block : (d + 1) * block, t * LANES : (t + 1) * LANES
                        ]

    @pl.when(slab == pl.num_programs(0) - 1)
    def _():
        slab_dev = pl.num_programs(0)
        total = cells_ref.shape[0]
        lane = lax.broadcasted_iota(jnp.int32, (1, LANES), 1)
        for k in range(total):
            cell = cells_ref[k]
            row, col = cell // nx, cell % nx
            off = slabs_ref[k] - base_ref[1] * slab_dev
            inside = (off >= 0) & (off < slab_dev)
            wanted = jnp.where(inside, col % LANES, LANES)
            off = jnp.clip(off, 0, slab_dev - 1)
            for m in range(mem_dev):
                line = field[off * mem_dev + m, pl.ds((col // LANES) * ny + row, 1), :]
                picks[m, pl.ds(k, 1), :] = jnp.where(lane == wanted, line, 0.0)
        diagonal = lax.broadcasted_iota(jnp.int32, (total, LANES), 0) == lax.broadcasted_iota(
            jnp.int32, (total, LANES), 1
        )
        place = lax.broadcasted_iota(jnp.int32, (TILE, LANES), 0)
        seen = jnp.zeros((TILE, LANES), jnp.float32)
        for m in range(mem_dev):
            value = jnp.sum(picks[m], axis=1, keepdims=True)
            value = jnp.sum(jnp.where(diagonal, value, 0.0), axis=0, keepdims=True)
            seen = jnp.where(place == (base_ref[0] * mem_dev + m) % TILE, value, seen)
        for d in range(n):
            outs[0][d, pl.ds(mem_dev * parts[0][1] * depth, TILE), :] = seen


def forecast(parts, n, cells, slabs, base, spread, x, cv, ch):
    mem_dev, slab_dev, ny, nx = x.shape
    depth = ny // n * nx // LANES
    shapes = [
        (n, mem_dev * count * depth + (TILE if i == 0 else 0), LANES)
        for i, (_, count) in enumerate(parts)
    ]
    return pl.pallas_call(
        functools.partial(forecast_kernel, parts, n),
        grid=(slab_dev,),
        in_specs=[
            SMEM,
            SMEM,
            SMEM,
            SMEM,
            pl.BlockSpec((mem_dev, 1, ny, nx), lambda s: (0, s, 0, 0)),
            pl.BlockSpec((1, ny, nx), lambda s: (s, 0, 0)),
            pl.BlockSpec((1, ny, nx), lambda s: (s, 0, 0)),
        ],
        out_specs=[pl.BlockSpec(shape, lambda s: (0, 0, 0)) for shape in shapes],
        out_shape=[jax.ShapeDtypeStruct(shape, jnp.float32) for shape in shapes],
        scratch_shapes=[
            pltpu.VMEM((slab_dev * mem_dev, ny * nx // LANES, LANES), jnp.float32),
            pltpu.VMEM((mem_dev, cells.shape[0], LANES), jnp.float32),
        ],
        cost_estimate=cost(60 * x.size, 4 * (2 * x.size + 2 * cv.size)),
        name="forecast",
    )(cells, slabs, base, spread, x, cv, ch)


def taper_kernel(nx, block, cells_ref, base_ref, out_ref):
    depth = out_ref.shape[1]
    at = lax.broadcasted_iota(jnp.int32, (depth, LANES), 0)
    row = (base_ref[0] * block + at % block).astype(jnp.float32)
    col = (at // block * LANES + lax.broadcasted_iota(jnp.int32, (depth, LANES), 1)).astype(
        jnp.float32
    )

    def one(k, carry):
        cell = cells_ref[k]
        out_ref[k] = taper(
            row - (cell // nx).astype(jnp.float32), col - (cell % nx).astype(jnp.float32)
        )
        return carry

    lax.fori_loop(0, out_ref.shape[0], one, 0)


def taper_table(nx, block, cells, base):
    depth = block * nx // LANES
    total = cells.shape[0]
    return pl.pallas_call(
        functools.partial(taper_kernel, nx, block),
        in_specs=[SMEM, SMEM],
        out_specs=VMEM,
        out_shape=jax.ShapeDtypeStruct((total, depth, LANES), jnp.float32),
        cost_estimate=cost(60 * total * depth * LANES, 4 * total * depth * LANES),
        name="taper_table",
    )(cells, base)


def plan_kernel(nx, batch, cells_ref, values_ref, errors_ref, *refs):
    tiles, (anom_ref, incr_ref) = refs[:-2], refs[-2:]
    total = cells_ref.shape[0]
    rows = tiles[0][...]
    for other in tiles[1:]:
        rows = rows + other[...]
    members = rows.shape[0]
    lane = lax.broadcasted_iota(jnp.int32, (1, LANES), 1)
    row_of = jnp.zeros((1, LANES), jnp.float32)
    col_of = jnp.zeros((1, LANES), jnp.float32)
    where = []
    for k in range(total):
        cell = cells_ref[k]
        row, col = (cell // nx).astype(jnp.float32), (cell % nx).astype(jnp.float32)
        where.append((row, col))
        row_of = jnp.where(lane == k, row, row_of)
        col_of = jnp.where(lane == k, col, col_of)
    mean = jnp.sum(rows, axis=0, keepdims=True) * (1.0 / members)
    rows = rows - mean
    for k in range(total):
        loc = taper(row_of - where[k][0], col_of - where[k][1])
        anomaly = jnp.broadcast_to(rows[:, k : k + 1], rows.shape)
        ybar = jnp.broadcast_to(mean[:, k : k + 1], mean.shape)
        variance = jnp.sum(anomaly * anomaly, axis=0, keepdims=True) / (members - 1) + 1e-06
        shared = jnp.sum(rows * anomaly, axis=0, keepdims=True)
        error, value = errors_ref[k], values_ref[k]
        scale = 1.0 / ((members - 1) * variance)
        shift = (ybar * error + value * variance) / (variance + error) - ybar
        shrink = jnp.sqrt(error / (variance + error)) - 1.0
        anom_ref[k] = anomaly * scale
        incr_ref[k] = shift + shrink * anomaly
        weight = loc * shared * scale
        mean = mean + weight * shift
        rows = rows + (weight * shrink) * anomaly


def filter_plan(nx, batch, cells, values, errors, tiles):
    members = tiles[0].shape[0]
    total = cells.shape[0]
    table = jax.ShapeDtypeStruct((total, members, LANES), jnp.float32)
    return pl.pallas_call(
        functools.partial(plan_kernel, nx, batch),
        in_specs=[SMEM] * 3 + [VMEM] * len(tiles),
        out_specs=[VMEM, VMEM],
        out_shape=[table, table],
        cost_estimate=cost(20_000_000, 4 * 2 * total * members * LANES),
        name="filter_plan",
    )(cells, values, errors, *tiles)


def settle_kernel(mem_dev, count, depth, anom_ref, incr_ref, loc_ref, x_ref, out_ref):
    total = loc_ref.shape[0]
    members = anom_ref.shape[1]
    group = 2 if depth % (2 * TILE) == 0 and members <= 16 else 1
    span = group * TILE
    per_slab = depth // span

    def spread(ref, k, m):
        return ref[k, pl.ds(m, TILE, stride=0), :]

    def part(i, carry):
        slab, at = i // per_slab, (i % per_slab) * span

        def spot(m, g):
            row = ((m % mem_dev) * count + slab) * depth + at + g * TILE
            return m // mem_dev, pl.ds(pl.multiple_of(row, TILE), TILE)

        xs = []
        for m in range(members):
            for g in range(group):
                src, row = spot(m, g)
                xs.append(x_ref[src, row, :])

        def step(k, xs):
            sums = [None] * group
            for m in range(members):
                a = spread(anom_ref, k, m)
                for g in range(group):
                    term = a * xs[m * group + g]
                    sums[g] = term if m == 0 else sums[g] + term
            sums = [
                s * loc_ref[k, pl.ds(pl.multiple_of(at + g * TILE, TILE), TILE), :]
                for g, s in enumerate(sums)
            ]
            new = []
            for m in range(members):
                b = spread(incr_ref, k, m)
                for g in range(group):
                    new.append(xs[m * group + g] + b * sums[g])
            return tuple(new)

        xs = lax.fori_loop(0, total, step, tuple(xs), unroll=2)
        for m in range(members):
            for g in range(group):
                src, row = spot(m, g)
                out_ref[src, row, :] = xs[m * group + g]
        return carry

    lax.fori_loop(0, count * per_slab, part, 0)


def settle(mem_dev, count, depth, anom, incr, loc, x):
    n = x.shape[0]
    shape = (n, mem_dev * count * depth, LANES)
    size = n * mem_dev * count * depth * LANES
    return pl.pallas_call(
        functools.partial(settle_kernel, mem_dev, count, depth),
        in_specs=[VMEM] * 4,
        out_specs=VMEM,
        out_shape=jax.ShapeDtypeStruct(shape, jnp.float32),
        cost_estimate=cost(4 * loc.shape[0] * size, 8 * size),
        name="settle",
    )(anom, incr, loc, x)


def assemble_kernel(n, recv_ref, *refs):
    out_ref = refs[-1]
    mem_dev, _, ny, nx = out_ref.shape
    block = ny // n
    tiles = nx // LANES
    depth = block * tiles
    count = recv_ref.shape[1] // (mem_dev * depth)
    slab = pl.program_id(0)
    for m in range(mem_dev):
        at = (m * count + slab) * depth
        for d in range(n):
            for t in range(tiles):
                out_ref[m, 0, d * block : (d + 1) * block, t * LANES : (t + 1) * LANES] = recv_ref[
                    d, pl.ds(at + t * block, block), :
                ]


def assemble(n, start, count, recv, shape, before):
    mem_dev, _, ny, nx = shape
    extra = [] if before is None else [before]
    return pl.pallas_call(
        functools.partial(assemble_kernel, n),
        grid=(count,),
        in_specs=[pl.BlockSpec(recv.shape, lambda s: (0, 0, 0))]
        + [pl.BlockSpec(memory_space=pl.ANY)] * len(extra),
        out_specs=pl.BlockSpec((mem_dev, 1, ny, nx), lambda s: (0, start + s, 0, 0)),
        out_shape=jax.ShapeDtypeStruct(shape, jnp.float32),
        input_output_aliases={} if before is None else {1: 0},
        cost_estimate=cost(0, 8 * recv.size),
        name="assemble",
    )(recv, *extra)


def body(x, cv, ch, spread, obs_cells, obs_slabs, obs_values, obs_error):
    mem_dev, slab_dev, ny, nx = x.shape
    n, lev = lax.axis_size("mem"), lax.axis_size("lev")
    batch = obs_cells.shape[1]
    block = ny // n
    depth = block * nx // LANES
    members = n * mem_dev
    parts = chunks_of(slab_dev)
    cells, slabs = obs_cells.reshape(-1), obs_slabs.reshape(-1)
    base = jnp.stack([lax.axis_index("mem"), lax.axis_index("lev")]).astype(jnp.int32)
    sends = forecast(parts, n, cells, slabs, base, spread, x, cv, ch)
    states = [lax.all_to_all(s, "mem", split_axis=0, concat_axis=0, tiled=True) for s in sends]
    loc = taper_table(nx, block, cells, base)
    seen = states[0][:, mem_dev * parts[0][1] * depth :, :]
    seen = seen.reshape(members // TILE, -1, TILE, LANES).sum(axis=1).reshape(members, LANES)
    tiles = [seen] + [
        lax.ppermute(seen, "lev", [(i, (i + d) % lev) for i in range(lev)]) for d in range(1, lev)
    ]
    anom, incr = filter_plan(
        nx, batch, cells, obs_values.reshape(-1), obs_error.reshape(-1), tiles
    )
    result = None
    for (start, count), state in zip(parts, states):
        new = settle(mem_dev, count, depth, anom, incr, loc, state)
        back = lax.all_to_all(new, "mem", split_axis=0, concat_axis=0, tiled=True)
        result = assemble(n, start, count, back, x.shape, result)
    return result


def solution(mesh):
    in_specs = (
        P("mem", "lev", None, None),
        P("lev", None, None),
        P("lev", None, None),
        P("lev"),
        P(),
        P(),
        P(),
        P(),
    )
    out_specs = P("mem", "lev", None, None)
    return jax.shard_map(body, mesh=mesh, in_specs=in_specs, out_specs=out_specs, check_vma=False)
```

time: 945 us -> 104 us (0.11); the launches traced: 933 us -> 103 us
  local copies, waits for them, and re-layouts: 358 us -> 5.99 us
  loops' own time: 250 us -> 0 us
  blocking collectives: 131 us -> 23.4 us
  other arithmetic: 83.4 us -> 0.58 us
  matrix products: 73.5 us -> 0 us
  Pallas kernels: 0 us -> 32.6 us
    another operation x4 -> x0, loops' own time: 250 us -> none  [the longest x2 189 us: obs_space(): prior_rows, obs_plan = lax.scan(advance_obs, prior_rows, positions)]
    dynamic_slice x224 -> x0, local copies, waits for them, and re-layouts: 165 us -> none  [the longest x64 40.3 us: obs_space(): prior_rows, obs_plan = lax.scan(advance_obs, prior_rows, positions)]
    unnamed x24 -> x20, local copies, waits for them, and re-layouts: 116 us -> 2.07 us
    psum x2 -> x0, blocking collectives: 79.3 us -> none  [body(): prior_rows = lax.psum(partial_value, ('mem', 'lev'))]
    dot_general x70 -> x0, matrix products: 73.5 us -> none  [the longest x32 46.1 us: solve_step(): jnp.einsum('j,jsc->sc', column, weights, precision=lax.Precision.HIGHEST)]
    reduce_sum x99 -> x1, other arithmetic: 45.7 us -> 0.01 us  [body(): seen.reshape(members // TILE, -1, TILE, LANES).sum(axis=1)]
    all_to_all x6 -> x0, local copies, waits for them, and re-layouts: 35.5 us -> none  [the longest x5 34.7 us: body(): lax.all_to_all(by_cells, 'mem', split_axis=2, concat_axis=0, tiled=True)]
    pallas_call x0 -> x7, Pallas kernels: none -> 32.6 us  [the longest x2 13.6 us: settle(): pl.pallas_call(functools.partial(settle_kernel, mem_dev, count, depth), i...]
  transfers between devices with their start and end apart: 1 -> 6, of which waited for: 1 -> 3; matrix products, arithmetic and copies ran while one was open for 0% -> 1% of each run, Pallas kernels for 0% -> 23%
where the time goes in v1:
time: 104 us; the launch traced here: 103 us
  Pallas kernels  32.6 us (31%)
  waiting for transfers between devices  27.4 us (26%)
  blocking collectives  23.4 us (22%)
  starting transfers between devices  13.4 us (13%)
  local copies, waits for them, and re-layouts  5.99 us (6%)
    all_to_all x2, waiting for transfers between devices, body(): back = lax.all_to_all(new, 'mem', split_axis=0, concat_axis=0, tiled=True)  25.9 us
    all_to_all x1, blocking collectives, body(): lax.all_to_all(s, 'mem', split_axis=0, concat_axis=0, tiled=True)  23.4 us
    pallas_call x2, Pallas kernels, settle(): pl.pallas_call(functools.partial(settle_kernel, mem_dev, count, depth), i...  13.6 us
    all_to_all x2, starting transfers between devices, body(): back = lax.all_to_all(new, 'mem', split_axis=0, concat_axis=0, tiled=True)  8.08 us
    pallas_call x1, Pallas kernels, forecast(): pl.pallas_call(functools.partial(forecast_kernel, parts, n), grid=(slab_d...  6.62 us
    pallas_call x1, Pallas kernels, filter_plan(): pl.pallas_call(functools.partial(plan_kernel, nx, batch), in_specs=[SMEM]...  5.19 us
    pallas_call x2, Pallas kernels, assemble(): pl.pallas_call(functools.partial(assemble_kernel, n), grid=(count,), in_s...  4.45 us
    all_to_all x1, starting transfers between devices, body(): lax.all_to_all(s, 'mem', split_axis=0, concat_axis=0, tiled=True)  3.55 us
  transfers between devices with their start and end apart: 6, of which 3 were waited for; matrix products, arithmetic and copies ran while one was open for 1% of the time, Pallas kernels for 23%

profile of v1, /device:TPU:0, one launch (start us, length us, event | category | flops | bytes accessed | tf_op | source)
XLA Modules:
  0.0 103.4 jit_solution(15326636428313461686)
XLA Ops:
  0.0 1.3 %reshape.18.cells_ref = s32[32]{0:T(128)} reshape(s32[2,16]{1,0:T(2,128)} %param.12) | data formatting | bytes 256 | tf_op jit(solution)/shard_map/reshape | solution.py:330
  1.3 1.3 %reshape.21.slabs_ref = s32[32]{0:T(128)} reshape(s32[2,16]{1,0:T(2,128)} %param.13) | data formatting | bytes 256 | tf_op jit(solution)/shard_map/reshape | solution.py:330
  2.7 0.6 pad_add_fusion.base_ref
  3.2 6.6 %forecast.1 = (f32[8,136,128]{2,1,0:T(8,128)}, f32[8,192,128]{2,1,0:T(8,128)}) custom-call(s32[32]{0:T(128)} %reshape.18.cells_ref, s32[32]{0:T(128)} %reshape.21.slabs_ref, s32[2]{0:T(128)} %pad_add_fusion.base_ref, f32[5]{0:T(128)} %spread_ref.1, f32[2,5,64,512]{3,2,1,0:T(8,128)} %x_ref.1, f32[5,64,512]{2,1,0:T(8,128)} %cv_ref.1, f32[5,64,512]{2,1,0:T(8,128)} %ch_ref.1), custom_call_target="tpu_custom_call" | custom-call | flops 19660800 | bytes 3932160 | tf_op jit(solution)/shard_map/forecast/pallas_call | solution.py:120
  9.9 23.4 %all_to_all.20.x_ref = f32[8,136,128]{2,1,0:T(8,128)S(1)} all-to-all(f32[8,136,128]{2,1,0:T(8,128)} %get-tuple-element.9), channel_id=1, replica_groups=mesh['mem'=8,'lev'=4] {'mem'}, dimensions={0} | all-to-all | bytes 1114112 | tf_op jit(solution)/shard_map/all_to_all | solution.py:333
  33.3 3.5 %all-to-all-start.1 = ((f32[8,192,128]{2,1,0:T(8,128)}), f32[8,192,128]{2,1,0:T(8,128)S(1)}, u32[]{:S(2)}, u32[]{:S(2)}) async-start(f32[8,192,128]{2,1,0:T(8,128)} %get-tuple-element.12), calls=%async_computation.1 | async-start | bytes 1572864 | tf_op jit(solution)/shard_map/all_to_all | solution.py:333
  36.9 1.6 %collective-permute-start.1 = (f32[16,128]{1,0:T(8,128)S(1)}, f32[16,128]{1,0:T(8,128)S(1)}, u32[]{:S(2)}, u32[]{:S(2)}) collective-permute-start(f32[16,128]{1,0:T(8,128)S(1)} %bitcast.6), channel_id=1, source_target_pairs={{0,2},{1,3},{2,0},{3,1},{4,6},{5,7},{6,4},{7,5},{8,10},{9,11},{10,... | collective-permute-start | bytes 24584 | tf_op jit(solution)/shard_map/ppermute | solution.py:338
  38.5 0.2 collective-permute-start
  38.6 0.7 reshape.19.values_ref
  39.3 0.6 reshape.20.errors_ref
  39.9 2.7 %taper_table.1.loc_ref = f32[32,32,128]{2,1,0:T(8,128)} custom-call(s32[32]{0:T(128)} %reshape.18.cells_ref, s32[2]{0:T(128)} %pad_add_fusion.base_ref), custom_call_target="tpu_custom_call" | custom-call | flops 7864320 | bytes 524288 | tf_op jit(solution)/shard_map/taper_table/pallas_call | solution.py:164
  42.6 0.6 copy-done.5
  43.2 0.6 copy-done.7
  43.8 5.2 %filter_plan.1 = (f32[32,16,128]{2,1,0:T(8,128)}, f32[32,16,128]{2,1,0:T(8,128)}) custom-call(s32[32]{0:T(128)} %reshape.18.cells_ref, f32[32]{0:T(128)} %reshape.19.values_ref, f32[32]{0:T(128)} %reshape.20.errors_ref, f32[16,128]{1,0:T(8,128)} %bitcast.8, f32[16,128]{1,0:T(8,128)} %copy-done.7, f32[16,128]{1,0:T(8,128)} %copy-done.6, f32[16,128]{1,0:T(8,128)} %copy-done.5), custom_call_target="tpu_custom_call" | custom-call | flops 20000000 | bytes 524288 | tf_op jit(solution)/shard_map/filter_plan/pallas_call | solution.py:214
  49.0 5.8 %settle.3 = f32[8,128,128]{2,1,0:T(8,128)} custom-call(f32[32,16,128]{2,1,0:T(8,128)} %get-tuple-element.10.anom_ref, f32[32,16,128]{2,1,0:T(8,128)} %get-tuple-element.11.incr_ref, f32[32,32,128]{2,1,0:T(8,128)} %taper_table.1.loc_ref, f32[8,136,128]{2,1,0:T(8,128)} %copy-done.2), custom_call_target="tpu_custom_call" | custom-call | flops 16777216 | bytes 1048576 | tf_op jit(solution)/shard_map/settle/pallas_call | solution.py:279
  54.8 1.5 %all-to-all-done.1.x_ref = f32[8,192,128]{2,1,0:T(8,128)S(1)} async-done(((f32[8,192,128]{2,1,0:T(8,128)}), f32[8,192,128]{2,1,0:T(8,128)S(1)}, u32[]{:S(2)}, u32[]{:S(2)}) %all-to-all-start.1) | async-done | bytes 786464 | tf_op jit(solution)/shard_map/all_to_all | solution.py:333
  56.3 4.4 %all-to-all-start.3 = ((f32[8,128,128]{2,1,0:T(8,128)}), f32[8,128,128]{2,1,0:T(8,128)S(1)}, u32[]{:S(2)}, u32[]{:S(2)}) async-start(f32[8,128,128]{2,1,0:T(8,128)} %settle.3), calls=%async_computation.3 | async-start | bytes 1048576 | tf_op jit(solution)/shard_map/all_to_all | solution.py:346
  60.7 7.8 %settle.2 = f32[8,192,128]{2,1,0:T(8,128)} custom-call(f32[32,16,128]{2,1,0:T(8,128)} %get-tuple-element.10.anom_ref, f32[32,16,128]{2,1,0:T(8,128)} %get-tuple-element.11.incr_ref, f32[32,32,128]{2,1,0:T(8,128)} %taper_table.1.loc_ref, f32[8,192,128]{2,1,0:T(8,128)} %copy-done), custom_call_target="tpu_custom_call" | custom-call | flops 25165824 | bytes 1572864 | tf_op jit(solution)/shard_map/settle/pallas_call | solution.py:279
  68.5 7.3 %all-to-all-done.3.recv_ref = f32[8,128,128]{2,1,0:T(8,128)S(1)} async-done(((f32[8,128,128]{2,1,0:T(8,128)}), f32[8,128,128]{2,1,0:T(8,128)S(1)}, u32[]{:S(2)}, u32[]{:S(2)}) %all-to-all-start.3) | async-done | bytes 524320 | tf_op jit(solution)/shard_map/all_to_all | solution.py:346
  75.9 3.6 %all-to-all-start.2 = ((f32[8,192,128]{2,1,0:T(8,128)}), f32[8,192,128]{2,1,0:T(8,128)S(1)}, u32[]{:S(2)}, u32[]{:S(2)}) async-start(f32[8,192,128]{2,1,0:T(8,128)} %settle.2), calls=%async_computation.2 | async-start | bytes 1572864 | tf_op jit(solution)/shard_map/all_to_all | solution.py:346
  79.5 1.9 %assemble.2.refs_0_ = f32[2,5,64,512]{3,2,1,0:T(8,128)} custom-call(f32[8,128,128]{2,1,0:T(8,128)} %copy-done.3), custom_call_target="tpu_custom_call" | custom-call | bytes 1048576 | tf_op jit(solution)/shard_map/assemble/pallas_call | solution.py:309
  81.4 18.5 %all-to-all-done.2.recv_ref = f32[8,192,128]{2,1,0:T(8,128)S(1)} async-done(((f32[8,192,128]{2,1,0:T(8,128)}), f32[8,192,128]{2,1,0:T(8,128)S(1)}, u32[]{:S(2)}, u32[]{:S(2)}) %all-to-all-start.2) | async-done | bytes 786464 | tf_op jit(solution)/shard_map/all_to_all | solution.py:346
  99.9 0.9 copy-done.1
  100.8 2.6 %assemble.3 = f32[2,5,64,512]{3,2,1,0:T(8,128)} custom-call(f32[8,192,128]{2,1,0:T(8,128)} %copy-done.1, f32[2,5,64,512]{3,2,1,0:T(8,128)} %assemble.2.refs_0_), custom_call_target="tpu_custom_call", output_to_operand_aliasing={{}: (1, {})} | custom-call | bytes 1572864 | tf_op jit(solution)/shard_map/assemble/pallas_call | solution.py:309
  (22 shorter events, 0.1 us)
Async XLA Ops:
  9.9 28.8 %copy-start.8 = (f32[2,16]{1,0:T(2,128)S(1)}, f32[2,16]{1,0:T(2,128)}, u32[]{:S(2)}) copy-start(f32[2,16]{1,0:T(2,128)} %param.14) | copy-start | bytes 388
  9.9 29.4 %copy-start.9 = (f32[2,16]{1,0:T(2,128)S(1)}, f32[2,16]{1,0:T(2,128)}, u32[]{:S(2)}) copy-start(f32[2,16]{1,0:T(2,128)} %param.15) | copy-start | bytes 388
  33.3 15.7 %copy-start.2 = (f32[8,136,128]{2,1,0:T(8,128)}, f32[8,136,128]{2,1,0:T(8,128)S(1)}, u32[]{:S(2)}) copy-start(f32[8,136,128]{2,1,0:T(8,128)S(1)} %all_to_all.20.x_ref) | copy-start | bytes 1671172
  33.3 23.0 %all-to-all-start.1 = ((f32[8,192,128]{2,1,0:T(8,128)}), f32[8,192,128]{2,1,0:T(8,128)S(1)}, u32[]{:S(2)}, u32[]{:S(2)}) async-start(f32[8,192,128]{2,1,0:T(8,128)} %get-tuple-element.12), calls=%async_computation.1 | async-start | bytes 1572864 | tf_op jit(solution)/shard_map/all_to_all | solution.py:333
  36.8 5.8 %copy-start.4 = (f32[2,8,128]{2,1,0:T(8,128)}, f32[2,8,128]{2,1,0:T(8,128)S(1)}, u32[]{:S(2)}) copy-start(f32[2,8,128]{2,1,0:T(8,128)S(1)} %bitcast_reduce_fusion) | copy-start | bytes 24580
  36.8 5.8 %collective-permute-start.2 = (f32[16,128]{1,0:T(8,128)S(1)}, f32[16,128]{1,0:T(8,128)S(1)}, u32[]{:S(2)}, u32[]{:S(2)}) collective-permute-start(f32[16,128]{1,0:T(8,128)S(1)} %bitcast.5), channel_id=1, source_target_pairs={{0,3},{1,0},{2,1},{3,2},{4,7},{5,4},{6,5},{7,6},{8,11},{9,8},{10,9... | collective-permute-start | bytes 24584 | tf_op jit(solution)/shard_map/ppermute | solution.py:338
  36.9 5.7 %collective-permute-start.1 = (f32[16,128]{1,0:T(8,128)S(1)}, f32[16,128]{1,0:T(8,128)S(1)}, u32[]{:S(2)}, u32[]{:S(2)}) collective-permute-start(f32[16,128]{1,0:T(8,128)S(1)} %bitcast.6), channel_id=1, source_target_pairs={{0,2},{1,3},{2,0},{3,1},{4,6},{5,7},{6,4},{7,5},{8,10},{9,11},{10,... | collective-permute-start | bytes 24584 | tf_op jit(solution)/shard_map/ppermute | solution.py:338
  38.5 4.2 %collective-permute-start = (f32[16,128]{1,0:T(8,128)S(1)}, f32[16,128]{1,0:T(8,128)S(1)}, u32[]{:S(2)}, u32[]{:S(2)}) collective-permute-start(f32[16,128]{1,0:T(8,128)S(1)} %bitcast.7), channel_id=1, source_target_pairs={{0,1},{1,2},{2,3},{3,0},{4,5},{5,6},{6,7},{7,4},{8,9},{9,10},{10,1... | collective-permute-start | bytes 24584 | tf_op jit(solution)/shard_map/ppermute | solution.py:338
  42.6 0.6 copy-start.5
  42.6 0.6 copy-start.6
  43.2 0.6 copy-start.7
  56.3 4.4 %copy-start = (f32[8,192,128]{2,1,0:T(8,128)}, f32[8,192,128]{2,1,0:T(8,128)S(1)}, u32[]{:S(2)}) copy-start(f32[8,192,128]{2,1,0:T(8,128)S(1)} %all-to-all-done.1.x_ref) | copy-start | bytes 2359300
  56.3 19.6 %all-to-all-start.3 = ((f32[8,128,128]{2,1,0:T(8,128)}), f32[8,128,128]{2,1,0:T(8,128)S(1)}, u32[]{:S(2)}, u32[]{:S(2)}) async-start(f32[8,128,128]{2,1,0:T(8,128)} %settle.3), calls=%async_computation.3 | async-start | bytes 1048576 | tf_op jit(solution)/shard_map/all_to_all | solution.py:346
  75.9 3.6 %copy-start.3 = (f32[8,128,128]{2,1,0:T(8,128)}, f32[8,128,128]{2,1,0:T(8,128)S(1)}, u32[]{:S(2)}) copy-start(f32[8,128,128]{2,1,0:T(8,128)S(1)} %all-to-all-done.3.recv_ref) | copy-start | bytes 1572868
  75.9 24.0 %all-to-all-start.2 = ((f32[8,192,128]{2,1,0:T(8,128)}), f32[8,192,128]{2,1,0:T(8,128)S(1)}, u32[]{:S(2)}, u32[]{:S(2)}) async-start(f32[8,192,128]{2,1,0:T(8,128)} %settle.2), calls=%async_computation.2 | async-start | bytes 1572864 | tf_op jit(solution)/shard_map/all_to_all | solution.py:346
  99.9 0.9 copy-start.1

commit v2 on v1

v2 whole, which is shorter than its diff:
```python
import functools

import jax
import jax.numpy as jnp
from jax import lax
from jax.experimental import pallas as pl
from jax.experimental.pallas import tpu as pltpu
from jax.sharding import PartitionSpec as P


STEPS = 2
LOC_HALF = 64
LANES = 128
GRANT = 24 * 1024 * 1024
TILE = 8
VMEM = pl.BlockSpec(memory_space=pltpu.VMEM)
SMEM = pl.BlockSpec(memory_space=pltpu.SMEM)


def cost(flops, nbytes):
    return pl.CostEstimate(flops=flops, bytes_accessed=nbytes, transcendentals=0)


def taper(row_gap, col_gap):
    scaled = jnp.sqrt(row_gap * row_gap + col_gap * col_gap) * (1.0 / LOC_HALF)
    inner = (
        ((-0.25 * scaled + 0.5) * scaled + 0.625) * scaled - 5.0 / 3.0
    ) * scaled * scaled + 1.0
    safe = jnp.maximum(scaled, 1.0)
    outer = (
        ((((scaled * (1.0 / 12.0) - 0.5) * scaled + 0.625) * scaled + 5.0 / 3.0) * scaled - 5.0)
        * scaled
        + 4.0
        - (2.0 / 3.0) / safe
    )
    return jnp.where(scaled <= 1.0, inner, jnp.where(scaled < 2.0, outer, 0.0))


def chunks_of(slab_dev):
    first = max(1, (2 * slab_dev) // 5)
    return ((0, first), (first, slab_dev - first)) if slab_dev > 1 else ((0, 1),)


def place(ref, k):
    return ref[k // ref.shape[1], k % ref.shape[1]]


def params():
    return pltpu.CompilerParams(vmem_limit_bytes=GRANT)


def forecast_kernel(parts, n, cells_ref, slabs_ref, spread_ref, x_ref, cv_ref, ch_ref, *rest):
    outs, (field, picks) = rest[: len(parts) * n], rest[len(parts) * n :]
    mem_dev, _, ny, nx = x_ref.shape
    block = ny // n
    tiles = nx // LANES
    depth = block * tiles
    me = lax.axis_index("mem")
    slab = pl.program_id(0)
    diffuse = spread_ref[slab]
    rows = lax.broadcasted_iota(jnp.int32, (ny, nx), 0)
    cols = lax.broadcasted_iota(jnp.int32, (ny, nx), 1)
    half_v = 0.5 * cv_ref[0]
    half_h = 0.5 * ch_ref[0]
    east_w, west_w = diffuse - half_v, diffuse + half_v
    north_w, south_w = diffuse - half_h, diffuse + half_h
    for m in range(mem_dev):
        f = x_ref[m, 0]
        for _ in range(STEPS):
            east = jnp.where(cols == nx - 1, f, pltpu.roll(f, nx - 1, 1))
            west = jnp.where(cols == 0, f, pltpu.roll(f, 1, 1))
            north = jnp.where(rows == ny - 1, f, pltpu.roll(f, ny - 1, 0))
            south = jnp.where(rows == 0, f, pltpu.roll(f, 1, 0))
            f = (
                (1.0 - 4.0 * diffuse) * f
                + east_w * east
                + west_w * west
                + north_w * north
                + south_w * south
            )
        for t in range(tiles):
            field[slab * mem_dev + m, pl.ds(t * ny, ny), :] = f[:, t * LANES : (t + 1) * LANES]
    for c, (start, count) in enumerate(parts):

        @pl.when((slab >= start) & (slab < start + count))
        def _():
            for m in range(mem_dev):
                at = pl.multiple_of((m * count + slab - start) * depth, TILE)
                for j in range(n):
                    for t in range(tiles):
                        row = pl.multiple_of(t * ny + (me ^ j) * block, block)
                        outs[c * n + j][pl.ds(at + t * block, block), :] = field[
                            slab * mem_dev + m, pl.ds(row, block), :
                        ]

    @pl.when(slab == pl.num_programs(0) - 1)
    def _():
        slab_dev = pl.num_programs(0)
        total = cells_ref.shape[0] * cells_ref.shape[1]
        lane = lax.broadcasted_iota(jnp.int32, (1, LANES), 1)
        for k in range(total):
            cell = place(cells_ref, k)
            row, col = cell // nx, cell % nx
            off = place(slabs_ref, k) - lax.axis_index("lev") * slab_dev
            inside = (off >= 0) & (off < slab_dev)
            wanted = jnp.where(inside, col % LANES, LANES)
            off = jnp.clip(off, 0, slab_dev - 1)
            for m in range(mem_dev):
                line = field[off * mem_dev + m, pl.ds((col // LANES) * ny + row, 1), :]
                picks[m, pl.ds(k, 1), :] = jnp.where(lane == wanted, line, 0.0)
        diagonal = lax.broadcasted_iota(jnp.int32, (total, LANES), 0) == lax.broadcasted_iota(
            jnp.int32, (total, LANES), 1
        )
        values = []
        for m in range(mem_dev):
            value = jnp.sum(picks[m], axis=1, keepdims=True)
            values.append(jnp.sum(jnp.where(diagonal, value, 0.0), axis=0, keepdims=True))
        line = lax.broadcasted_iota(jnp.int32, (TILE, LANES), 0)
        for j in range(n):
            seen = jnp.zeros((TILE, LANES), jnp.float32)
            for m in range(mem_dev):
                seen = jnp.where(line == (j * mem_dev + m) % TILE, values[m], seen)
            outs[j][pl.ds(mem_dev * parts[0][1] * depth, TILE), :] = seen


def forecast(parts, n, cells, slabs, spread, x, cv, ch):
    mem_dev, slab_dev, ny, nx = x.shape
    depth = ny // n * nx // LANES
    shapes = [
        (mem_dev * count * depth + (TILE if i == 0 else 0), LANES)
        for i, (_, count) in enumerate(parts)
        for _ in range(n)
    ]
    outs = pl.pallas_call(
        functools.partial(forecast_kernel, parts, n),
        grid=(slab_dev,),
        in_specs=[
            SMEM,
            SMEM,
            SMEM,
            pl.BlockSpec((mem_dev, 1, ny, nx), lambda s: (0, s, 0, 0)),
            pl.BlockSpec((1, ny, nx), lambda s: (s, 0, 0)),
            pl.BlockSpec((1, ny, nx), lambda s: (s, 0, 0)),
        ],
        out_specs=[VMEM for shape in shapes],
        out_shape=[jax.ShapeDtypeStruct(shape, jnp.float32) for shape in shapes],
        scratch_shapes=[
            pltpu.VMEM((slab_dev * mem_dev, ny * nx // LANES, LANES), jnp.float32),
            pltpu.VMEM((mem_dev, cells.size, LANES), jnp.float32),
        ],
        cost_estimate=cost(60 * x.size, 4 * (2 * x.size + 2 * cv.size)),
        compiler_params=params(),
        name="forecast",
    )(cells, slabs, spread, x, cv, ch)
    return [outs[c * n : (c + 1) * n] for c in range(len(parts))]


def taper_kernel(nx, block, cells_ref, out_ref):
    depth = out_ref.shape[1]
    at = lax.broadcasted_iota(jnp.int32, (depth, LANES), 0)
    row = (lax.axis_index("mem") * block + at % block).astype(jnp.float32)
    col = (at // block * LANES + lax.broadcasted_iota(jnp.int32, (depth, LANES), 1)).astype(
        jnp.float32
    )

    def one(k, carry):
        cell = place(cells_ref, k)
        out_ref[k] = taper(
            row - (cell // nx).astype(jnp.float32), col - (cell % nx).astype(jnp.float32)
        )
        return carry

    lax.fori_loop(0, out_ref.shape[0], one, 0)


def taper_table(nx, block, cells):
    depth = block * nx // LANES
    total = cells.size
    return pl.pallas_call(
        functools.partial(taper_kernel, nx, block),
        in_specs=[SMEM],
        out_specs=VMEM,
        out_shape=jax.ShapeDtypeStruct((total, depth, LANES), jnp.float32),
        cost_estimate=cost(60 * total * depth * LANES, 4 * total * depth * LANES),
        compiler_params=params(),
        name="taper_table",
    )(cells)


def plan_kernel(nx, cells_ref, values_ref, errors_ref, *refs):
    tiles, (anom_ref, incr_ref) = refs[:-2], refs[-2:]
    total = cells_ref.shape[0] * cells_ref.shape[1]
    rows = tiles[0][...]
    for other in tiles[1:]:
        rows = rows + other[...]
    members = rows.shape[0]
    lane = lax.broadcasted_iota(jnp.int32, (1, LANES), 1)
    row_of = jnp.zeros((1, LANES), jnp.float32)
    col_of = jnp.zeros((1, LANES), jnp.float32)
    where = []
    for k in range(total):
        cell = place(cells_ref, k)
        row, col = (cell // nx).astype(jnp.float32), (cell % nx).astype(jnp.float32)
        where.append((row, col))
        row_of = jnp.where(lane == k, row, row_of)
        col_of = jnp.where(lane == k, col, col_of)
    mean = jnp.sum(rows, axis=0, keepdims=True) * (1.0 / members)
    rows = rows - mean
    for k in range(total):
        loc = taper(row_of - where[k][0], col_of - where[k][1])
        anomaly = jnp.broadcast_to(rows[:, k : k + 1], rows.shape)
        ybar = jnp.broadcast_to(mean[:, k : k + 1], mean.shape)
        variance = jnp.sum(anomaly * anomaly, axis=0, keepdims=True) / (members - 1) + 1e-06
        shared = jnp.sum(rows * anomaly, axis=0, keepdims=True)
        error, value = place(errors_ref, k), place(values_ref, k)
        scale = 1.0 / ((members - 1) * variance)
        shift = (ybar * error + value * variance) / (variance + error) - ybar
        shrink = jnp.sqrt(error / (variance + error)) - 1.0
        anom_ref[k] = anomaly * scale
        incr_ref[k] = shift + shrink * anomaly
        weight = loc * shared * scale
        mean = mean + weight * shift
        rows = rows + (weight * shrink) * anomaly


def filter_plan(nx, cells, values, errors, tiles):
    members = tiles[0].shape[0]
    total = cells.size
    table = jax.ShapeDtypeStruct((total, members, LANES), jnp.float32)
    return pl.pallas_call(
        functools.partial(plan_kernel, nx),
        in_specs=[SMEM] * 3 + [VMEM] * len(tiles),
        out_specs=[VMEM, VMEM],
        out_shape=[table, table],
        cost_estimate=cost(20_000_000, 4 * 2 * total * members * LANES),
        compiler_params=params(),
        name="filter_plan",
    )(cells, values, errors, *tiles)


def settle_kernel(n, mem_dev, count, depth, anom_ref, incr_ref, loc_ref, *refs):
    x_refs, out_refs = refs[:n], refs[n:]
    total = loc_ref.shape[0]
    members = n * mem_dev
    group = 2 if depth % (2 * TILE) == 0 and members <= 16 else 1
    span = group * TILE
    per_slab = depth // span

    def spread(ref, k, m):
        return ref[k, pl.ds(m, TILE, stride=0), :]

    def part(i, carry):
        slab, at = i // per_slab, (i % per_slab) * span

        def spot(m, g):
            row = ((m % mem_dev) * count + slab) * depth + at + g * TILE
            return m // mem_dev, pl.ds(pl.multiple_of(row, TILE), TILE)

        xs = []
        for m in range(members):
            for g in range(group):
                src, row = spot(m, g)
                xs.append(x_refs[src][row, :])

        def step(k, xs):
            sums = [None] * group
            for m in range(members):
                a = spread(anom_ref, k, m)
                for g in range(group):
                    term = a * xs[m * group + g]
                    sums[g] = term if m == 0 else sums[g] + term
            sums = [
                s * loc_ref[k, pl.ds(pl.multiple_of(at + g * TILE, TILE), TILE), :]
                for g, s in enumerate(sums)
            ]
            new = []
            for m in range(members):
                b = spread(incr_ref, k, m)
                for g in range(group):
                    new.append(xs[m * group + g] + b * sums[g])
            return tuple(new)

        xs = lax.fori_loop(0, total, step, tuple(xs), unroll=2)
        for m in range(members):
            for g in range(group):
                src, row = spot(m, g)
                out_refs[src][row, :] = xs[m * group + g]
        return carry

    lax.fori_loop(0, count * per_slab, part, 0)


def settle(mem_dev, count, depth, anom, incr, loc, xs):
    n = len(xs)
    shape = jax.ShapeDtypeStruct((mem_dev * count * depth, LANES), jnp.float32)
    size = n * mem_dev * count * depth * LANES
    return pl.pallas_call(
        functools.partial(settle_kernel, n, mem_dev, count, depth),
        in_specs=[VMEM] * (3 + n),
        out_specs=[VMEM] * n,
        out_shape=[shape] * n,
        cost_estimate=cost(4 * loc.shape[0] * size, 8 * size),
        compiler_params=params(),
        name="settle",
    )(anom, incr, loc, *xs)


def assemble_kernel(n, *refs):
    recv, out_ref, turn = refs[:n], refs[-2], refs[-1]
    mem_dev, _, ny, nx = out_ref.shape
    block = ny // n
    tiles = nx // LANES
    depth = block * tiles
    count = recv[0].shape[0] // (mem_dev * depth)
    slab = pl.program_id(0)
    me = lax.axis_index("mem")
    for m in range(mem_dev):
        at = pl.multiple_of((m * count + slab) * depth, TILE)
        for t in range(tiles):
            lanes = slice(t * LANES, (t + 1) * LANES)
            lines = pl.ds(at + t * block, block)
            for j in range(n):
                if block % TILE == 0:
                    row = pl.multiple_of((me ^ j) * block, block)
                    out_ref[m, 0, pl.ds(row, block), lanes] = recv[j][lines, :]
                else:
                    turn[pl.ds(j * block, block), :] = recv[j][lines, :]
            if block % TILE:
                for d in range(n):
                    out_ref[m, 0, d * block : (d + 1) * block, lanes] = turn[
                        pl.ds((me ^ d) * block, block), :
                    ]


def assemble(start, count, recv, shape, before):
    mem_dev, _, ny, nx = shape
    n = len(recv)
    extra = [] if before is None else [before]
    return pl.pallas_call(
        functools.partial(assemble_kernel, n),
        grid=(count,),
        in_specs=[VMEM] * n + [pl.BlockSpec(memory_space=pl.ANY)] * len(extra),
        out_specs=pl.BlockSpec((mem_dev, 1, ny, nx), lambda s: (0, start + s, 0, 0)),
        out_shape=jax.ShapeDtypeStruct(shape, jnp.float32),
        scratch_shapes=[pltpu.VMEM((ny, LANES), jnp.float32)],
        input_output_aliases={} if before is None else {n: 0},
        cost_estimate=cost(0, 8 * n * recv[0].size),
        compiler_params=params(),
        name="assemble",
    )(*recv, *extra)


def exchange(blocks):
    n = len(blocks)
    order = sorted(range(1, n), reverse=True)
    got = {
        j: lax.ppermute(blocks[j], "mem", [(i, i ^ j) for i in range(n)]) for j in order
    }
    return blocks[:1] + [got[j] for j in range(1, n)]


def body(x, cv, ch, spread, obs_cells, obs_slabs, obs_values, obs_error):
    mem_dev, slab_dev, ny, nx = x.shape
    n, lev = lax.axis_size("mem"), lax.axis_size("lev")
    block = ny // n
    depth = block * nx // LANES
    parts = chunks_of(slab_dev)
    sends = forecast(parts, n, obs_cells, obs_slabs, spread, x, cv, ch)
    states = []
    for blocks in sends:
        states.append(exchange(list(blocks)))
    loc = taper_table(nx, block, obs_cells)
    per = TILE // mem_dev
    seen = [s[mem_dev * parts[0][1] * depth :, :] for s in states[0]]
    seen = jnp.concatenate([sum(seen[g : g + per]) for g in range(0, n, per)])
    tiles = [seen] + [
        lax.ppermute(seen, "lev", [(i, (i + d) % lev) for i in range(lev)])
        for d in range(1, lev)
    ]
    anom, incr = filter_plan(nx, obs_cells, obs_values, obs_error, tiles)
    result = None
    for (start, count), state in zip(parts, states):
        new = settle(mem_dev, count, depth, anom, incr, loc, state)
        back = exchange(list(new))
        anom, _ = lax.optimization_barrier((anom, new[0]))
        result = assemble(start, count, back, x.shape, result)
    return result


def solution(mesh):
    in_specs = (
        P("mem", "lev", None, None),
        P("lev", None, None),
        P("lev", None, None),
        P("lev"),
        P(),
        P(),
        P(),
        P(),
    )
    out_specs = P("mem", "lev", None, None)
    return jax.shard_map(body, mesh=mesh, in_specs=in_specs, out_specs=out_specs, check_vma=False)
```

time: 104 us -> 92.6 us (0.89)
  starting transfers between devices: 13.4 us -> 53.1 us
  blocking collectives: 23.4 us -> 0 us
  waiting for transfers between devices: 27.4 us -> 11.6 us
  Pallas kernels: 32.6 us -> 21.9 us
    ppermute x0 -> x28, starting transfers between devices: none -> 49.9 us  [exchange(): lax.ppermute(blocks[j], 'mem', [(i, i ^ j) for i in range(n)])]
    all_to_all x3 -> x0, waiting for transfers between devices: 27.4 us -> none  [the longest x2 25.9 us: body(): back = lax.all_to_all(new, 'mem', split_axis=0, concat_axis=0, tiled=True)]
    all_to_all x1 -> x0, blocking collectives: 23.4 us -> none  [body(): lax.all_to_all(s, 'mem', split_axis=0, concat_axis=0, tiled=True)]
    all_to_all x3 -> x0, starting transfers between devices: 11.6 us -> none  [the longest x2 8.08 us: body(): back = lax.all_to_all(new, 'mem', split_axis=0, concat_axis=0, tiled=True)]
    ppermute x0 -> x28, waiting for transfers between devices: none -> 11.1 us  [exchange(): lax.ppermute(blocks[j], 'mem', [(i, i ^ j) for i in range(n)])]
    pallas_call x3, Pallas kernels: 18.8 us -> 13.3 us  [the longest x2 9.11 us: settle(): pl.pallas_call(functools.partial(settle_kernel, n, mem_dev, count, depth)...]
    reshape x4 -> x0, local copies, waits for them, and re-layouts: 3.92 us -> none  [the longest x2 2.65 us: body(): cells, slabs = (obs_cells.reshape(-1), obs_slabs.reshape(-1))]
    unnamed x20 -> x16, local copies, waits for them, and re-layouts: 2.07 us -> 5.51 us
  transfers between devices with their start and end apart: 6 -> 31, of which waited for: 3 -> 7; matrix products, arithmetic and copies ran while one was open for 1% -> 0% of each run, Pallas kernels for 23% -> 18%
where the time goes in v2:
time: 92.6 us; the launch traced here: 92.3 us
  starting transfers between devices  53.1 us (57%)
  Pallas kernels  21.9 us (24%)
  waiting for transfers between devices  11.6 us (13%)
  local copies, waits for them, and re-layouts  5.51 us (6%)
    ppermute x28, starting transfers between devices, exchange(): lax.ppermute(blocks[j], 'mem', [(i, i ^ j) for i in range(n)])  49.9 us
    ppermute x28, waiting for transfers between devices, exchange(): lax.ppermute(blocks[j], 'mem', [(i, i ^ j) for i in range(n)])  11.1 us
    pallas_call x2, Pallas kernels, settle(): pl.pallas_call(functools.partial(settle_kernel, n, mem_dev, count, depth)...  9.11 us
    unnamed x16, local copies, waits for them, and re-layouts  5.51 us
    pallas_call x1, Pallas kernels, forecast(): pl.pallas_call(functools.partial(forecast_kernel, parts, n), grid=(slab_d...  4.21 us
    pallas_call x1, Pallas kernels, filter_plan(): pl.pallas_call(functools.partial(plan_kernel, nx), in_specs=[SMEM] * 3 +...  4.2 us
    ppermute x3, starting transfers between devices, body(): lax.ppermute(seen, 'lev', [(i, (i + d) % lev) for i in range(lev)])  3.29 us
    pallas_call x2, Pallas kernels, assemble(): pl.pallas_call(functools.partial(assemble_kernel, n), grid=(count,), in_s...  2.33 us
  transfers between devices with their start and end apart: 31, of which 7 were waited for; matrix products, arithmetic and copies ran while one was open for 0% of the time, Pallas kernels for 18%

profile of v2, /device:TPU:0, one launch (start us, length us, event | category | flops | bytes accessed | tf_op | source)
XLA Modules:
  0.0 92.3 jit_solution(12362153487200134932)
XLA Ops:
  5.5 4.2 %forecast.1 = (f32[136,128]{1,0:T(8,128)S(1)}, f32[136,128]{1,0:T(8,128)S(1)}, f32[136,128]{1,0:T(8,128)S(1)}, f32[136,128]{1,0:T(8,128)S(1)}, f32[136,128]{1,0:...) custom-call(s32[2,16]{1,0:T(2,128)S(1)} %copy-done.3, ...), custom_call_target="tpu_custom_call" | custom-call | flops 19660800 | bytes 3932160 | tf_op jit(solution)/shard_map/forecast/pallas_call | solution.py:134
  9.7 3.1 %collective-permute-start = (f32[136,128]{1,0:T(8,128)S(1)}, f32[136,128]{1,0:T(8,128)S(1)}, u32[]{:S(2)}, u32[]{:S(2)}) collective-permute-start(f32[136,128]{1,0:T(8,128)S(1)} %get-tuple-element.41), channel_id=1, source_target_pairs={{0,4},{4,0},{8,12},{12,8},{16,20},{20,16},{24,28},{28,24},{1,5},{5... | collective-permute-start | bytes 208904 | tf_op jit(solution)/shard_map/ppermute | solution.py:357
  14.4 3.0 %collective-permute-start.3 = (f32[136,128]{1,0:T(8,128)S(1)}, f32[136,128]{1,0:T(8,128)S(1)}, u32[]{:S(2)}, u32[]{:S(2)}) collective-permute-start(f32[136,128]{1,0:T(8,128)S(1)} %get-tuple-element.44), channel_id=1, source_target_pairs={{0,16},{4,20},{8,24},{12,28},{16,0},{20,4},{24,8},{28,12},{1,17},{... | collective-permute-start | bytes 208904 | tf_op jit(solution)/shard_map/ppermute | solution.py:357
  18.6 3.6 %collective-permute-start.5 = (f32[136,128]{1,0:T(8,128)S(1)}, f32[136,128]{1,0:T(8,128)S(1)}, u32[]{:S(2)}, u32[]{:S(2)}) collective-permute-start(f32[136,128]{1,0:T(8,128)S(1)} %get-tuple-element.46), channel_id=1, source_target_pairs={{0,24},{4,28},{8,16},{12,20},{16,8},{20,12},{24,0},{28,4},{1,25},{... | collective-permute-start | bytes 208904 | tf_op jit(solution)/shard_map/ppermute | solution.py:357
  22.3 1.7 %collective-permute-start.10 = (f32[192,128]{1,0:T(8,128)S(1)}, f32[192,128]{1,0:T(8,128)S(1)}, u32[]{:S(2)}, u32[]{:S(2)}) collective-permute-start(f32[192,128]{1,0:T(8,128)S(1)} %get-tuple-element.53), channel_id=1, source_target_pairs={{0,4},{4,0},{8,12},{12,8},{16,20},{20,16},{24,28},{28,24},{1,5},{5... | collective-permute-start | bytes 294920 | tf_op jit(solution)/shard_map/ppermute | solution.py:357
  24.4 3.7 %collective-permute-done.4.refs_5_ = f32[136,128]{1,0:T(8,128)S(1)} collective-permute-done((f32[136,128]{1,0:T(8,128)S(1)}, f32[136,128]{1,0:T(8,128)S(1)}, u32[]{:S(2)}, u32[]{:S(2)}) %collective-permute-start.4) | collective-permute-done | bytes 69664 | tf_op jit(solution)/shard_map/ppermute | solution.py:357
  31.6 1.7 %collective-permute-start.7 = (f32[16,128]{1,0:T(8,128)S(1)}, f32[16,128]{1,0:T(8,128)S(1)}, u32[]{:S(2)}, u32[]{:S(2)}) collective-permute-start(f32[16,128]{1,0:T(8,128)S(1)} %pad_maximum_fusion.refs_0_), channel_id=1, source_target_pairs={{0,1},{1,2},{2,3},{3,0},{4,5},{5,6},{6,7},{7,4},{8,9},{9,10},{10,1... | collective-permute-start | bytes 24584 | tf_op jit(solution)/shard_map/ppermute | solution.py:377
  33.8 3.6 %collective-permute-start.13 = (f32[192,128]{1,0:T(8,128)S(1)}, f32[192,128]{1,0:T(8,128)S(1)}, u32[]{:S(2)}, u32[]{:S(2)}) collective-permute-start(f32[192,128]{1,0:T(8,128)S(1)} %get-tuple-element.56), channel_id=1, source_target_pairs={{0,16},{4,20},{8,24},{12,28},{16,0},{20,4},{24,8},{28,12},{1,17},{... | collective-permute-start | bytes 294920 | tf_op jit(solution)/shard_map/ppermute | solution.py:357
  37.8 2.2 %collective-permute-start.15 = (f32[192,128]{1,0:T(8,128)S(1)}, f32[192,128]{1,0:T(8,128)S(1)}, u32[]{:S(2)}, u32[]{:S(2)}) collective-permute-start(f32[192,128]{1,0:T(8,128)S(1)} %get-tuple-element.58), channel_id=1, source_target_pairs={{0,24},{4,28},{8,16},{12,20},{16,8},{20,12},{24,0},{28,4},{1,25},{... | collective-permute-start | bytes 294920 | tf_op jit(solution)/shard_map/ppermute | solution.py:357
  40.0 2.9 %collective-permute-start.16 = (f32[192,128]{1,0:T(8,128)S(1)}, f32[192,128]{1,0:T(8,128)S(1)}, u32[]{:S(2)}, u32[]{:S(2)}) collective-permute-start(f32[192,128]{1,0:T(8,128)S(1)} %get-tuple-element.59), channel_id=1, source_target_pairs={{0,28},{4,24},{8,20},{12,16},{16,12},{20,8},{24,4},{28,0},{1,29},{... | collective-permute-start | bytes 294920 | tf_op jit(solution)/shard_map/ppermute | solution.py:357
  42.9 2.1 %taper_table.1.loc_ref = f32[32,32,128]{2,1,0:T(8,128)S(1)} custom-call(s32[2,16]{1,0:T(2,128)S(1)} %copy-done.3), custom_call_target="tpu_custom_call" | custom-call | flops 7864320 | bytes 524288 | tf_op jit(solution)/shard_map/taper_table/pallas_call | solution.py:179
  45.0 4.2 %filter_plan.1 = (f32[32,16,128]{2,1,0:T(8,128)S(1)}, f32[32,16,128]{2,1,0:T(8,128)S(1)}) custom-call(s32[2,16]{1,0:T(2,128)S(1)} %copy-done.3, f32[2,16]{1,0:T(2,128)S(1)} %copy-done.6, f32[2,16]{1,0:T(2,128)S(1)} %copy-done.7, f32[16,128]{1,0:T(8,128)S(1)} %pad_maximum_fusion.refs_0_, f32[16,128]{1,0:T(8,128)S(1)} %collective-permute-done.7.refs_1_, ...), custom_call_target="tpu_custom_call" | custom-call | flops 20000000 | bytes 524288 | tf_op jit(solution)/shard_map/filter_plan/pallas_call | solution.py:230
  49.2 3.7 %settle.2 = (f32[128,128]{1,0:T(8,128)S(1)}, f32[128,128]{1,0:T(8,128)S(1)}, f32[128,128]{1,0:T(8,128)S(1)}, f32[128,128]{1,0:T(8,128)S(1)}, f32[128,128]{1,0:T(...) custom-call(f32[32,16,128]{2,1,0:T(8,128)S(1)} %get-tuple-element.51.anom_ref, ...), custom_call_target="tpu_custom_call" | custom-call | flops 16777216 | bytes 1048576 | tf_op jit(solution)/shard_map/settle/pallas_call | solution.py:297
  53.3 3.1 %collective-permute-start.26 = (f32[128,128]{1,0:T(8,128)S(1)}, f32[128,128]{1,0:T(8,128)S(1)}, u32[]{:S(2)}, u32[]{:S(2)}) collective-permute-start(f32[128,128]{1,0:T(8,128)S(1)} %get-tuple-element.70), channel_id=1, source_target_pairs={{0,12},{4,8},{8,4},{12,0},{16,28},{20,24},{24,20},{28,16},{1,13},{... | collective-permute-start | bytes 196616 | tf_op jit(solution)/shard_map/ppermute | solution.py:357
  56.7 5.5 %settle.3 = (f32[192,128]{1,0:T(8,128)S(1)}, f32[192,128]{1,0:T(8,128)S(1)}, f32[192,128]{1,0:T(8,128)S(1)}, f32[192,128]{1,0:T(8,128)S(1)}, f32[192,128]{1,0:T(...) custom-call(f32[32,16,128]{2,1,0:T(8,128)S(1)} %get-tuple-element.51.anom_ref, ...), custom_call_target="tpu_custom_call" | custom-call | flops 25165824 | bytes 1572864 | tf_op jit(solution)/shard_map/settle/pallas_call | solution.py:297
  63.0 2.0 %collective-permute-start.18 = (f32[192,128]{1,0:T(8,128)S(1)}, f32[192,128]{1,0:T(8,128)S(1)}, u32[]{:S(2)}, u32[]{:S(2)}) collective-permute-start(f32[192,128]{1,0:T(8,128)S(1)} %get-tuple-element.62), channel_id=1, source_target_pairs={{0,8},{4,12},{8,0},{12,4},{16,24},{20,28},{24,16},{28,20},{1,9},{5... | collective-permute-start | bytes 294920 | tf_op jit(solution)/shard_map/ppermute | solution.py:357
  66.4 1.7 %collective-permute-start.29 = (f32[128,128]{1,0:T(8,128)S(1)}, f32[128,128]{1,0:T(8,128)S(1)}, u32[]{:S(2)}, u32[]{:S(2)}) collective-permute-start(f32[128,128]{1,0:T(8,128)S(1)} %get-tuple-element.73), channel_id=1, source_target_pairs={{0,24},{4,28},{8,16},{12,20},{16,8},{20,12},{24,0},{28,4},{1,25},{... | collective-permute-start | bytes 196616 | tf_op jit(solution)/shard_map/ppermute | solution.py:357
  68.1 2.1 %collective-permute-start.30 = (f32[128,128]{1,0:T(8,128)S(1)}, f32[128,128]{1,0:T(8,128)S(1)}, u32[]{:S(2)}, u32[]{:S(2)}) collective-permute-start(f32[128,128]{1,0:T(8,128)S(1)} %get-tuple-element.74), channel_id=1, source_target_pairs={{0,28},{4,24},{8,20},{12,16},{16,12},{20,8},{24,4},{28,0},{1,29},{... | collective-permute-start | bytes 196616 | tf_op jit(solution)/shard_map/ppermute | solution.py:357
  70.2 2.1 %collective-permute-done.28.refs_5_ = f32[128,128]{1,0:T(8,128)S(1)} collective-permute-done((f32[128,128]{1,0:T(8,128)S(1)}, f32[128,128]{1,0:T(8,128)S(1)}, u32[]{:S(2)}, u32[]{:S(2)}) %collective-permute-start.28) | collective-permute-done | bytes 65568 | tf_op jit(solution)/shard_map/ppermute | solution.py:357
  72.9 5.4 %collective-permute-start.20 = (f32[192,128]{1,0:T(8,128)S(1)}, f32[192,128]{1,0:T(8,128)S(1)}, u32[]{:S(2)}, u32[]{:S(2)}) collective-permute-start(f32[192,128]{1,0:T(8,128)S(1)} %get-tuple-element.64), channel_id=1, source_target_pairs={{0,16},{4,20},{8,24},{12,28},{16,0},{20,4},{24,8},{28,12},{1,17},{... | collective-permute-start | bytes 294920 | tf_op jit(solution)/shard_map/ppermute | solution.py:357
  78.4 3.9 %collective-permute-start.21 = (f32[192,128]{1,0:T(8,128)S(1)}, f32[192,128]{1,0:T(8,128)S(1)}, u32[]{:S(2)}, u32[]{:S(2)}) collective-permute-start(f32[192,128]{1,0:T(8,128)S(1)} %get-tuple-element.65), channel_id=1, source_target_pairs={{0,20},{4,16},{8,28},{12,24},{16,4},{20,0},{24,12},{28,8},{1,21},{... | collective-permute-start | bytes 294920 | tf_op jit(solution)/shard_map/ppermute | solution.py:357
  83.4 2.7 %collective-permute-start.23 = (f32[192,128]{1,0:T(8,128)S(1)}, f32[192,128]{1,0:T(8,128)S(1)}, u32[]{:S(2)}, u32[]{:S(2)}) collective-permute-start(f32[192,128]{1,0:T(8,128)S(1)} %get-tuple-element.67), channel_id=1, source_target_pairs={{0,28},{4,24},{8,20},{12,16},{16,12},{20,8},{24,4},{28,0},{1,29},{... | collective-permute-start | bytes 294920 | tf_op jit(solution)/shard_map/ppermute | solution.py:357
  86.9 1.9 %collective-permute-done.22.refs_6_ = f32[192,128]{1,0:T(8,128)S(1)} collective-permute-done((f32[192,128]{1,0:T(8,128)S(1)}, f32[192,128]{1,0:T(8,128)S(1)}, u32[]{:S(2)}, u32[]{:S(2)}) %collective-permute-start.22) | collective-permute-done | bytes 98336 | tf_op jit(solution)/shard_map/ppermute | solution.py:357
  88.8 2.0 %collective-permute-done.23.refs_7_ = f32[192,128]{1,0:T(8,128)S(1)} collective-permute-done((f32[192,128]{1,0:T(8,128)S(1)}, f32[192,128]{1,0:T(8,128)S(1)}, u32[]{:S(2)}, u32[]{:S(2)}) %collective-permute-start.23) | collective-permute-done | bytes 98336 | tf_op jit(solution)/shard_map/ppermute | solution.py:357
  (64 shorter events, 20.5 us)
Async XLA Ops:
  9.7 8.9 %collective-permute-start = (f32[136,128]{1,0:T(8,128)S(1)}, f32[136,128]{1,0:T(8,128)S(1)}, u32[]{:S(2)}, u32[]{:S(2)}) collective-permute-start(f32[136,128]{1,0:T(8,128)S(1)} %get-tuple-element.41), channel_id=1, source_target_pairs={{0,4},{4,0},{8,12},{12,8},{16,20},{20,16},{24,28},{28,24},{1,5},{5... | collective-permute-start | bytes 208904 | tf_op jit(solution)/shard_map/ppermute | solution.py:357
  12.8 9.5 %collective-permute-start.1 = (f32[136,128]{1,0:T(8,128)S(1)}, f32[136,128]{1,0:T(8,128)S(1)}, u32[]{:S(2)}, u32[]{:S(2)}) collective-permute-start(f32[136,128]{1,0:T(8,128)S(1)} %get-tuple-element.42), channel_id=1, source_target_pairs={{0,8},{4,12},{8,0},{12,4},{16,24},{20,28},{24,16},{28,20},{1,9},{5... | collective-permute-start | bytes 208904 | tf_op jit(solution)/shard_map/ppermute | solution.py:357
  14.4 7.9 %collective-permute-start.2 = (f32[136,128]{1,0:T(8,128)S(1)}, f32[136,128]{1,0:T(8,128)S(1)}, u32[]{:S(2)}, u32[]{:S(2)}) collective-permute-start(f32[136,128]{1,0:T(8,128)S(1)} %get-tuple-element.43), channel_id=1, source_target_pairs={{0,12},{4,8},{8,4},{12,0},{16,28},{20,24},{24,20},{28,16},{1,13},{... | collective-permute-start | bytes 208904 | tf_op jit(solution)/shard_map/ppermute | solution.py:357
  14.4 9.6 %collective-permute-start.3 = (f32[136,128]{1,0:T(8,128)S(1)}, f32[136,128]{1,0:T(8,128)S(1)}, u32[]{:S(2)}, u32[]{:S(2)}) collective-permute-start(f32[136,128]{1,0:T(8,128)S(1)} %get-tuple-element.44), channel_id=1, source_target_pairs={{0,16},{4,20},{8,24},{12,28},{16,0},{20,4},{24,8},{28,12},{1,17},{... | collective-permute-start | bytes 208904 | tf_op jit(solution)/shard_map/ppermute | solution.py:357
  17.3 10.7 %collective-permute-start.4 = (f32[136,128]{1,0:T(8,128)S(1)}, f32[136,128]{1,0:T(8,128)S(1)}, u32[]{:S(2)}, u32[]{:S(2)}) collective-permute-start(f32[136,128]{1,0:T(8,128)S(1)} %get-tuple-element.45), channel_id=1, source_target_pairs={{0,20},{4,16},{8,28},{12,24},{16,4},{20,0},{24,12},{28,8},{1,21},{... | collective-permute-start | bytes 208904 | tf_op jit(solution)/shard_map/ppermute | solution.py:357
  18.6 10.1 %collective-permute-start.5 = (f32[136,128]{1,0:T(8,128)S(1)}, f32[136,128]{1,0:T(8,128)S(1)}, u32[]{:S(2)}, u32[]{:S(2)}) collective-permute-start(f32[136,128]{1,0:T(8,128)S(1)} %get-tuple-element.46), channel_id=1, source_target_pairs={{0,24},{4,28},{8,16},{12,20},{16,8},{20,12},{24,0},{28,4},{1,25},{... | collective-permute-start | bytes 208904 | tf_op jit(solution)/shard_map/ppermute | solution.py:357
  22.2 7.8 %collective-permute-start.6 = (f32[136,128]{1,0:T(8,128)S(1)}, f32[136,128]{1,0:T(8,128)S(1)}, u32[]{:S(2)}, u32[]{:S(2)}) collective-permute-start(f32[136,128]{1,0:T(8,128)S(1)} %get-tuple-element.47), channel_id=1, source_target_pairs={{0,28},{4,24},{8,20},{12,16},{16,12},{20,8},{24,4},{28,0},{1,29},{... | collective-permute-start | bytes 208904 | tf_op jit(solution)/shard_map/ppermute | solution.py:357
  22.3 15.6 %collective-permute-start.10 = (f32[192,128]{1,0:T(8,128)S(1)}, f32[192,128]{1,0:T(8,128)S(1)}, u32[]{:S(2)}, u32[]{:S(2)}) collective-permute-start(f32[192,128]{1,0:T(8,128)S(1)} %get-tuple-element.53), channel_id=1, source_target_pairs={{0,4},{4,0},{8,12},{12,8},{16,20},{20,16},{24,28},{28,24},{1,5},{5... | collective-permute-start | bytes 294920 | tf_op jit(solution)/shard_map/ppermute | solution.py:357
  23.9 16.1 %collective-permute-start.11 = (f32[192,128]{1,0:T(8,128)S(1)}, f32[192,128]{1,0:T(8,128)S(1)}, u32[]{:S(2)}, u32[]{:S(2)}) collective-permute-start(f32[192,128]{1,0:T(8,128)S(1)} %get-tuple-element.54), channel_id=1, source_target_pairs={{0,8},{4,12},{8,0},{12,4},{16,24},{20,28},{24,16},{28,20},{1,9},{5... | collective-permute-start | bytes 294920 | tf_op jit(solution)/shard_map/ppermute | solution.py:357
  28.1 24.7 %collective-permute-start.12 = (f32[192,128]{1,0:T(8,128)S(1)}, f32[192,128]{1,0:T(8,128)S(1)}, u32[]{:S(2)}, u32[]{:S(2)}) collective-permute-start(f32[192,128]{1,0:T(8,128)S(1)} %get-tuple-element.55), channel_id=1, source_target_pairs={{0,12},{4,8},{8,4},{12,0},{16,28},{20,24},{24,20},{28,16},{1,13},{... | collective-permute-start | bytes 294920 | tf_op jit(solution)/shard_map/ppermute | solution.py:357
  33.8 19.4 %collective-permute-start.13 = (f32[192,128]{1,0:T(8,128)S(1)}, f32[192,128]{1,0:T(8,128)S(1)}, u32[]{:S(2)}, u32[]{:S(2)}) collective-permute-start(f32[192,128]{1,0:T(8,128)S(1)} %get-tuple-element.56), channel_id=1, source_target_pairs={{0,16},{4,20},{8,24},{12,28},{16,0},{20,4},{24,8},{28,12},{1,17},{... | collective-permute-start | bytes 294920 | tf_op jit(solution)/shard_map/ppermute | solution.py:357
  37.3 16.0 %collective-permute-start.14 = (f32[192,128]{1,0:T(8,128)S(1)}, f32[192,128]{1,0:T(8,128)S(1)}, u32[]{:S(2)}, u32[]{:S(2)}) collective-permute-start(f32[192,128]{1,0:T(8,128)S(1)} %get-tuple-element.57), channel_id=1, source_target_pairs={{0,20},{4,16},{8,28},{12,24},{16,4},{20,0},{24,12},{28,8},{1,21},{... | collective-permute-start | bytes 294920 | tf_op jit(solution)/shard_map/ppermute | solution.py:357
  37.8 18.6 %collective-permute-start.15 = (f32[192,128]{1,0:T(8,128)S(1)}, f32[192,128]{1,0:T(8,128)S(1)}, u32[]{:S(2)}, u32[]{:S(2)}) collective-permute-start(f32[192,128]{1,0:T(8,128)S(1)} %get-tuple-element.58), channel_id=1, source_target_pairs={{0,24},{4,28},{8,16},{12,20},{16,8},{20,12},{24,0},{28,4},{1,25},{... | collective-permute-start | bytes 294920 | tf_op jit(solution)/shard_map/ppermute | solution.py:357
  40.0 16.7 %collective-permute-start.16 = (f32[192,128]{1,0:T(8,128)S(1)}, f32[192,128]{1,0:T(8,128)S(1)}, u32[]{:S(2)}, u32[]{:S(2)}) collective-permute-start(f32[192,128]{1,0:T(8,128)S(1)} %get-tuple-element.59), channel_id=1, source_target_pairs={{0,28},{4,24},{8,20},{12,16},{16,12},{20,8},{24,4},{28,0},{1,29},{... | collective-permute-start | bytes 294920 | tf_op jit(solution)/shard_map/ppermute | solution.py:357
  52.8 10.1 %collective-permute-start.24 = (f32[128,128]{1,0:T(8,128)S(1)}, f32[128,128]{1,0:T(8,128)S(1)}, u32[]{:S(2)}, u32[]{:S(2)}) collective-permute-start(f32[128,128]{1,0:T(8,128)S(1)} %get-tuple-element.68), channel_id=1, source_target_pairs={{0,4},{4,0},{8,12},{12,8},{16,20},{20,16},{24,28},{28,24},{1,5},{5... | collective-permute-start | bytes 196616 | tf_op jit(solution)/shard_map/ppermute | solution.py:357
  53.2 11.8 %collective-permute-start.25 = (f32[128,128]{1,0:T(8,128)S(1)}, f32[128,128]{1,0:T(8,128)S(1)}, u32[]{:S(2)}, u32[]{:S(2)}) collective-permute-start(f32[128,128]{1,0:T(8,128)S(1)} %get-tuple-element.69), channel_id=1, source_target_pairs={{0,8},{4,12},{8,0},{12,4},{16,24},{20,28},{24,16},{28,20},{1,9},{5... | collective-permute-start | bytes 196616 | tf_op jit(solution)/shard_map/ppermute | solution.py:357
  53.3 13.1 %collective-permute-start.26 = (f32[128,128]{1,0:T(8,128)S(1)}, f32[128,128]{1,0:T(8,128)S(1)}, u32[]{:S(2)}, u32[]{:S(2)}) collective-permute-start(f32[128,128]{1,0:T(8,128)S(1)} %get-tuple-element.70), channel_id=1, source_target_pairs={{0,12},{4,8},{8,4},{12,0},{16,28},{20,24},{24,20},{28,16},{1,13},{... | collective-permute-start | bytes 196616 | tf_op jit(solution)/shard_map/ppermute | solution.py:357
  56.4 11.7 %collective-permute-start.27 = (f32[128,128]{1,0:T(8,128)S(1)}, f32[128,128]{1,0:T(8,128)S(1)}, u32[]{:S(2)}, u32[]{:S(2)}) collective-permute-start(f32[128,128]{1,0:T(8,128)S(1)} %get-tuple-element.71), channel_id=1, source_target_pairs={{0,16},{4,20},{8,24},{12,28},{16,0},{20,4},{24,8},{28,12},{1,17},{... | collective-permute-start | bytes 196616 | tf_op jit(solution)/shard_map/ppermute | solution.py:357
  62.2 20.1 %collective-permute-start.17 = (f32[192,128]{1,0:T(8,128)S(1)}, f32[192,128]{1,0:T(8,128)S(1)}, u32[]{:S(2)}, u32[]{:S(2)}) collective-permute-start(f32[192,128]{1,0:T(8,128)S(1)} %get-tuple-element.61), channel_id=1, source_target_pairs={{0,4},{4,0},{8,12},{12,8},{16,20},{20,16},{24,28},{28,24},{1,5},{5... | collective-permute-start | bytes 294920 | tf_op jit(solution)/shard_map/ppermute | solution.py:357
  63.0 20.4 %collective-permute-start.18 = (f32[192,128]{1,0:T(8,128)S(1)}, f32[192,128]{1,0:T(8,128)S(1)}, u32[]{:S(2)}, u32[]{:S(2)}) collective-permute-start(f32[192,128]{1,0:T(8,128)S(1)} %get-tuple-element.62), channel_id=1, source_target_pairs={{0,8},{4,12},{8,0},{12,4},{16,24},{20,28},{24,16},{28,20},{1,9},{5... | collective-permute-start | bytes 294920 | tf_op jit(solution)/shard_map/ppermute | solution.py:357
  68.1 10.2 %collective-permute-start.30 = (f32[128,128]{1,0:T(8,128)S(1)}, f32[128,128]{1,0:T(8,128)S(1)}, u32[]{:S(2)}, u32[]{:S(2)}) collective-permute-start(f32[128,128]{1,0:T(8,128)S(1)} %get-tuple-element.74), channel_id=1, source_target_pairs={{0,28},{4,24},{8,20},{12,16},{16,12},{20,8},{24,4},{28,0},{1,29},{... | collective-permute-start | bytes 196616 | tf_op jit(solution)/shard_map/ppermute | solution.py:357
  72.3 14.6 %collective-permute-start.19 = (f32[192,128]{1,0:T(8,128)S(1)}, f32[192,128]{1,0:T(8,128)S(1)}, u32[]{:S(2)}, u32[]{:S(2)}) collective-permute-start(f32[192,128]{1,0:T(8,128)S(1)} %get-tuple-element.63), channel_id=1, source_target_pairs={{0,12},{4,8},{8,4},{12,0},{16,28},{20,24},{24,20},{28,16},{1,13},{... | collective-permute-start | bytes 294920 | tf_op jit(solution)/shard_map/ppermute | solution.py:357
  72.9 14.0 %collective-permute-start.20 = (f32[192,128]{1,0:T(8,128)S(1)}, f32[192,128]{1,0:T(8,128)S(1)}, u32[]{:S(2)}, u32[]{:S(2)}) collective-permute-start(f32[192,128]{1,0:T(8,128)S(1)} %get-tuple-element.64), channel_id=1, source_target_pairs={{0,16},{4,20},{8,24},{12,28},{16,0},{20,4},{24,8},{28,12},{1,17},{... | collective-permute-start | bytes 294920 | tf_op jit(solution)/shard_map/ppermute | solution.py:357
  78.4 8.6 %collective-permute-start.21 = (f32[192,128]{1,0:T(8,128)S(1)}, f32[192,128]{1,0:T(8,128)S(1)}, u32[]{:S(2)}, u32[]{:S(2)}) collective-permute-start(f32[192,128]{1,0:T(8,128)S(1)} %get-tuple-element.65), channel_id=1, source_target_pairs={{0,20},{4,16},{8,28},{12,24},{16,4},{20,0},{24,12},{28,8},{1,21},{... | collective-permute-start | bytes 294920 | tf_op jit(solution)/shard_map/ppermute | solution.py:357
  (15 other events, 123.2 us)

commit v3 on v2

v3 whole, which is shorter than its diff:
```python
import functools

import jax
import jax.numpy as jnp
from jax import lax
from jax.experimental import pallas as pl
from jax.experimental.pallas import tpu as pltpu
from jax.sharding import PartitionSpec as P


STEPS = 2
LOC_HALF = 64
LANES = 128
GRANT = 24 * 1024 * 1024
TILE = 8
VMEM = pl.BlockSpec(memory_space=pltpu.VMEM)
SMEM = pl.BlockSpec(memory_space=pltpu.SMEM)


def cost(flops, nbytes):
    return pl.CostEstimate(flops=flops, bytes_accessed=nbytes, transcendentals=0)


def taper(row_gap, col_gap):
    scaled = jnp.sqrt(row_gap * row_gap + col_gap * col_gap) * (1.0 / LOC_HALF)
    inner = (
        ((-0.25 * scaled + 0.5) * scaled + 0.625) * scaled - 5.0 / 3.0
    ) * scaled * scaled + 1.0
    safe = jnp.maximum(scaled, 1.0)
    outer = (
        ((((scaled * (1.0 / 12.0) - 0.5) * scaled + 0.625) * scaled + 5.0 / 3.0) * scaled - 5.0)
        * scaled
        + 4.0
        - (2.0 / 3.0) / safe
    )
    return jnp.where(scaled <= 1.0, inner, jnp.where(scaled < 2.0, outer, 0.0))


def chunks_of(slab_dev):
    first = max(1, (2 * slab_dev) // 5)
    if slab_dev == 1:
        return ((0, 1, True),)
    return ((0, first, True), (first, slab_dev - first, False))


def place(ref, k):
    return ref[k // ref.shape[1], k % ref.shape[1]]


def params():
    return pltpu.CompilerParams(vmem_limit_bytes=GRANT)


def blocks_in(refs, n, whole):
    me = lax.axis_index("mem")
    if whole:
        return [(refs[0].at[d], d) for d in range(n)]
    return [(refs[j], me ^ j) for j in range(n)]


def block_shapes(n, whole, rows):
    if whole:
        return [jax.ShapeDtypeStruct((n, rows, LANES), jnp.float32)]
    return [jax.ShapeDtypeStruct((rows, LANES), jnp.float32)] * n


def forecast_kernel(parts, n, cells_hbm, slabs_hbm, spread_hbm, x_hbm, cv_hbm, ch_hbm, *rest):
    outs = []
    for start, count, whole in parts:
        width = 1 if whole else n
        outs.append(blocks_in(rest[:width], n, whole))
        rest = rest[width:]
    x_buf, cv_buf, ch_buf, cells, slabs, spread, field, picks, sem, small = rest
    slab_dev, mem_dev, ny, nx = x_buf.shape
    block = ny // n
    tiles = nx // LANES
    depth = block * tiles
    total = cells.shape[0] * cells.shape[1]

    def loads(s):
        return (
            pltpu.make_async_copy(x_hbm.at[:, s], x_buf.at[s], sem.at[0, s]),
            pltpu.make_async_copy(cv_hbm.at[s], cv_buf.at[s], sem.at[1, s]),
            pltpu.make_async_copy(ch_hbm.at[s], ch_buf.at[s], sem.at[2, s]),
        )

    lists = (
        pltpu.make_async_copy(spread_hbm, spread, small.at[0]),
        pltpu.make_async_copy(cells_hbm, cells, small.at[1]),
        pltpu.make_async_copy(slabs_hbm, slabs, small.at[2]),
    )
    for copy in lists:
        copy.start()
    for s in range(slab_dev):
        for copy in loads(s):
            copy.start()
    for copy in lists:
        copy.wait()
    rows = lax.broadcasted_iota(jnp.int32, (ny, nx), 0)
    cols = lax.broadcasted_iota(jnp.int32, (ny, nx), 1)

    for (start, count, whole), blocks in zip(parts, outs):

        def one(s, carry):
            slab = start + s
            for copy in loads(slab):
                copy.wait()
            diffuse = spread[slab]
            half_v = 0.5 * cv_buf[slab]
            half_h = 0.5 * ch_buf[slab]
            east_w, west_w = diffuse - half_v, diffuse + half_v
            north_w, south_w = diffuse - half_h, diffuse + half_h
            for m in range(mem_dev):
                f = x_buf[slab, m]
                for _ in range(STEPS):
                    east = jnp.where(cols == nx - 1, f, pltpu.roll(f, nx - 1, 1))
                    west = jnp.where(cols == 0, f, pltpu.roll(f, 1, 1))
                    north = jnp.where(rows == ny - 1, f, pltpu.roll(f, ny - 1, 0))
                    south = jnp.where(rows == 0, f, pltpu.roll(f, 1, 0))
                    f = (
                        (1.0 - 4.0 * diffuse) * f
                        + east_w * east
                        + west_w * west
                        + north_w * north
                        + south_w * south
                    )
                for t in range(tiles):
                    field[slab * mem_dev + m, pl.ds(t * ny, ny), :] = f[
                        :, t * LANES : (t + 1) * LANES
                    ]
                at = pl.multiple_of((m * count + s) * depth, TILE)
                for ref, d in blocks:
                    for t in range(tiles):
                        row = t * ny + d * block
                        if not whole:
                            row = pl.multiple_of(row, block)
                        ref[pl.ds(at + t * block, block), :] = field[
                            slab * mem_dev + m, pl.ds(row, block), :
                        ]
            return carry

        lax.fori_loop(0, count, one, 0)

    lane = lax.broadcasted_iota(jnp.int32, (1, LANES), 1)
    for k in range(total):
        cell = place(cells, k)
        row, col = cell // nx, cell % nx
        off = place(slabs, k) - lax.axis_index("lev") * slab_dev
        inside = (off >= 0) & (off < slab_dev)
        wanted = jnp.where(inside, col % LANES, LANES)
        off = jnp.clip(off, 0, slab_dev - 1)
        for m in range(mem_dev):
            line = field[off * mem_dev + m, pl.ds((col // LANES) * ny + row, 1), :]
            picks[m, pl.ds(k, 1), :] = jnp.where(lane == wanted, line, 0.0)
    diagonal = lax.broadcasted_iota(jnp.int32, (total, LANES), 0) == lax.broadcasted_iota(
        jnp.int32, (total, LANES), 1
    )
    line = lax.broadcasted_iota(jnp.int32, (TILE, LANES), 0)
    seen = jnp.zeros((TILE, LANES), jnp.float32)
    for m in range(mem_dev):
        value = jnp.sum(picks[m], axis=1, keepdims=True)
        value = jnp.sum(jnp.where(diagonal, value, 0.0), axis=0, keepdims=True)
        seen = jnp.where(line == (lax.axis_index("mem") * mem_dev + m) % TILE, value, seen)
    for ref, d in outs[0]:
        ref[pl.ds(mem_dev * parts[0][1] * depth, TILE), :] = seen


def forecast(parts, n, cells, slabs, spread, x, cv, ch):
    mem_dev, slab_dev, ny, nx = x.shape
    depth = ny // n * nx // LANES
    shapes = []
    for i, (_, count, whole) in enumerate(parts):
        shapes.append(block_shapes(n, whole, mem_dev * count * depth + (0 if i else TILE)))
    outs = pl.pallas_call(
        functools.partial(forecast_kernel, parts, n),
        in_specs=[pl.BlockSpec(memory_space=pltpu.HBM)] * 6,
        out_specs=[VMEM for group in shapes for _ in group],
        out_shape=[shape for group in shapes for shape in group],
        scratch_shapes=[
            pltpu.VMEM((slab_dev, mem_dev, ny, nx), jnp.float32),
            pltpu.VMEM(cv.shape, jnp.float32),
            pltpu.VMEM(ch.shape, jnp.float32),
            pltpu.SMEM(cells.shape, jnp.int32),
            pltpu.SMEM(slabs.shape, jnp.int32),
            pltpu.SMEM(spread.shape, jnp.float32),
            pltpu.VMEM((slab_dev * mem_dev, ny * nx // LANES, LANES), jnp.float32),
            pltpu.VMEM((mem_dev, cells.size, LANES), jnp.float32),
            pltpu.SemaphoreType.DMA((3, slab_dev)),
            pltpu.SemaphoreType.DMA((3,)),
        ],
        cost_estimate=cost(60 * x.size, 4 * (2 * x.size + 2 * cv.size)),
        compiler_params=params(),
        name="forecast",
    )(*[pltpu.with_memory_space_constraint(a, pltpu.HBM) for a in (cells, slabs, spread, x, cv, ch)])
    sends = []
    for group in shapes:
        sends.append(list(outs[: len(group)]))
        outs = outs[len(group) :]
    return sends


def taper_kernel(nx, block, cells_ref, out_ref):
    depth = out_ref.shape[1]
    at = lax.broadcasted_iota(jnp.int32, (depth, LANES), 0)
    row = (lax.axis_index("mem") * block + at % block).astype(jnp.float32)
    col = (at // block * LANES + lax.broadcasted_iota(jnp.int32, (depth, LANES), 1)).astype(
        jnp.float32
    )

    def one(k, carry):
        cell = place(cells_ref, k)
        out_ref[k] = taper(
            row - (cell // nx).astype(jnp.float32), col - (cell % nx).astype(jnp.float32)
        )
        return carry

    lax.fori_loop(0, out_ref.shape[0], one, 0)


def taper_table(nx, block, cells):
    depth = block * nx // LANES
    total = cells.size
    return pl.pallas_call(
        functools.partial(taper_kernel, nx, block),
        in_specs=[SMEM],
        out_specs=VMEM,
        out_shape=jax.ShapeDtypeStruct((total, depth, LANES), jnp.float32),
        cost_estimate=cost(60 * total * depth * LANES, 4 * total * depth * LANES),
        compiler_params=params(),
        name="taper_table",
    )(cells)


def plan_kernel(nx, cells_ref, values_ref, errors_ref, *refs):
    tiles, (anom_ref, incr_ref) = refs[:-2], refs[-2:]
    total = cells_ref.shape[0] * cells_ref.shape[1]
    rows = tiles[0][...]
    for other in tiles[1:]:
        rows = rows + other[...]
    members = rows.shape[0]
    lane = lax.broadcasted_iota(jnp.int32, (1, LANES), 1)
    row_of = jnp.zeros((1, LANES), jnp.float32)
    col_of = jnp.zeros((1, LANES), jnp.float32)
    where = []
    for k in range(total):
        cell = place(cells_ref, k)
        row, col = (cell // nx).astype(jnp.float32), (cell % nx).astype(jnp.float32)
        where.append((row, col))
        row_of = jnp.where(lane == k, row, row_of)
        col_of = jnp.where(lane == k, col, col_of)
    mean = jnp.sum(rows, axis=0, keepdims=True) * (1.0 / members)
    rows = rows - mean
    for k in range(total):
        loc = taper(row_of - where[k][0], col_of - where[k][1])
        anomaly = jnp.broadcast_to(rows[:, k : k + 1], rows.shape)
        ybar = jnp.broadcast_to(mean[:, k : k + 1], mean.shape)
        variance = jnp.sum(anomaly * anomaly, axis=0, keepdims=True) / (members - 1) + 1e-06
        shared = jnp.sum(rows * anomaly, axis=0, keepdims=True)
        error, value = place(errors_ref, k), place(values_ref, k)
        scale = 1.0 / ((members - 1) * variance)
        shift = (ybar * error + value * variance) / (variance + error) - ybar
        shrink = jnp.sqrt(error / (variance + error)) - 1.0
        anom_ref[k, 0:members, :] = anomaly * scale
        incr_ref[k, 0:members, :] = shift + shrink * anomaly
        weight = loc * shared * scale
        mean = mean + weight * shift
        rows = rows + (weight * shrink) * anomaly


def filter_plan(nx, cells, values, errors, tiles):
    members = tiles[0].shape[0]
    total = cells.size
    table = jax.ShapeDtypeStruct((total, members + TILE, LANES), jnp.float32)
    return pl.pallas_call(
        functools.partial(plan_kernel, nx),
        in_specs=[SMEM] * 3 + [VMEM] * len(tiles),
        out_specs=[VMEM, VMEM],
        out_shape=[table, table],
        cost_estimate=cost(20_000_000, 4 * 2 * total * members * LANES),
        compiler_params=params(),
        name="filter_plan",
    )(cells, values, errors, *tiles)


def settle_kernel(n, mem_dev, count, depth, whole, anom_ref, incr_ref, loc_ref, *refs):
    width = 1 if whole else n
    ins, outs = blocks_in(refs[:width], n, whole), blocks_in(refs[width:], n, whole)
    total = loc_ref.shape[0]
    members = n * mem_dev
    group = 2 if depth % (2 * TILE) == 0 and members <= 16 else 1
    span = group * TILE
    per_slab = depth // span

    def spread(ref, k, m):
        member = ins[m // mem_dev][1] * mem_dev + m % mem_dev
        return ref[k, pl.ds(member, TILE, stride=0), :]

    def part(i, carry):
        slab, at = i // per_slab, (i % per_slab) * span

        def spot(m, g):
            row = ((m % mem_dev) * count + slab) * depth + at + g * TILE
            return m // mem_dev, pl.ds(pl.multiple_of(row, TILE), TILE)

        xs = []
        for m in range(members):
            for g in range(group):
                src, row = spot(m, g)
                xs.append(ins[src][0][row, :])

        def step(k, xs):
            sums = [None] * group
            for m in range(members):
                a = spread(anom_ref, k, m)
                for g in range(group):
                    term = a * xs[m * group + g]
                    sums[g] = term if m == 0 else sums[g] + term
            sums = [
                s * loc_ref[k, pl.ds(pl.multiple_of(at + g * TILE, TILE), TILE), :]
                for g, s in enumerate(sums)
            ]
            new = []
            for m in range(members):
                b = spread(incr_ref, k, m)
                for g in range(group):
                    new.append(xs[m * group + g] + b * sums[g])
            return tuple(new)

        xs = lax.fori_loop(0, total, step, tuple(xs), unroll=2)
        for m in range(members):
            for g in range(group):
                src, row = spot(m, g)
                outs[src][0][row, :] = xs[m * group + g]
        return carry

    lax.fori_loop(0, count * per_slab, part, 0)


def settle(n, mem_dev, count, depth, whole, anom, incr, loc, xs):
    shapes = block_shapes(n, whole, mem_dev * count * depth)
    size = n * mem_dev * count * depth * LANES
    return pl.pallas_call(
        functools.partial(settle_kernel, n, mem_dev, count, depth, whole),
        in_specs=[VMEM] * (3 + len(xs)),
        out_specs=[VMEM] * len(shapes),
        out_shape=shapes,
        cost_estimate=cost(4 * loc.shape[0] * size, 8 * size),
        compiler_params=params(),
        name="settle",
    )(anom, incr, loc, *xs)


def assemble_kernel(n, count, whole, *refs):
    recv, out_ref, turn = refs[: 1 if whole else n], refs[-2], refs[-1]
    blocks = blocks_in(recv, n, whole)
    mem_dev, _, ny, nx = out_ref.shape
    block = ny // n
    tiles = nx // LANES
    depth = block * tiles
    slab = pl.program_id(0)
    for m in range(mem_dev):
        at = pl.multiple_of((m * count + slab) * depth, TILE)
        for t in range(tiles):
            lanes = slice(t * LANES, (t + 1) * LANES)
            lines = pl.ds(at + t * block, block)
            for j, (ref, d) in enumerate(blocks):
                if whole:
                    out_ref[m, 0, d * block : (d + 1) * block, lanes] = ref[lines, :]
                elif block % TILE == 0:
                    row = pl.multiple_of(d * block, block)
                    out_ref[m, 0, pl.ds(row, block), lanes] = ref[lines, :]
                else:
                    turn[pl.ds(j * block, block), :] = ref[lines, :]
            if block % TILE and not whole:
                for d, (_, j) in enumerate(blocks):
                    out_ref[m, 0, d * block : (d + 1) * block, lanes] = turn[
                        pl.ds(j * block, block), :
                    ]


def assemble(n, start, count, whole, recv, shape, before):
    mem_dev, _, ny, nx = shape
    extra = [] if before is None else [before]
    return pl.pallas_call(
        functools.partial(assemble_kernel, n, count, whole),
        grid=(count,),
        in_specs=[VMEM] * len(recv) + [pl.BlockSpec(memory_space=pl.ANY)] * len(extra),
        out_specs=pl.BlockSpec((mem_dev, 1, ny, nx), lambda s: (0, start + s, 0, 0)),
        out_shape=jax.ShapeDtypeStruct(shape, jnp.float32),
        scratch_shapes=[pltpu.VMEM((ny, LANES), jnp.float32)],
        input_output_aliases={} if before is None else {len(recv): 0},
        cost_estimate=cost(0, 8 * len(recv) * recv[0].size),
        compiler_params=params(),
        name="assemble",
    )(*recv, *extra)


def exchange(blocks, n, whole):
    if whole:
        return [lax.all_to_all(blocks[0], "mem", split_axis=0, concat_axis=0, tiled=True)]
    got = {}
    for j in range(n - 1, 0, -1):
        got[j] = lax.ppermute(blocks[j], "mem", [(i, i ^ j) for i in range(n)])
    return blocks[:1] + [got[j] for j in range(1, n)]


def body(x, cv, ch, spread, obs_cells, obs_slabs, obs_values, obs_error):
    mem_dev, slab_dev, ny, nx = x.shape
    n, lev = lax.axis_size("mem"), lax.axis_size("lev")
    block = ny // n
    depth = block * nx // LANES
    parts = chunks_of(slab_dev)
    sends = forecast(parts, n, obs_cells, obs_slabs, spread, x, cv, ch)
    states = []
    for c, blocks in enumerate(sends):
        states.append(exchange(blocks, n, parts[c][2]))
    loc = taper_table(nx, block, obs_cells)
    per = TILE // mem_dev
    seen = states[0][0][:, mem_dev * parts[0][1] * depth :, :]
    seen = seen.reshape(n // per, per, TILE, LANES).sum(axis=1).reshape(-1, LANES)
    tiles = [seen] + [
        lax.ppermute(seen, "lev", [(i, (i + d) % lev) for i in range(lev)])
        for d in range(1, lev)
    ]
    anom, incr = filter_plan(nx, obs_cells, obs_values, obs_error, tiles)
    result = None
    for (start, count, whole), state in zip(parts, states):
        new = settle(n, mem_dev, count, depth, whole, anom, incr, loc, state)
        back = exchange(list(new), n, whole)
        anom, _ = lax.optimization_barrier((anom, new[0]))
        result = assemble(n, start, count, whole, back, x.shape, result)
    return result


def solution(mesh):
    in_specs = (
        P("mem", "lev", None, None),
        P("lev", None, None),
        P("lev", None, None),
        P("lev"),
        P(),
        P(),
        P(),
        P(),
    )
    out_specs = P("mem", "lev", None, None)
    return jax.shard_map(body, mesh=mesh, in_specs=in_specs, out_specs=out_specs, check_vma=False)
```

time: 92.6 us -> 104 us (1.12); the launches traced: 92.3 us -> 102 us
  blocking collectives: 0 us -> 23.1 us
  starting transfers between devices: 53.1 us -> 34.6 us
  waiting for transfers between devices: 11.6 us -> 21.7 us
  local copies, waits for them, and re-layouts: 5.51 us -> 0.02 us
  Pallas kernels: 21.9 us -> 23 us
    all_to_all x0 -> x1, blocking collectives: none -> 23.1 us  [exchange(): lax.all_to_all(blocks[0], 'mem', split_axis=0, concat_axis=0, tiled=True)]
    ppermute x28 -> x14, starting transfers between devices: 49.9 us -> 29.4 us  [exchange(): got[j] = lax.ppermute(blocks[j], 'mem', [(i, i ^ j) for i in range(n)])]
    ppermute x28 -> x14, waiting for transfers between devices: 11.1 us -> 20.8 us  [exchange(): got[j] = lax.ppermute(blocks[j], 'mem', [(i, i ^ j) for i in range(n)])]
    unnamed x16 -> x6, local copies, waits for them, and re-layouts: 5.51 us -> 0.02 us
    all_to_all x0 -> x1, starting transfers between devices: none -> 3.49 us  [exchange(): lax.all_to_all(blocks[0], 'mem', split_axis=0, concat_axis=0, tiled=True)]
    ppermute x3, starting transfers between devices: 3.29 us -> 1.71 us  [body(): lax.ppermute(seen, 'lev', [(i, (i + d) % lev) for i in range(lev)])]
    pallas_call x5, Pallas kernels: 15.7 us -> 16.8 us  [the longest x2 10 us: settle(): pl.pallas_call(functools.partial(settle_kernel, n, mem_dev, count, depth,...]
  transfers between devices with their start and end apart: 31 -> 18, of which waited for: 7 -> 7; matrix products, arithmetic and copies ran while one was open for 0% -> 0% of each run, Pallas kernels for 18% -> 8%
where the time goes in v3:
time: 104 us; the launch traced here: 102 us
  starting transfers between devices  34.6 us (33%)
  blocking collectives  23.1 us (22%)
  Pallas kernels  23 us (22%)
  waiting for transfers between devices  21.7 us (21%)
    ppermute x14, starting transfers between devices, exchange(): got[j] = lax.ppermute(blocks[j], 'mem', [(i, i ^ j) for i in range(n)])  29.4 us
    all_to_all x1, blocking collectives, exchange(): lax.all_to_all(blocks[0], 'mem', split_axis=0, concat_axis=0, tiled=True)  23.1 us
    ppermute x14, waiting for transfers between devices, exchange(): got[j] = lax.ppermute(blocks[j], 'mem', [(i, i ^ j) for i in range(n)])  20.8 us
    pallas_call x2, Pallas kernels, settle(): pl.pallas_call(functools.partial(settle_kernel, n, mem_dev, count, depth,...  10 us
    pallas_call x1, Pallas kernels, forecast(): pl.pallas_call(functools.partial(forecast_kernel, parts, n), in_specs=[pl...  4.41 us
    pallas_call x1, Pallas kernels, filter_plan(): pl.pallas_call(functools.partial(plan_kernel, nx), in_specs=[SMEM] * 3 +...  4.2 us
    all_to_all x1, starting transfers between devices, exchange(): lax.all_to_all(blocks[0], 'mem', split_axis=0, concat_axis=0, tiled=True)  3.49 us
    pallas_call x2, Pallas kernels, assemble(): pl.pallas_call(functools.partial(assemble_kernel, n, count, whole), grid=...  2.34 us
  transfers between devices with their start and end apart: 18, of which 7 were waited for; matrix products, arithmetic and copies ran while one was open for 0% of the time, Pallas kernels for 8%

profile of v3, /device:TPU:0, one launch (start us, length us, event | category | flops | bytes accessed | tf_op | source)
XLA Modules:
  0.0 102.4 jit_solution(13839322503737040295)
XLA Ops:
  0.0 4.4 %forecast.1 = (f32[8,136,128]{2,1,0:T(8,128)S(1)}, f32[192,128]{1,0:T(8,128)S(1)}, f32[192,128]{1,0:T(8,128)S(1)}, f32[192,128]{1,0:T(8,128)S(1)}, f32[192,128]{...) custom-call(s32[2,16]{1,0:T(2,128)} %cells_ref.3, ...), custom_call_target="tpu_custom_call" | custom-call | flops 19660800 | bytes 3932160 | tf_op jit(solution)/shard_map/forecast/pallas_call | solution.py:174
  4.4 23.1 %all_to_all.10.refs_0_ = f32[8,136,128]{2,1,0:T(8,128)S(1)} all-to-all(f32[8,136,128]{2,1,0:T(8,128)S(1)} %get-tuple-element.25), channel_id=1, replica_groups=mesh['mem'=8,'lev'=4] {'mem'}, dimensions={0} | all-to-all | bytes 1114112 | tf_op jit(solution)/shard_map/all_to_all | solution.py:400
  27.5 1.6 %collective-permute-start.1 = (f32[16,128]{1,0:T(8,128)S(1)}, f32[16,128]{1,0:T(8,128)S(1)}, u32[]{:S(2)}, u32[]{:S(2)}) collective-permute-start(f32[16,128]{1,0:T(8,128)S(1)} %bitcast.4), channel_id=1, source_target_pairs={{0,2},{1,3},{2,0},{3,1},{4,6},{5,7},{6,4},{7,5},{8,10},{9,11},{10,... | collective-permute-start | bytes 24584 | tf_op jit(solution)/shard_map/ppermute | solution.py:422
  29.2 2.1 %taper_table.1.loc_ref = f32[32,32,128]{2,1,0:T(8,128)S(1)} custom-call(s32[2,16]{1,0:T(2,128)S(1)} %copy-done), custom_call_target="tpu_custom_call" | custom-call | flops 7864320 | bytes 524288 | tf_op jit(solution)/shard_map/taper_table/pallas_call | solution.py:223
  32.2 4.2 %filter_plan.1 = (f32[32,24,128]{2,1,0:T(8,128)S(1)}, f32[32,24,128]{2,1,0:T(8,128)S(1)}) custom-call(s32[2,16]{1,0:T(2,128)S(1)} %copy-done, f32[2,16]{1,0:T(2,128)S(1)} %copy-done.1, f32[2,16]{1,0:T(2,128)S(1)} %copy-done.2, f32[16,128]{1,0:T(8,128)S(1)} %bitcast.6, f32[16,128]{1,0:T(8,128)S(1)} %collective-permute-done.refs_1_, ...), custom_call_target="tpu_custom_call" | custom-call | flops 20000000 | bytes 524288 | tf_op jit(solution)/shard_map/filter_plan/pallas_call | solution.py:274
  36.4 4.4 %settle.2 = f32[8,128,128]{2,1,0:T(8,128)} custom-call(f32[32,24,128]{2,1,0:T(8,128)S(1)} %get-tuple-element.28.anom_ref, f32[32,24,128]{2,1,0:T(8,128)S(1)} %get-tuple-element.27.incr_ref, f32[32,32,128]{2,1,0:T(8,128)S(1)} %taper_table.1.loc_ref, f32[8,136,128]{2,1,0:T(8,128)S(1)} %all_to_all.10.refs_0_), custom_call_target="tpu_custom_call" | custom-call | flops 16777216 | bytes 1048576 | tf_op jit(solution)/shard_map/settle/pallas_call | solution.py:342
  40.8 3.5 %all-to-all-start.1 = ((f32[8,128,128]{2,1,0:T(8,128)}), f32[8,128,128]{2,1,0:T(8,128)S(1)}, u32[]{:S(2)}, u32[]{:S(2)}) async-start(f32[8,128,128]{2,1,0:T(8,128)} %settle.2), calls=%async_computation.1 | async-start | bytes 1048576 | tf_op jit(solution)/shard_map/all_to_all | solution.py:400
  44.3 1.9 %collective-permute-start.3 = (f32[192,128]{1,0:T(8,128)S(1)}, f32[192,128]{1,0:T(8,128)S(1)}, u32[]{:S(2)}, u32[]{:S(2)}) collective-permute-start(f32[192,128]{1,0:T(8,128)S(1)} %get-tuple-element.30), channel_id=1, source_target_pairs={{0,4},{4,0},{8,12},{12,8},{16,20},{20,16},{24,28},{28,24},{1,5},{5... | collective-permute-start | bytes 294920 | tf_op jit(solution)/shard_map/ppermute | solution.py:403
  46.2 1.5 %collective-permute-start.4 = (f32[192,128]{1,0:T(8,128)S(1)}, f32[192,128]{1,0:T(8,128)S(1)}, u32[]{:S(2)}, u32[]{:S(2)}) collective-permute-start(f32[192,128]{1,0:T(8,128)S(1)} %get-tuple-element.31), channel_id=1, source_target_pairs={{0,8},{4,12},{8,0},{12,4},{16,24},{20,28},{24,16},{28,20},{1,9},{5... | collective-permute-start | bytes 294920 | tf_op jit(solution)/shard_map/ppermute | solution.py:403
  47.9 2.8 %collective-permute-start.6 = (f32[192,128]{1,0:T(8,128)S(1)}, f32[192,128]{1,0:T(8,128)S(1)}, u32[]{:S(2)}, u32[]{:S(2)}) collective-permute-start(f32[192,128]{1,0:T(8,128)S(1)} %get-tuple-element.33), channel_id=1, source_target_pairs={{0,16},{4,20},{8,24},{12,28},{16,0},{20,4},{24,8},{28,12},{1,17},{... | collective-permute-start | bytes 294920 | tf_op jit(solution)/shard_map/ppermute | solution.py:403
  50.6 1.4 %collective-permute-start.7 = (f32[192,128]{1,0:T(8,128)S(1)}, f32[192,128]{1,0:T(8,128)S(1)}, u32[]{:S(2)}, u32[]{:S(2)}) collective-permute-start(f32[192,128]{1,0:T(8,128)S(1)} %get-tuple-element.34), channel_id=1, source_target_pairs={{0,20},{4,16},{8,28},{12,24},{16,4},{20,0},{24,12},{28,8},{1,21},{... | collective-permute-start | bytes 294920 | tf_op jit(solution)/shard_map/ppermute | solution.py:403
  52.2 5.4 %collective-permute-start.8 = (f32[192,128]{1,0:T(8,128)S(1)}, f32[192,128]{1,0:T(8,128)S(1)}, u32[]{:S(2)}, u32[]{:S(2)}) collective-permute-start(f32[192,128]{1,0:T(8,128)S(1)} %get-tuple-element.35), channel_id=1, source_target_pairs={{0,24},{4,28},{8,16},{12,20},{16,8},{20,12},{24,0},{28,4},{1,25},{... | collective-permute-start | bytes 294920 | tf_op jit(solution)/shard_map/ppermute | solution.py:403
  57.7 3.2 %collective-permute-start.9 = (f32[192,128]{1,0:T(8,128)S(1)}, f32[192,128]{1,0:T(8,128)S(1)}, u32[]{:S(2)}, u32[]{:S(2)}) collective-permute-start(f32[192,128]{1,0:T(8,128)S(1)} %get-tuple-element.36), channel_id=1, source_target_pairs={{0,28},{4,24},{8,20},{12,16},{16,12},{20,8},{24,4},{28,0},{1,29},{... | collective-permute-start | bytes 294920 | tf_op jit(solution)/shard_map/ppermute | solution.py:403
  60.9 1.1 %collective-permute-done.5.refs_3_ = f32[192,128]{1,0:T(8,128)S(1)} collective-permute-done((f32[192,128]{1,0:T(8,128)S(1)}, f32[192,128]{1,0:T(8,128)S(1)}, u32[]{:S(2)}, u32[]{:S(2)}) %collective-permute-start.5) | collective-permute-done | bytes 98336 | tf_op jit(solution)/shard_map/ppermute | solution.py:403
  61.9 8.7 %collective-permute-done.6.refs_4_ = f32[192,128]{1,0:T(8,128)S(1)} collective-permute-done((f32[192,128]{1,0:T(8,128)S(1)}, f32[192,128]{1,0:T(8,128)S(1)}, u32[]{:S(2)}, u32[]{:S(2)}) %collective-permute-start.6) | collective-permute-done | bytes 98336 | tf_op jit(solution)/shard_map/ppermute | solution.py:403
  70.7 2.7 %collective-permute-done.7.refs_5_ = f32[192,128]{1,0:T(8,128)S(1)} collective-permute-done((f32[192,128]{1,0:T(8,128)S(1)}, f32[192,128]{1,0:T(8,128)S(1)}, u32[]{:S(2)}, u32[]{:S(2)}) %collective-permute-start.7) | collective-permute-done | bytes 98336 | tf_op jit(solution)/shard_map/ppermute | solution.py:403
  73.4 5.6 %settle.3 = (f32[192,128]{1,0:T(8,128)S(1)}, f32[192,128]{1,0:T(8,128)S(1)}, f32[192,128]{1,0:T(8,128)S(1)}, f32[192,128]{1,0:T(8,128)S(1)}, f32[192,128]{1,0:T(...) custom-call(f32[32,24,128]{2,1,0:T(8,128)S(1)} %get-tuple-element.28.anom_ref, ...), custom_call_target="tpu_custom_call" | custom-call | flops 25165824 | bytes 1572864 | tf_op jit(solution)/shard_map/settle/pallas_call | solution.py:342
  79.9 3.5 %collective-permute-start.11 = (f32[192,128]{1,0:T(8,128)S(1)}, f32[192,128]{1,0:T(8,128)S(1)}, u32[]{:S(2)}, u32[]{:S(2)}) collective-permute-start(f32[192,128]{1,0:T(8,128)S(1)} %get-tuple-element.39), channel_id=1, source_target_pairs={{0,8},{4,12},{8,0},{12,4},{16,24},{20,28},{24,16},{28,20},{1,9},{5... | collective-permute-start | bytes 294920 | tf_op jit(solution)/shard_map/ppermute | solution.py:403
  84.3 2.0 %collective-permute-start.13 = (f32[192,128]{1,0:T(8,128)S(1)}, f32[192,128]{1,0:T(8,128)S(1)}, u32[]{:S(2)}, u32[]{:S(2)}) collective-permute-start(f32[192,128]{1,0:T(8,128)S(1)} %get-tuple-element.41), channel_id=1, source_target_pairs={{0,16},{4,20},{8,24},{12,28},{16,0},{20,4},{24,8},{28,12},{1,17},{... | collective-permute-start | bytes 294920 | tf_op jit(solution)/shard_map/ppermute | solution.py:403
  87.2 1.5 %collective-permute-start.15 = (f32[192,128]{1,0:T(8,128)S(1)}, f32[192,128]{1,0:T(8,128)S(1)}, u32[]{:S(2)}, u32[]{:S(2)}) collective-permute-start(f32[192,128]{1,0:T(8,128)S(1)} %get-tuple-element.43), channel_id=1, source_target_pairs={{0,24},{4,28},{8,16},{12,20},{16,8},{20,12},{24,0},{28,4},{1,25},{... | collective-permute-start | bytes 294920 | tf_op jit(solution)/shard_map/ppermute | solution.py:403
  88.7 3.2 %collective-permute-start.16 = (f32[192,128]{1,0:T(8,128)S(1)}, f32[192,128]{1,0:T(8,128)S(1)}, u32[]{:S(2)}, u32[]{:S(2)}) collective-permute-start(f32[192,128]{1,0:T(8,128)S(1)} %get-tuple-element.44), channel_id=1, source_target_pairs={{0,28},{4,24},{8,20},{12,16},{16,12},{20,8},{24,4},{28,0},{1,29},{... | collective-permute-start | bytes 294920 | tf_op jit(solution)/shard_map/ppermute | solution.py:403
  92.8 6.2 %collective-permute-done.13.refs_4_ = f32[192,128]{1,0:T(8,128)S(1)} collective-permute-done((f32[192,128]{1,0:T(8,128)S(1)}, f32[192,128]{1,0:T(8,128)S(1)}, u32[]{:S(2)}, u32[]{:S(2)}) %collective-permute-start.13) | collective-permute-done | bytes 98336 | tf_op jit(solution)/shard_map/ppermute | solution.py:403
  98.9 2.0 %collective-permute-done.14.refs_5_ = f32[192,128]{1,0:T(8,128)S(1)} collective-permute-done((f32[192,128]{1,0:T(8,128)S(1)}, f32[192,128]{1,0:T(8,128)S(1)}, u32[]{:S(2)}, u32[]{:S(2)}) %collective-permute-start.14) | collective-permute-done | bytes 98336 | tf_op jit(solution)/shard_map/ppermute | solution.py:403
  100.9 1.5 %assemble.3 = f32[2,5,64,512]{3,2,1,0:T(8,128)} custom-call(f32[192,128]{1,0:T(8,128)S(1)} %get-tuple-element.37.refs_0_, f32[192,128]{1,0:T(8,128)S(1)} %collective-permute-done.10.refs_1_, f32[192,128]{1,0:T(8,128)S(1)} %collective-permute-done.11.refs_2_, f32[192,128]{1,0:T(8,128)S(1)} %collective-permute-done.12.refs_3_, ...), custom_call_target="tpu_custom_call", output_to_operand_aliasing={{}: (8, {})} | custom-call | bytes 1572864 | tf_op jit(solution)/shard_map/assemble/pallas_call | solution.py:384
  (27 shorter events, 4.8 us)
Async XLA Ops:
  0.0 29.2 %copy-start = (s32[2,16]{1,0:T(2,128)S(1)}, s32[2,16]{1,0:T(2,128)}, u32[]{:S(2)}) copy-start(s32[2,16]{1,0:T(2,128)} %cells_ref.3) | copy-start | bytes 388
  4.4 27.7 %copy-start.1 = (f32[2,16]{1,0:T(2,128)S(1)}, f32[2,16]{1,0:T(2,128)}, u32[]{:S(2)}) copy-start(f32[2,16]{1,0:T(2,128)} %values_ref.1) | copy-start | bytes 388
  4.4 27.7 %copy-start.2 = (f32[2,16]{1,0:T(2,128)S(1)}, f32[2,16]{1,0:T(2,128)}, u32[]{:S(2)}) copy-start(f32[2,16]{1,0:T(2,128)} %errors_ref.1) | copy-start | bytes 388
  27.5 3.8 %collective-permute-start.2 = (f32[16,128]{1,0:T(8,128)S(1)}, f32[16,128]{1,0:T(8,128)S(1)}, u32[]{:S(2)}, u32[]{:S(2)}) collective-permute-start(f32[16,128]{1,0:T(8,128)S(1)} %bitcast.3), channel_id=1, source_target_pairs={{0,3},{1,0},{2,1},{3,2},{4,7},{5,4},{6,5},{7,6},{8,11},{9,8},{10,9... | collective-permute-start | bytes 24584 | tf_op jit(solution)/shard_map/ppermute | solution.py:422
  27.5 3.8 %collective-permute-start.1 = (f32[16,128]{1,0:T(8,128)S(1)}, f32[16,128]{1,0:T(8,128)S(1)}, u32[]{:S(2)}, u32[]{:S(2)}) collective-permute-start(f32[16,128]{1,0:T(8,128)S(1)} %bitcast.4), channel_id=1, source_target_pairs={{0,2},{1,3},{2,0},{3,1},{4,6},{5,7},{6,4},{7,5},{8,10},{9,11},{10,... | collective-permute-start | bytes 24584 | tf_op jit(solution)/shard_map/ppermute | solution.py:422
  29.1 3.1 %collective-permute-start = (f32[16,128]{1,0:T(8,128)S(1)}, f32[16,128]{1,0:T(8,128)S(1)}, u32[]{:S(2)}, u32[]{:S(2)}) collective-permute-start(f32[16,128]{1,0:T(8,128)S(1)} %bitcast.5), channel_id=1, source_target_pairs={{0,1},{1,2},{2,3},{3,0},{4,5},{5,6},{6,7},{7,4},{8,9},{9,10},{10,1... | collective-permute-start | bytes 24584 | tf_op jit(solution)/shard_map/ppermute | solution.py:422
  40.8 51.1 %all-to-all-start.1 = ((f32[8,128,128]{2,1,0:T(8,128)}), f32[8,128,128]{2,1,0:T(8,128)S(1)}, u32[]{:S(2)}, u32[]{:S(2)}) async-start(f32[8,128,128]{2,1,0:T(8,128)} %settle.2), calls=%async_computation.1 | async-start | bytes 1048576 | tf_op jit(solution)/shard_map/all_to_all | solution.py:400
  44.3 7.9 %collective-permute-start.3 = (f32[192,128]{1,0:T(8,128)S(1)}, f32[192,128]{1,0:T(8,128)S(1)}, u32[]{:S(2)}, u32[]{:S(2)}) collective-permute-start(f32[192,128]{1,0:T(8,128)S(1)} %get-tuple-element.30), channel_id=1, source_target_pairs={{0,4},{4,0},{8,12},{12,8},{16,20},{20,16},{24,28},{28,24},{1,5},{5... | collective-permute-start | bytes 294920 | tf_op jit(solution)/shard_map/ppermute | solution.py:403
  46.2 11.4 %collective-permute-start.4 = (f32[192,128]{1,0:T(8,128)S(1)}, f32[192,128]{1,0:T(8,128)S(1)}, u32[]{:S(2)}, u32[]{:S(2)}) collective-permute-start(f32[192,128]{1,0:T(8,128)S(1)} %get-tuple-element.31), channel_id=1, source_target_pairs={{0,8},{4,12},{8,0},{12,4},{16,24},{20,28},{24,16},{28,20},{1,9},{5... | collective-permute-start | bytes 294920 | tf_op jit(solution)/shard_map/ppermute | solution.py:403
  47.7 14.2 %collective-permute-start.5 = (f32[192,128]{1,0:T(8,128)S(1)}, f32[192,128]{1,0:T(8,128)S(1)}, u32[]{:S(2)}, u32[]{:S(2)}) collective-permute-start(f32[192,128]{1,0:T(8,128)S(1)} %get-tuple-element.32), channel_id=1, source_target_pairs={{0,12},{4,8},{8,4},{12,0},{16,28},{20,24},{24,20},{28,16},{1,13},{... | collective-permute-start | bytes 294920 | tf_op jit(solution)/shard_map/ppermute | solution.py:403
  47.9 22.8 %collective-permute-start.6 = (f32[192,128]{1,0:T(8,128)S(1)}, f32[192,128]{1,0:T(8,128)S(1)}, u32[]{:S(2)}, u32[]{:S(2)}) collective-permute-start(f32[192,128]{1,0:T(8,128)S(1)} %get-tuple-element.33), channel_id=1, source_target_pairs={{0,16},{4,20},{8,24},{12,28},{16,0},{20,4},{24,8},{28,12},{1,17},{... | collective-permute-start | bytes 294920 | tf_op jit(solution)/shard_map/ppermute | solution.py:403
  50.6 22.8 %collective-permute-start.7 = (f32[192,128]{1,0:T(8,128)S(1)}, f32[192,128]{1,0:T(8,128)S(1)}, u32[]{:S(2)}, u32[]{:S(2)}) collective-permute-start(f32[192,128]{1,0:T(8,128)S(1)} %get-tuple-element.34), channel_id=1, source_target_pairs={{0,20},{4,16},{8,28},{12,24},{16,4},{20,0},{24,12},{28,8},{1,21},{... | collective-permute-start | bytes 294920 | tf_op jit(solution)/shard_map/ppermute | solution.py:403
  52.2 21.2 %collective-permute-start.8 = (f32[192,128]{1,0:T(8,128)S(1)}, f32[192,128]{1,0:T(8,128)S(1)}, u32[]{:S(2)}, u32[]{:S(2)}) collective-permute-start(f32[192,128]{1,0:T(8,128)S(1)} %get-tuple-element.35), channel_id=1, source_target_pairs={{0,24},{4,28},{8,16},{12,20},{16,8},{20,12},{24,0},{28,4},{1,25},{... | collective-permute-start | bytes 294920 | tf_op jit(solution)/shard_map/ppermute | solution.py:403
  57.7 15.7 %collective-permute-start.9 = (f32[192,128]{1,0:T(8,128)S(1)}, f32[192,128]{1,0:T(8,128)S(1)}, u32[]{:S(2)}, u32[]{:S(2)}) collective-permute-start(f32[192,128]{1,0:T(8,128)S(1)} %get-tuple-element.36), channel_id=1, source_target_pairs={{0,28},{4,24},{8,20},{12,16},{16,12},{20,8},{24,4},{28,0},{1,29},{... | collective-permute-start | bytes 294920 | tf_op jit(solution)/shard_map/ppermute | solution.py:403
  79.0 8.2 %collective-permute-start.10 = (f32[192,128]{1,0:T(8,128)S(1)}, f32[192,128]{1,0:T(8,128)S(1)}, u32[]{:S(2)}, u32[]{:S(2)}) collective-permute-start(f32[192,128]{1,0:T(8,128)S(1)} %get-tuple-element.38), channel_id=1, source_target_pairs={{0,4},{4,0},{8,12},{12,8},{16,20},{20,16},{24,28},{28,24},{1,5},{5... | collective-permute-start | bytes 294920 | tf_op jit(solution)/shard_map/ppermute | solution.py:403
  79.9 8.8 %collective-permute-start.11 = (f32[192,128]{1,0:T(8,128)S(1)}, f32[192,128]{1,0:T(8,128)S(1)}, u32[]{:S(2)}, u32[]{:S(2)}) collective-permute-start(f32[192,128]{1,0:T(8,128)S(1)} %get-tuple-element.39), channel_id=1, source_target_pairs={{0,8},{4,12},{8,0},{12,4},{16,24},{20,28},{24,16},{28,20},{1,9},{5... | collective-permute-start | bytes 294920 | tf_op jit(solution)/shard_map/ppermute | solution.py:403
  83.4 9.4 %collective-permute-start.12 = (f32[192,128]{1,0:T(8,128)S(1)}, f32[192,128]{1,0:T(8,128)S(1)}, u32[]{:S(2)}, u32[]{:S(2)}) collective-permute-start(f32[192,128]{1,0:T(8,128)S(1)} %get-tuple-element.40), channel_id=1, source_target_pairs={{0,12},{4,8},{8,4},{12,0},{16,28},{20,24},{24,20},{28,16},{1,13},{... | collective-permute-start | bytes 294920 | tf_op jit(solution)/shard_map/ppermute | solution.py:403
  84.3 14.7 %collective-permute-start.13 = (f32[192,128]{1,0:T(8,128)S(1)}, f32[192,128]{1,0:T(8,128)S(1)}, u32[]{:S(2)}, u32[]{:S(2)}) collective-permute-start(f32[192,128]{1,0:T(8,128)S(1)} %get-tuple-element.41), channel_id=1, source_target_pairs={{0,16},{4,20},{8,24},{12,28},{16,0},{20,4},{24,8},{28,12},{1,17},{... | collective-permute-start | bytes 294920 | tf_op jit(solution)/shard_map/ppermute | solution.py:403
  86.3 14.6 %collective-permute-start.14 = (f32[192,128]{1,0:T(8,128)S(1)}, f32[192,128]{1,0:T(8,128)S(1)}, u32[]{:S(2)}, u32[]{:S(2)}) collective-permute-start(f32[192,128]{1,0:T(8,128)S(1)} %get-tuple-element.42), channel_id=1, source_target_pairs={{0,20},{4,16},{8,28},{12,24},{16,4},{20,0},{24,12},{28,8},{1,21},{... | collective-permute-start | bytes 294920 | tf_op jit(solution)/shard_map/ppermute | solution.py:403
  87.2 13.7 %collective-permute-start.15 = (f32[192,128]{1,0:T(8,128)S(1)}, f32[192,128]{1,0:T(8,128)S(1)}, u32[]{:S(2)}, u32[]{:S(2)}) collective-permute-start(f32[192,128]{1,0:T(8,128)S(1)} %get-tuple-element.43), channel_id=1, source_target_pairs={{0,24},{4,28},{8,16},{12,20},{16,8},{20,12},{24,0},{28,4},{1,25},{... | collective-permute-start | bytes 294920 | tf_op jit(solution)/shard_map/ppermute | solution.py:403
  88.7 12.2 %collective-permute-start.16 = (f32[192,128]{1,0:T(8,128)S(1)}, f32[192,128]{1,0:T(8,128)S(1)}, u32[]{:S(2)}, u32[]{:S(2)}) collective-permute-start(f32[192,128]{1,0:T(8,128)S(1)} %get-tuple-element.44), channel_id=1, source_target_pairs={{0,28},{4,24},{8,20},{12,16},{16,12},{20,8},{24,4},{28,0},{1,29},{... | collective-permute-start | bytes 294920 | tf_op jit(solution)/shard_map/ppermute | solution.py:403

commit v4 on v3

--- a/solution.py
+++ b/solution.py
@@ -37,10 +37,10 @@
 
 
 def chunks_of(slab_dev):
-    first = max(1, (2 * slab_dev) // 5)
+    first = max(1, (3 * slab_dev) // 5)
     if slab_dev == 1:
-        return ((0, 1, True),)
-    return ((0, first, True), (first, slab_dev - first, False))
+        return ((0, 1, False),)
+    return ((0, first, False), (first, slab_dev - first, True))
 
 
 def place(ref, k):
@@ -70,6 +70,7 @@
         width = 1 if whole else n
         outs.append(blocks_in(rest[:width], n, whole))
         rest = rest[width:]
+    seen_ref, rest = rest[0], rest[1:]
     x_buf, cv_buf, ch_buf, cells, slabs, spread, field, picks, sem, small = rest
     slab_dev, mem_dev, ny, nx = x_buf.shape
     block = ny // n
@@ -161,16 +162,17 @@
         value = jnp.sum(picks[m], axis=1, keepdims=True)
         value = jnp.sum(jnp.where(diagonal, value, 0.0), axis=0, keepdims=True)
         seen = jnp.where(line == (lax.axis_index("mem") * mem_dev + m) % TILE, value, seen)
-    for ref, d in outs[0]:
-        ref[pl.ds(mem_dev * parts[0][1] * depth, TILE), :] = seen
-
-
-def forecast(parts, n, cells, slabs, spread, x, cv, ch):
+    for d in range(seen_ref.shape[0]):
+        seen_ref[d] = seen
+
+
+def forecast(parts, n, lev, cells, slabs, spread, x, cv, ch):
     mem_dev, slab_dev, ny, nx = x.shape
     depth = ny // n * nx // LANES
     shapes = []
-    for i, (_, count, whole) in enumerate(parts):
-        shapes.append(block_shapes(n, whole, mem_dev * count * depth + (0 if i else TILE)))
+    for _, count, whole in parts:
+        shapes.append(block_shapes(n, whole, mem_dev * count * depth))
+    shapes.append([jax.ShapeDtypeStruct((n * lev, TILE, LANES), jnp.float32)])
     outs = pl.pallas_call(
         functools.partial(forecast_kernel, parts, n),
         in_specs=[pl.BlockSpec(memory_space=pltpu.HBM)] * 6,
@@ -231,13 +233,16 @@
     )(cells)
 
 
-def plan_kernel(nx, cells_ref, values_ref, errors_ref, *refs):
-    tiles, (anom_ref, incr_ref) = refs[:-2], refs[-2:]
+def plan_kernel(nx, members, cells_ref, values_ref, errors_ref, seen_ref, anom_ref, incr_ref):
     total = cells_ref.shape[0] * cells_ref.shape[1]
-    rows = tiles[0][...]
-    for other in tiles[1:]:
-        rows = rows + other[...]
-    members = rows.shape[0]
+    per = seen_ref.shape[0] * TILE // members
+    rows = []
+    for g in range(members // TILE):
+        tile = seen_ref[g * per]
+        for i in range(1, per):
+            tile = tile + seen_ref[g * per + i]
+        rows.append(tile)
+    rows = jnp.concatenate(rows)
     lane = lax.broadcasted_iota(jnp.int32, (1, LANES), 1)
     row_of = jnp.zeros((1, LANES), jnp.float32)
     col_of = jnp.zeros((1, LANES), jnp.float32)
@@ -267,19 +272,18 @@
         rows = rows + (weight * shrink) * anomaly
 
 
-def filter_plan(nx, cells, values, errors, tiles):
-    members = tiles[0].shape[0]
+def filter_plan(nx, members, cells, values, errors, seen):
     total = cells.size
     table = jax.ShapeDtypeStruct((total, members + TILE, LANES), jnp.float32)
     return pl.pallas_call(
-        functools.partial(plan_kernel, nx),
-        in_specs=[SMEM] * 3 + [VMEM] * len(tiles),
+        functools.partial(plan_kernel, nx, members),
+        in_specs=[SMEM] * 3 + [VMEM],
         out_specs=[VMEM, VMEM],
         out_shape=[table, table],
         cost_estimate=cost(20_000_000, 4 * 2 * total * members * LANES),
         compiler_params=params(),
         name="filter_plan",
-    )(cells, values, errors, *tiles)
+    )(cells, values, errors, seen)
 
 
 def settle_kernel(n, mem_dev, count, depth, whole, anom_ref, incr_ref, loc_ref, *refs):
@@ -410,19 +414,15 @@
     block = ny // n
     depth = block * nx // LANES
     parts = chunks_of(slab_dev)
-    sends = forecast(parts, n, obs_cells, obs_slabs, spread, x, cv, ch)
+    sends = forecast(parts, n, lev, obs_cells, obs_slabs, spread, x, cv, ch)
+    seen = lax.all_to_all(sends[-1][0], ("mem", "lev"), 0, 0, tiled=True)
     states = []
-    for c, blocks in enumerate(sends):
+    for c, blocks in enumerate(sends[:-1]):
         states.append(exchange(blocks, n, parts[c][2]))
     loc = taper_table(nx, block, obs_cells)
-    per = TILE // mem_dev
-    seen = states[0][0][:, mem_dev * parts[0][1] * depth :, :]
-    seen = seen.reshape(n // per, per, TILE, LANES).sum(axis=1).reshape(-1, LANES)
-    tiles = [seen] + [
-        lax.ppermute(seen, "lev", [(i, (i + d) % lev) for i in range(lev)])
-        for d in range(1, lev)
-    ]
-    anom, incr = filter_plan(nx, obs_cells, obs_values, obs_error, tiles)
+    anom, incr = filter_plan(
+        nx, n * mem_dev, obs_cells, obs_values, obs_error, seen
+    )
     result = None
     for (start, count, whole), state in zip(parts, states):
         new = settle(n, mem_dev, count, depth, whole, anom, incr, loc, state)

time: 104 us -> 101 us (0.971)
  blocking collectives: 23.1 us -> 15.3 us
  starting transfers between devices: 34.6 us -> 40.4 us
    all_to_all x1, blocking collectives: 23.1 us -> 15.3 us  [body(): seen = lax.all_to_all(sends[-1][0], ('mem', 'lev'), 0, 0, tiled=True)]
    all_to_all x1 -> x2, starting transfers between devices: 3.49 us -> 8.83 us  [exchange(): lax.all_to_all(blocks[0], 'mem', split_axis=0, concat_axis=0, tiled=True)]
    ppermute x14, starting transfers between devices: 29.4 us -> 31.6 us  [exchange(): got[j] = lax.ppermute(blocks[j], 'mem', [(i, i ^ j) for i in range(n)])]
    ppermute x3 -> x0, starting transfers between devices: 1.71 us -> none  [body(): lax.ppermute(seen, 'lev', [(i, (i + d) % lev) for i in range(lev)])]
  transfers between devices with their start and end apart: 18 -> 16, of which waited for: 7 -> 7; matrix products, arithmetic and copies ran while one was open for 0% -> 0% of each run, Pallas kernels for 8% -> 13%
where the time goes in v4:
time: 101 us; the launch traced here: 100 us
  starting transfers between devices  40.4 us (40%)
  Pallas kernels  23.7 us (23%)
  waiting for transfers between devices  20.7 us (20%)
  blocking collectives  15.3 us (15%)
    ppermute x14, starting transfers between devices, exchange(): got[j] = lax.ppermute(blocks[j], 'mem', [(i, i ^ j) for i in range(n)])  31.6 us
    ppermute x14, waiting for transfers between devices, exchange(): got[j] = lax.ppermute(blocks[j], 'mem', [(i, i ^ j) for i in range(n)])  20.7 us
    all_to_all x1, blocking collectives, body(): seen = lax.all_to_all(sends[-1][0], ('mem', 'lev'), 0, 0, tiled=True)  15.3 us
    pallas_call x2, Pallas kernels, settle(): pl.pallas_call(functools.partial(settle_kernel, n, mem_dev, count, depth,...  10 us
    all_to_all x2, starting transfers between devices, exchange(): lax.all_to_all(blocks[0], 'mem', split_axis=0, concat_axis=0, tiled=True)  8.83 us
    pallas_call x1, Pallas kernels, forecast(): pl.pallas_call(functools.partial(forecast_kernel, parts, n), in_specs=[pl...  5.09 us
    pallas_call x1, Pallas kernels, filter_plan(): pl.pallas_call(functools.partial(plan_kernel, nx, members), in_specs=[SME...  4.2 us
    pallas_call x2, Pallas kernels, assemble(): pl.pallas_call(functools.partial(assemble_kernel, n, count, whole), grid=...  2.34 us
  transfers between devices with their start and end apart: 16, of which 7 were waited for; matrix products, arithmetic and copies ran while one was open for 0% of the time, Pallas kernels for 13%

profile of v4, /device:TPU:0, one launch (start us, length us, event | category | flops | bytes accessed | tf_op | source)
XLA Modules:
  0.0 100.3 jit_solution(16496784858904467726)
XLA Ops:
  0.0 5.1 %forecast.1 = (f32[192,128]{1,0:T(8,128)S(1)}, f32[192,128]{1,0:T(8,128)S(1)}, f32[192,128]{1,0:T(8,128)S(1)}, f32[192,128]{1,0:T(8,128)S(1)}, f32[192,128]{1,0:...) custom-call(s32[2,16]{1,0:T(2,128)} %cells_ref.3, ...), custom_call_target="tpu_custom_call" | custom-call | flops 19660800 | bytes 3932160 | tf_op jit(solution)/shard_map/forecast/pallas_call | solution.py:176
  5.1 15.3 %all_to_all.15.seen_ref = f32[32,8,128]{2,1,0:T(8,128)S(1)} all-to-all(f32[32,8,128]{2,1,0:T(8,128)S(1)} %get-tuple-element.26), channel_id=1, replica_groups=mesh['mem'=8,'lev'=4] {'mem','lev'}, dimensions={0} | all-to-all | bytes 262144 | tf_op jit(solution)/shard_map/all_to_all | solution.py:418
  20.5 3.5 %all-to-all-start.1 = ((f32[8,128,128]{2,1,0:T(8,128)}), f32[8,128,128]{2,1,0:T(8,128)S(1)}, u32[]{:S(2)}, u32[]{:S(2)}) async-start(f32[8,128,128]{2,1,0:T(8,128)} %get-tuple-element.39), calls=%async_computation.1 | async-start | bytes 1048576 | tf_op jit(solution)/shard_map/all_to_all | solution.py:404
  24.0 1.9 %collective-permute-start = (f32[192,128]{1,0:T(8,128)S(1)}, f32[192,128]{1,0:T(8,128)S(1)}, u32[]{:S(2)}, u32[]{:S(2)}) collective-permute-start(f32[192,128]{1,0:T(8,128)S(1)} %get-tuple-element.30), channel_id=1, source_target_pairs={{0,4},{4,0},{8,12},{12,8},{16,20},{20,16},{24,28},{28,24},{1,5},{5... | collective-permute-start | bytes 294920 | tf_op jit(solution)/shard_map/ppermute | solution.py:407
  25.9 1.5 %collective-permute-start.1 = (f32[192,128]{1,0:T(8,128)S(1)}, f32[192,128]{1,0:T(8,128)S(1)}, u32[]{:S(2)}, u32[]{:S(2)}) collective-permute-start(f32[192,128]{1,0:T(8,128)S(1)} %get-tuple-element.31), channel_id=1, source_target_pairs={{0,8},{4,12},{8,0},{12,4},{16,24},{20,28},{24,16},{28,20},{1,9},{5... | collective-permute-start | bytes 294920 | tf_op jit(solution)/shard_map/ppermute | solution.py:407
  27.5 2.8 %collective-permute-start.3 = (f32[192,128]{1,0:T(8,128)S(1)}, f32[192,128]{1,0:T(8,128)S(1)}, u32[]{:S(2)}, u32[]{:S(2)}) collective-permute-start(f32[192,128]{1,0:T(8,128)S(1)} %get-tuple-element.33), channel_id=1, source_target_pairs={{0,16},{4,20},{8,24},{12,28},{16,0},{20,4},{24,8},{28,12},{1,17},{... | collective-permute-start | bytes 294920 | tf_op jit(solution)/shard_map/ppermute | solution.py:407
  33.0 4.9 %collective-permute-start.5 = (f32[192,128]{1,0:T(8,128)S(1)}, f32[192,128]{1,0:T(8,128)S(1)}, u32[]{:S(2)}, u32[]{:S(2)}) collective-permute-start(f32[192,128]{1,0:T(8,128)S(1)} %get-tuple-element.35), channel_id=1, source_target_pairs={{0,24},{4,28},{8,16},{12,20},{16,8},{20,12},{24,0},{28,4},{1,25},{... | collective-permute-start | bytes 294920 | tf_op jit(solution)/shard_map/ppermute | solution.py:407
  37.9 2.5 %collective-permute-start.6 = (f32[192,128]{1,0:T(8,128)S(1)}, f32[192,128]{1,0:T(8,128)S(1)}, u32[]{:S(2)}, u32[]{:S(2)}) collective-permute-start(f32[192,128]{1,0:T(8,128)S(1)} %get-tuple-element.36), channel_id=1, source_target_pairs={{0,28},{4,24},{8,20},{12,16},{16,12},{20,8},{24,4},{28,0},{1,29},{... | collective-permute-start | bytes 294920 | tf_op jit(solution)/shard_map/ppermute | solution.py:407
  40.5 2.1 %taper_table.1.loc_ref = f32[32,32,128]{2,1,0:T(8,128)S(1)} custom-call(s32[2,16]{1,0:T(2,128)S(1)} %copy-done), custom_call_target="tpu_custom_call" | custom-call | flops 7864320 | bytes 524288 | tf_op jit(solution)/shard_map/taper_table/pallas_call | solution.py:225
  42.5 4.2 %filter_plan.1 = (f32[32,24,128]{2,1,0:T(8,128)S(1)}, f32[32,24,128]{2,1,0:T(8,128)S(1)}) custom-call(s32[2,16]{1,0:T(2,128)S(1)} %copy-done, f32[2,16]{1,0:T(2,128)S(1)} %copy-done.1, f32[2,16]{1,0:T(2,128)S(1)} %copy-done.2, f32[32,8,128]{2,1,0:T(8,128)S(1)} %all_to_all.15.seen_ref), custom_call_target="tpu_custom_call" | custom-call | flops 20000000 | bytes 524288 | tf_op jit(solution)/shard_map/filter_plan/pallas_call | solution.py:278
  46.8 3.6 %collective-permute-done.3.refs_4_ = f32[192,128]{1,0:T(8,128)S(1)} collective-permute-done((f32[192,128]{1,0:T(8,128)S(1)}, f32[192,128]{1,0:T(8,128)S(1)}, u32[]{:S(2)}, u32[]{:S(2)}) %collective-permute-start.3) | collective-permute-done | bytes 98336 | tf_op jit(solution)/shard_map/ppermute | solution.py:407
  50.4 3.0 %collective-permute-done.4.refs_5_ = f32[192,128]{1,0:T(8,128)S(1)} collective-permute-done((f32[192,128]{1,0:T(8,128)S(1)}, f32[192,128]{1,0:T(8,128)S(1)}, u32[]{:S(2)}, u32[]{:S(2)}) %collective-permute-start.4) | collective-permute-done | bytes 98336 | tf_op jit(solution)/shard_map/ppermute | solution.py:407
  53.4 5.6 %settle.2 = (f32[192,128]{1,0:T(8,128)S(1)}, f32[192,128]{1,0:T(8,128)S(1)}, f32[192,128]{1,0:T(8,128)S(1)}, f32[192,128]{1,0:T(8,128)S(1)}, f32[192,128]{1,0:T(...) custom-call(f32[32,24,128]{2,1,0:T(8,128)S(1)} %get-tuple-element.38.anom_ref, ...), custom_call_target="tpu_custom_call" | custom-call | flops 25165824 | bytes 1572864 | tf_op jit(solution)/shard_map/settle/pallas_call | solution.py:346
  58.9 4.4 %settle.3 = f32[8,128,128]{2,1,0:T(8,128)} custom-call(f32[32,24,128]{2,1,0:T(8,128)S(1)} %get-tuple-element.38.anom_ref, f32[32,24,128]{2,1,0:T(8,128)S(1)} %get-tuple-element.28.incr_ref, f32[32,32,128]{2,1,0:T(8,128)S(1)} %taper_table.1.loc_ref, f32[8,128,128]{2,1,0:T(8,128)S(1)} %all-to-all-done.1.refs_0_), custom_call_target="tpu_custom_call" | custom-call | flops 16777216 | bytes 1048576 | tf_op jit(solution)/shard_map/settle/pallas_call | solution.py:346
  63.4 5.3 %all-to-all-start.2 = ((f32[8,128,128]{2,1,0:T(8,128)}), f32[8,128,128]{2,1,0:T(8,128)S(1)}, u32[]{:S(2)}, u32[]{:S(2)}) async-start(f32[8,128,128]{2,1,0:T(8,128)} %settle.3), calls=%async_computation.2 | async-start | bytes 1048576 | tf_op jit(solution)/shard_map/all_to_all | solution.py:404
  68.7 2.0 %collective-permute-start.7 = (f32[192,128]{1,0:T(8,128)S(1)}, f32[192,128]{1,0:T(8,128)S(1)}, u32[]{:S(2)}, u32[]{:S(2)}) collective-permute-start(f32[192,128]{1,0:T(8,128)S(1)} %get-tuple-element.40), channel_id=1, source_target_pairs={{0,4},{4,0},{8,12},{12,8},{16,20},{20,16},{24,28},{28,24},{1,5},{5... | collective-permute-start | bytes 294920 | tf_op jit(solution)/shard_map/ppermute | solution.py:407
  70.7 1.5 %collective-permute-start.8 = (f32[192,128]{1,0:T(8,128)S(1)}, f32[192,128]{1,0:T(8,128)S(1)}, u32[]{:S(2)}, u32[]{:S(2)}) collective-permute-start(f32[192,128]{1,0:T(8,128)S(1)} %get-tuple-element.41), channel_id=1, source_target_pairs={{0,8},{4,12},{8,0},{12,4},{16,24},{20,28},{24,16},{28,20},{1,9},{5... | collective-permute-start | bytes 294920 | tf_op jit(solution)/shard_map/ppermute | solution.py:407
  72.4 2.7 %collective-permute-start.10 = (f32[192,128]{1,0:T(8,128)S(1)}, f32[192,128]{1,0:T(8,128)S(1)}, u32[]{:S(2)}, u32[]{:S(2)}) collective-permute-start(f32[192,128]{1,0:T(8,128)S(1)} %get-tuple-element.43), channel_id=1, source_target_pairs={{0,16},{4,20},{8,24},{12,28},{16,0},{20,4},{24,8},{28,12},{1,17},{... | collective-permute-start | bytes 294920 | tf_op jit(solution)/shard_map/ppermute | solution.py:407
  75.1 1.5 %collective-permute-start.11 = (f32[192,128]{1,0:T(8,128)S(1)}, f32[192,128]{1,0:T(8,128)S(1)}, u32[]{:S(2)}, u32[]{:S(2)}) collective-permute-start(f32[192,128]{1,0:T(8,128)S(1)} %get-tuple-element.44), channel_id=1, source_target_pairs={{0,20},{4,16},{8,28},{12,24},{16,4},{20,0},{24,12},{28,8},{1,21},{... | collective-permute-start | bytes 294920 | tf_op jit(solution)/shard_map/ppermute | solution.py:407
  76.8 5.4 %collective-permute-start.12 = (f32[192,128]{1,0:T(8,128)S(1)}, f32[192,128]{1,0:T(8,128)S(1)}, u32[]{:S(2)}, u32[]{:S(2)}) collective-permute-start(f32[192,128]{1,0:T(8,128)S(1)} %get-tuple-element.45), channel_id=1, source_target_pairs={{0,24},{4,28},{8,16},{12,20},{16,8},{20,12},{24,0},{28,4},{1,25},{... | collective-permute-start | bytes 294920 | tf_op jit(solution)/shard_map/ppermute | solution.py:407
  82.1 3.2 %collective-permute-start.13 = (f32[192,128]{1,0:T(8,128)S(1)}, f32[192,128]{1,0:T(8,128)S(1)}, u32[]{:S(2)}, u32[]{:S(2)}) collective-permute-start(f32[192,128]{1,0:T(8,128)S(1)} %get-tuple-element.46), channel_id=1, source_target_pairs={{0,28},{4,24},{8,20},{12,16},{16,12},{20,8},{24,4},{28,0},{1,29},{... | collective-permute-start | bytes 294920 | tf_op jit(solution)/shard_map/ppermute | solution.py:407
  86.5 8.7 %collective-permute-done.10.refs_4_ = f32[192,128]{1,0:T(8,128)S(1)} collective-permute-done((f32[192,128]{1,0:T(8,128)S(1)}, f32[192,128]{1,0:T(8,128)S(1)}, u32[]{:S(2)}, u32[]{:S(2)}) %collective-permute-start.10) | collective-permute-done | bytes 98336 | tf_op jit(solution)/shard_map/ppermute | solution.py:407
  95.2 2.8 %collective-permute-done.11.refs_5_ = f32[192,128]{1,0:T(8,128)S(1)} collective-permute-done((f32[192,128]{1,0:T(8,128)S(1)}, f32[192,128]{1,0:T(8,128)S(1)}, u32[]{:S(2)}, u32[]{:S(2)}) %collective-permute-start.11) | collective-permute-done | bytes 98336 | tf_op jit(solution)/shard_map/ppermute | solution.py:407
  97.9 1.5 %assemble.2.refs_1_ = f32[2,5,64,512]{3,2,1,0:T(8,128)} custom-call(f32[192,128]{1,0:T(8,128)S(1)} %get-tuple-element.37.refs_0_, f32[192,128]{1,0:T(8,128)S(1)} %collective-permute-done.7.refs_1_, f32[192,128]{1,0:T(8,128)S(1)} %collective-permute-done.8.refs_2_, f32[192,128]{1,0:T(8,128)S(1)} %collective-permute-done.9.refs_3_, ...), custom_call_target="tpu_custom_call" | custom-call | bytes 1572864 | tf_op jit(solution)/shard_map/assemble/pallas_call | solution.py:388
  (22 shorter events, 5.3 us)
Async XLA Ops:
  5.1 35.4 %copy-start = (s32[2,16]{1,0:T(2,128)S(1)}, s32[2,16]{1,0:T(2,128)}, u32[]{:S(2)}) copy-start(s32[2,16]{1,0:T(2,128)} %cells_ref.3) | copy-start | bytes 388
  5.1 37.4 %copy-start.1 = (f32[2,16]{1,0:T(2,128)S(1)}, f32[2,16]{1,0:T(2,128)}, u32[]{:S(2)}) copy-start(f32[2,16]{1,0:T(2,128)} %values_ref.1) | copy-start | bytes 388
  5.1 37.4 %copy-start.2 = (f32[2,16]{1,0:T(2,128)S(1)}, f32[2,16]{1,0:T(2,128)}, u32[]{:S(2)}) copy-start(f32[2,16]{1,0:T(2,128)} %errors_ref.1) | copy-start | bytes 388
  20.5 38.5 %all-to-all-start.1 = ((f32[8,128,128]{2,1,0:T(8,128)}), f32[8,128,128]{2,1,0:T(8,128)S(1)}, u32[]{:S(2)}, u32[]{:S(2)}) async-start(f32[8,128,128]{2,1,0:T(8,128)} %get-tuple-element.39), calls=%async_computation.1 | async-start | bytes 1048576 | tf_op jit(solution)/shard_map/all_to_all | solution.py:404
  24.0 9.0 %collective-permute-start = (f32[192,128]{1,0:T(8,128)S(1)}, f32[192,128]{1,0:T(8,128)S(1)}, u32[]{:S(2)}, u32[]{:S(2)}) collective-permute-start(f32[192,128]{1,0:T(8,128)S(1)} %get-tuple-element.30), channel_id=1, source_target_pairs={{0,4},{4,0},{8,12},{12,8},{16,20},{20,16},{24,28},{28,24},{1,5},{5... | collective-permute-start | bytes 294920 | tf_op jit(solution)/shard_map/ppermute | solution.py:407
  25.9 12.0 %collective-permute-start.1 = (f32[192,128]{1,0:T(8,128)S(1)}, f32[192,128]{1,0:T(8,128)S(1)}, u32[]{:S(2)}, u32[]{:S(2)}) collective-permute-start(f32[192,128]{1,0:T(8,128)S(1)} %get-tuple-element.31), channel_id=1, source_target_pairs={{0,8},{4,12},{8,0},{12,4},{16,24},{20,28},{24,16},{28,20},{1,9},{5... | collective-permute-start | bytes 294920 | tf_op jit(solution)/shard_map/ppermute | solution.py:407
  27.4 19.4 %collective-permute-start.2 = (f32[192,128]{1,0:T(8,128)S(1)}, f32[192,128]{1,0:T(8,128)S(1)}, u32[]{:S(2)}, u32[]{:S(2)}) collective-permute-start(f32[192,128]{1,0:T(8,128)S(1)} %get-tuple-element.32), channel_id=1, source_target_pairs={{0,12},{4,8},{8,4},{12,0},{16,28},{20,24},{24,20},{28,16},{1,13},{... | collective-permute-start | bytes 294920 | tf_op jit(solution)/shard_map/ppermute | solution.py:407
  27.5 22.8 %collective-permute-start.3 = (f32[192,128]{1,0:T(8,128)S(1)}, f32[192,128]{1,0:T(8,128)S(1)}, u32[]{:S(2)}, u32[]{:S(2)}) collective-permute-start(f32[192,128]{1,0:T(8,128)S(1)} %get-tuple-element.33), channel_id=1, source_target_pairs={{0,16},{4,20},{8,24},{12,28},{16,0},{20,4},{24,8},{28,12},{1,17},{... | collective-permute-start | bytes 294920 | tf_op jit(solution)/shard_map/ppermute | solution.py:407
  30.3 23.0 %collective-permute-start.4 = (f32[192,128]{1,0:T(8,128)S(1)}, f32[192,128]{1,0:T(8,128)S(1)}, u32[]{:S(2)}, u32[]{:S(2)}) collective-permute-start(f32[192,128]{1,0:T(8,128)S(1)} %get-tuple-element.34), channel_id=1, source_target_pairs={{0,20},{4,16},{8,28},{12,24},{16,4},{20,0},{24,12},{28,8},{1,21},{... | collective-permute-start | bytes 294920 | tf_op jit(solution)/shard_map/ppermute | solution.py:407
  33.0 20.3 %collective-permute-start.5 = (f32[192,128]{1,0:T(8,128)S(1)}, f32[192,128]{1,0:T(8,128)S(1)}, u32[]{:S(2)}, u32[]{:S(2)}) collective-permute-start(f32[192,128]{1,0:T(8,128)S(1)} %get-tuple-element.35), channel_id=1, source_target_pairs={{0,24},{4,28},{8,16},{12,20},{16,8},{20,12},{24,0},{28,4},{1,25},{... | collective-permute-start | bytes 294920 | tf_op jit(solution)/shard_map/ppermute | solution.py:407
  37.9 15.4 %collective-permute-start.6 = (f32[192,128]{1,0:T(8,128)S(1)}, f32[192,128]{1,0:T(8,128)S(1)}, u32[]{:S(2)}, u32[]{:S(2)}) collective-permute-start(f32[192,128]{1,0:T(8,128)S(1)} %get-tuple-element.36), channel_id=1, source_target_pairs={{0,28},{4,24},{8,20},{12,16},{16,12},{20,8},{24,4},{28,0},{1,29},{... | collective-permute-start | bytes 294920 | tf_op jit(solution)/shard_map/ppermute | solution.py:407
  63.4 36.1 %all-to-all-start.2 = ((f32[8,128,128]{2,1,0:T(8,128)}), f32[8,128,128]{2,1,0:T(8,128)S(1)}, u32[]{:S(2)}, u32[]{:S(2)}) async-start(f32[8,128,128]{2,1,0:T(8,128)} %settle.3), calls=%async_computation.2 | async-start | bytes 1048576 | tf_op jit(solution)/shard_map/all_to_all | solution.py:404
  68.7 8.1 %collective-permute-start.7 = (f32[192,128]{1,0:T(8,128)S(1)}, f32[192,128]{1,0:T(8,128)S(1)}, u32[]{:S(2)}, u32[]{:S(2)}) collective-permute-start(f32[192,128]{1,0:T(8,128)S(1)} %get-tuple-element.40), channel_id=1, source_target_pairs={{0,4},{4,0},{8,12},{12,8},{16,20},{20,16},{24,28},{28,24},{1,5},{5... | collective-permute-start | bytes 294920 | tf_op jit(solution)/shard_map/ppermute | solution.py:407
  70.7 11.4 %collective-permute-start.8 = (f32[192,128]{1,0:T(8,128)S(1)}, f32[192,128]{1,0:T(8,128)S(1)}, u32[]{:S(2)}, u32[]{:S(2)}) collective-permute-start(f32[192,128]{1,0:T(8,128)S(1)} %get-tuple-element.41), channel_id=1, source_target_pairs={{0,8},{4,12},{8,0},{12,4},{16,24},{20,28},{24,16},{28,20},{1,9},{5... | collective-permute-start | bytes 294920 | tf_op jit(solution)/shard_map/ppermute | solution.py:407
  72.2 14.3 %collective-permute-start.9 = (f32[192,128]{1,0:T(8,128)S(1)}, f32[192,128]{1,0:T(8,128)S(1)}, u32[]{:S(2)}, u32[]{:S(2)}) collective-permute-start(f32[192,128]{1,0:T(8,128)S(1)} %get-tuple-element.42), channel_id=1, source_target_pairs={{0,12},{4,8},{8,4},{12,0},{16,28},{20,24},{24,20},{28,16},{1,13},{... | collective-permute-start | bytes 294920 | tf_op jit(solution)/shard_map/ppermute | solution.py:407
  72.4 22.8 %collective-permute-start.10 = (f32[192,128]{1,0:T(8,128)S(1)}, f32[192,128]{1,0:T(8,128)S(1)}, u32[]{:S(2)}, u32[]{:S(2)}) collective-permute-start(f32[192,128]{1,0:T(8,128)S(1)} %get-tuple-element.43), channel_id=1, source_target_pairs={{0,16},{4,20},{8,24},{12,28},{16,0},{20,4},{24,8},{28,12},{1,17},{... | collective-permute-start | bytes 294920 | tf_op jit(solution)/shard_map/ppermute | solution.py:407
  75.1 22.8 %collective-permute-start.11 = (f32[192,128]{1,0:T(8,128)S(1)}, f32[192,128]{1,0:T(8,128)S(1)}, u32[]{:S(2)}, u32[]{:S(2)}) collective-permute-start(f32[192,128]{1,0:T(8,128)S(1)} %get-tuple-element.44), channel_id=1, source_target_pairs={{0,20},{4,16},{8,28},{12,24},{16,4},{20,0},{24,12},{28,8},{1,21},{... | collective-permute-start | bytes 294920 | tf_op jit(solution)/shard_map/ppermute | solution.py:407
  76.8 21.1 %collective-permute-start.12 = (f32[192,128]{1,0:T(8,128)S(1)}, f32[192,128]{1,0:T(8,128)S(1)}, u32[]{:S(2)}, u32[]{:S(2)}) collective-permute-start(f32[192,128]{1,0:T(8,128)S(1)} %get-tuple-element.45), channel_id=1, source_target_pairs={{0,24},{4,28},{8,16},{12,20},{16,8},{20,12},{24,0},{28,4},{1,25},{... | collective-permute-start | bytes 294920 | tf_op jit(solution)/shard_map/ppermute | solution.py:407
  82.1 15.8 %collective-permute-start.13 = (f32[192,128]{1,0:T(8,128)S(1)}, f32[192,128]{1,0:T(8,128)S(1)}, u32[]{:S(2)}, u32[]{:S(2)}) collective-permute-start(f32[192,128]{1,0:T(8,128)S(1)} %get-tuple-element.46), channel_id=1, source_target_pairs={{0,28},{4,24},{8,20},{12,16},{16,12},{20,8},{24,4},{28,0},{1,29},{... | collective-permute-start | bytes 294920 | tf_op jit(solution)/shard_map/ppermute | solution.py:407

commit v5 on v3

--- a/solution.py
+++ b/solution.py
@@ -37,10 +37,10 @@
 
 
 def chunks_of(slab_dev):
-    first = max(1, (2 * slab_dev) // 5)
+    first = max(1, (3 * slab_dev) // 5)
     if slab_dev == 1:
-        return ((0, 1, True),)
-    return ((0, first, True), (first, slab_dev - first, False))
+        return ((0, 1, False),)
+    return ((0, first, False), (first, slab_dev - first, True))
 
 
 def place(ref, k):
@@ -70,6 +70,7 @@
         width = 1 if whole else n
         outs.append(blocks_in(rest[:width], n, whole))
         rest = rest[width:]
+    seen_ref, rest = rest[0], rest[1:]
     x_buf, cv_buf, ch_buf, cells, slabs, spread, field, picks, sem, small = rest
     slab_dev, mem_dev, ny, nx = x_buf.shape
     block = ny // n
@@ -161,16 +162,17 @@
         value = jnp.sum(picks[m], axis=1, keepdims=True)
         value = jnp.sum(jnp.where(diagonal, value, 0.0), axis=0, keepdims=True)
         seen = jnp.where(line == (lax.axis_index("mem") * mem_dev + m) % TILE, value, seen)
-    for ref, d in outs[0]:
-        ref[pl.ds(mem_dev * parts[0][1] * depth, TILE), :] = seen
+    for d in range(seen_ref.shape[0]):
+        seen_ref[d] = seen
 
 
 def forecast(parts, n, cells, slabs, spread, x, cv, ch):
     mem_dev, slab_dev, ny, nx = x.shape
     depth = ny // n * nx // LANES
     shapes = []
-    for i, (_, count, whole) in enumerate(parts):
-        shapes.append(block_shapes(n, whole, mem_dev * count * depth + (0 if i else TILE)))
+    for _, count, whole in parts:
+        shapes.append(block_shapes(n, whole, mem_dev * count * depth))
+    shapes.append([jax.ShapeDtypeStruct((n, TILE, LANES), jnp.float32)])
     outs = pl.pallas_call(
         functools.partial(forecast_kernel, parts, n),
         in_specs=[pl.BlockSpec(memory_space=pltpu.HBM)] * 6,
@@ -199,45 +201,19 @@
     return sends
 
 
-def taper_kernel(nx, block, cells_ref, out_ref):
-    depth = out_ref.shape[1]
-    at = lax.broadcasted_iota(jnp.int32, (depth, LANES), 0)
-    row = (lax.axis_index("mem") * block + at % block).astype(jnp.float32)
-    col = (at // block * LANES + lax.broadcasted_iota(jnp.int32, (depth, LANES), 1)).astype(
-        jnp.float32
-    )
-
-    def one(k, carry):
-        cell = place(cells_ref, k)
-        out_ref[k] = taper(
-            row - (cell // nx).astype(jnp.float32), col - (cell % nx).astype(jnp.float32)
-        )
-        return carry
-
-    lax.fori_loop(0, out_ref.shape[0], one, 0)
-
-
-def taper_table(nx, block, cells):
-    depth = block * nx // LANES
-    total = cells.size
-    return pl.pallas_call(
-        functools.partial(taper_kernel, nx, block),
-        in_specs=[SMEM],
-        out_specs=VMEM,
-        out_shape=jax.ShapeDtypeStruct((total, depth, LANES), jnp.float32),
-        cost_estimate=cost(60 * total * depth * LANES, 4 * total * depth * LANES),
-        compiler_params=params(),
-        name="taper_table",
-    )(cells)
-
-
-def plan_kernel(nx, cells_ref, values_ref, errors_ref, *refs):
-    tiles, (anom_ref, incr_ref) = refs[:-2], refs[-2:]
+def plan_kernel(nx, block, cells_ref, values_ref, errors_ref, *refs):
+    seen_refs, (anom_ref, incr_ref, loc_ref) = refs[:-3], refs[-3:]
     total = cells_ref.shape[0] * cells_ref.shape[1]
-    rows = tiles[0][...]
-    for other in tiles[1:]:
+    rows = seen_refs[0][...]
+    for other in seen_refs[1:]:
         rows = rows + other[...]
     members = rows.shape[0]
+    depth = loc_ref.shape[1]
+    at = lax.broadcasted_iota(jnp.int32, (depth, LANES), 0)
+    cell_row = (lax.axis_index("mem") * block + at % block).astype(jnp.float32)
+    cell_col = (
+        at // block * LANES + lax.broadcasted_iota(jnp.int32, (depth, LANES), 1)
+    ).astype(jnp.float32)
     lane = lax.broadcasted_iota(jnp.int32, (1, LANES), 1)
     row_of = jnp.zeros((1, LANES), jnp.float32)
     col_of = jnp.zeros((1, LANES), jnp.float32)
@@ -251,6 +227,7 @@
     mean = jnp.sum(rows, axis=0, keepdims=True) * (1.0 / members)
     rows = rows - mean
     for k in range(total):
+        loc_ref[k] = taper(cell_row - where[k][0], cell_col - where[k][1])
         loc = taper(row_of - where[k][0], col_of - where[k][1])
         anomaly = jnp.broadcast_to(rows[:, k : k + 1], rows.shape)
         ybar = jnp.broadcast_to(mean[:, k : k + 1], mean.shape)
@@ -267,19 +244,21 @@
         rows = rows + (weight * shrink) * anomaly
 
 
-def filter_plan(nx, cells, values, errors, tiles):
-    members = tiles[0].shape[0]
+def filter_plan(nx, block, cells, values, errors, seen):
+    members = seen[0].shape[0]
     total = cells.size
+    depth = block * nx // LANES
     table = jax.ShapeDtypeStruct((total, members + TILE, LANES), jnp.float32)
+    tapers = jax.ShapeDtypeStruct((total, depth, LANES), jnp.float32)
     return pl.pallas_call(
-        functools.partial(plan_kernel, nx),
-        in_specs=[SMEM] * 3 + [VMEM] * len(tiles),
-        out_specs=[VMEM, VMEM],
-        out_shape=[table, table],
-        cost_estimate=cost(20_000_000, 4 * 2 * total * members * LANES),
+        functools.partial(plan_kernel, nx, block),
+        in_specs=[SMEM] * 3 + [VMEM] * len(seen),
+        out_specs=[VMEM] * 3,
+        out_shape=[table, table, tapers],
+        cost_estimate=cost(20_000_000, 4 * total * (2 * members + depth) * LANES),
         compiler_params=params(),
         name="filter_plan",
-    )(cells, values, errors, *tiles)
+    )(cells, values, errors, *seen)
 
 
 def settle_kernel(n, mem_dev, count, depth, whole, anom_ref, incr_ref, loc_ref, *refs):
@@ -411,18 +390,17 @@
     depth = block * nx // LANES
     parts = chunks_of(slab_dev)
     sends = forecast(parts, n, obs_cells, obs_slabs, spread, x, cv, ch)
+    seen = lax.all_to_all(sends[-1][0], "mem", 0, 0, tiled=True)
     states = []
-    for c, blocks in enumerate(sends):
+    for c, blocks in enumerate(sends[:-1]):
         states.append(exchange(blocks, n, parts[c][2]))
-    loc = taper_table(nx, block, obs_cells)
     per = TILE // mem_dev
-    seen = states[0][0][:, mem_dev * parts[0][1] * depth :, :]
     seen = seen.reshape(n // per, per, TILE, LANES).sum(axis=1).reshape(-1, LANES)
     tiles = [seen] + [
         lax.ppermute(seen, "lev", [(i, (i + d) % lev) for i in range(lev)])
         for d in range(1, lev)
     ]
-    anom, incr = filter_plan(nx, obs_cells, obs_values, obs_error, tiles)
+    anom, incr, loc = filter_plan(nx, block, obs_cells, obs_values, obs_error, tiles)
     result = None
     for (start, count, whole), state in zip(parts, states):
         new = settle(n, mem_dev, count, depth, whole, anom, incr, loc, state)

time: 104 us -> 97.3 us (0.936)
  blocking collectives: 23.1 us -> 13.8 us
  starting transfers between devices: 34.6 us -> 39.1 us
    all_to_all x1, blocking collectives: 23.1 us -> 13.8 us  [body(): seen = lax.all_to_all(sends[-1][0], 'mem', 0, 0, tiled=True)]
    all_to_all x1 -> x2, starting transfers between devices: 3.49 us -> 8.14 us  [exchange(): lax.all_to_all(blocks[0], 'mem', split_axis=0, concat_axis=0, tiled=True)]
    ppermute x14, waiting for transfers between devices: 20.8 us -> 19.3 us  [exchange(): got[j] = lax.ppermute(blocks[j], 'mem', [(i, i ^ j) for i in range(n)])]
    pallas_call x2 -> x1, Pallas kernels: 6.26 us -> 4.81 us  [filter_plan(): pl.pallas_call(functools.partial(plan_kernel, nx, block), in_specs=[SMEM]...]
  transfers between devices with their start and end apart: 18 -> 19, of which waited for: 7 -> 6; matrix products, arithmetic and copies ran while one was open for 0% -> 0% of each run, Pallas kernels for 8% -> 12%
where the time goes in v5:
time: 97.3 us; the launch traced here: 96.5 us
  starting transfers between devices  39.1 us (40%)
  Pallas kernels  22.3 us (23%)
  waiting for transfers between devices  21.2 us (22%)
  blocking collectives  13.8 us (14%)
    ppermute x14, starting transfers between devices, exchange(): got[j] = lax.ppermute(blocks[j], 'mem', [(i, i ^ j) for i in range(n)])  29.3 us
    ppermute x14, waiting for transfers between devices, exchange(): got[j] = lax.ppermute(blocks[j], 'mem', [(i, i ^ j) for i in range(n)])  19.3 us
    all_to_all x1, blocking collectives, body(): seen = lax.all_to_all(sends[-1][0], 'mem', 0, 0, tiled=True)  13.8 us
    pallas_call x2, Pallas kernels, settle(): pl.pallas_call(functools.partial(settle_kernel, n, mem_dev, count, depth,...  10 us
    all_to_all x2, starting transfers between devices, exchange(): lax.all_to_all(blocks[0], 'mem', split_axis=0, concat_axis=0, tiled=True)  8.14 us
    pallas_call x1, Pallas kernels, forecast(): pl.pallas_call(functools.partial(forecast_kernel, parts, n), in_specs=[pl...  5.13 us
    pallas_call x1, Pallas kernels, filter_plan(): pl.pallas_call(functools.partial(plan_kernel, nx, block), in_specs=[SMEM]...  4.81 us
    pallas_call x2, Pallas kernels, assemble(): pl.pallas_call(functools.partial(assemble_kernel, n, count, whole), grid=...  2.34 us
  transfers between devices with their start and end apart: 19, of which 6 were waited for; matrix products, arithmetic and copies ran while one was open for 0% of the time, Pallas kernels for 12%

profile of v5, /device:TPU:0, one launch (start us, length us, event | category | flops | bytes accessed | tf_op | source)
XLA Modules:
  0.0 96.5 jit_solution(36230296023697292)
XLA Ops:
  0.0 5.1 %forecast.1 = (f32[192,128]{1,0:T(8,128)S(1)}, f32[192,128]{1,0:T(8,128)S(1)}, f32[192,128]{1,0:T(8,128)S(1)}, f32[192,128]{1,0:T(8,128)S(1)}, f32[192,128]{1,0:...) custom-call(s32[2,16]{1,0:T(2,128)} %cells_ref.1, ...), custom_call_target="tpu_custom_call" | custom-call | flops 19660800 | bytes 3932160 | tf_op jit(solution)/shard_map/forecast/pallas_call | solution.py:176
  5.1 13.8 %all_to_all.15 = f32[8,8,128]{2,1,0:T(8,128)S(1)} all-to-all(f32[8,8,128]{2,1,0:T(8,128)S(1)} %get-tuple-element.27), channel_id=1, replica_groups=mesh['mem'=8,'lev'=4] {'mem'}, dimensions={0} | all-to-all | bytes 65536 | tf_op jit(solution)/shard_map/all_to_all | solution.py:393
  18.9 3.5 %all-to-all-start.1 = ((f32[8,128,128]{2,1,0:T(8,128)}), f32[8,128,128]{2,1,0:T(8,128)S(1)}, u32[]{:S(2)}, u32[]{:S(2)}) async-start(f32[8,128,128]{2,1,0:T(8,128)} %get-tuple-element.41), calls=%async_computation.1 | async-start | bytes 1048576 | tf_op jit(solution)/shard_map/all_to_all | solution.py:379
  22.4 1.9 %collective-permute-start.3 = (f32[192,128]{1,0:T(8,128)S(1)}, f32[192,128]{1,0:T(8,128)S(1)}, u32[]{:S(2)}, u32[]{:S(2)}) collective-permute-start(f32[192,128]{1,0:T(8,128)S(1)} %get-tuple-element.32), channel_id=1, source_target_pairs={{0,4},{4,0},{8,12},{12,8},{16,20},{20,16},{24,28},{28,24},{1,5},{5... | collective-permute-start | bytes 294920 | tf_op jit(solution)/shard_map/ppermute | solution.py:382
  24.4 1.5 %collective-permute-start.4 = (f32[192,128]{1,0:T(8,128)S(1)}, f32[192,128]{1,0:T(8,128)S(1)}, u32[]{:S(2)}, u32[]{:S(2)}) collective-permute-start(f32[192,128]{1,0:T(8,128)S(1)} %get-tuple-element.33), channel_id=1, source_target_pairs={{0,8},{4,12},{8,0},{12,4},{16,24},{20,28},{24,16},{28,20},{1,9},{5... | collective-permute-start | bytes 294920 | tf_op jit(solution)/shard_map/ppermute | solution.py:382
  25.9 1.6 %collective-permute-start.1 = (f32[16,128]{1,0:T(8,128)S(1)}, f32[16,128]{1,0:T(8,128)S(1)}, u32[]{:S(2)}, u32[]{:S(2)}) collective-permute-start(f32[16,128]{1,0:T(8,128)S(1)} %bitcast.4), channel_id=1, source_target_pairs={{0,2},{1,3},{2,0},{3,1},{4,6},{5,7},{6,4},{7,5},{8,10},{9,11},{10,... | collective-permute-start | bytes 24584 | tf_op jit(solution)/shard_map/ppermute | solution.py:400
  27.7 1.8 %collective-permute-done.1.refs_2_ = f32[16,128]{1,0:T(8,128)S(1)} collective-permute-done((f32[16,128]{1,0:T(8,128)S(1)}, f32[16,128]{1,0:T(8,128)S(1)}, u32[]{:S(2)}, u32[]{:S(2)}) %collective-permute-start.1) | collective-permute-done | bytes 8224 | tf_op jit(solution)/shard_map/ppermute | solution.py:400
  29.6 2.4 %collective-permute-start.6 = (f32[192,128]{1,0:T(8,128)S(1)}, f32[192,128]{1,0:T(8,128)S(1)}, u32[]{:S(2)}, u32[]{:S(2)}) collective-permute-start(f32[192,128]{1,0:T(8,128)S(1)} %get-tuple-element.35), channel_id=1, source_target_pairs={{0,16},{4,20},{8,24},{12,28},{16,0},{20,4},{24,8},{28,12},{1,17},{... | collective-permute-start | bytes 294920 | tf_op jit(solution)/shard_map/ppermute | solution.py:382
  32.9 2.4 %collective-permute-start.8 = (f32[192,128]{1,0:T(8,128)S(1)}, f32[192,128]{1,0:T(8,128)S(1)}, u32[]{:S(2)}, u32[]{:S(2)}) collective-permute-start(f32[192,128]{1,0:T(8,128)S(1)} %get-tuple-element.37), channel_id=1, source_target_pairs={{0,24},{4,28},{8,16},{12,20},{16,8},{20,12},{24,0},{28,4},{1,25},{... | collective-permute-start | bytes 294920 | tf_op jit(solution)/shard_map/ppermute | solution.py:382
  35.3 3.5 %collective-permute-start.9 = (f32[192,128]{1,0:T(8,128)S(1)}, f32[192,128]{1,0:T(8,128)S(1)}, u32[]{:S(2)}, u32[]{:S(2)}) collective-permute-start(f32[192,128]{1,0:T(8,128)S(1)} %get-tuple-element.38), channel_id=1, source_target_pairs={{0,28},{4,24},{8,20},{12,16},{16,12},{20,8},{24,4},{28,0},{1,29},{... | collective-permute-start | bytes 294920 | tf_op jit(solution)/shard_map/ppermute | solution.py:382
  38.8 4.8 %filter_plan.1 = (f32[32,24,128]{2,1,0:T(8,128)S(1)}, f32[32,24,128]{2,1,0:T(8,128)S(1)}, f32[32,32,128]{2,1,0:T(8,128)S(1)}) custom-call(s32[2,16]{1,0:T(2,128)S(1)} %copy-done, f32[2,16]{1,0:T(2,128)S(1)} %copy-done.1, f32[2,16]{1,0:T(2,128)S(1)} %copy-done.2, f32[16,128]{1,0:T(8,128)S(1)} %bitcast.6, f32[16,128]{1,0:T(8,128)S(1)} %collective-permute-done.refs_1_, ...), custom_call_target="tpu_custom_call" | custom-call | flops 20000000 | bytes 1048576 | tf_op jit(solution)/shard_map/filter_plan/pallas_call | solution.py:253
  43.6 3.9 %collective-permute-done.6.refs_4_ = f32[192,128]{1,0:T(8,128)S(1)} collective-permute-done((f32[192,128]{1,0:T(8,128)S(1)}, f32[192,128]{1,0:T(8,128)S(1)}, u32[]{:S(2)}, u32[]{:S(2)}) %collective-permute-start.6) | collective-permute-done | bytes 98336 | tf_op jit(solution)/shard_map/ppermute | solution.py:382
  47.5 3.2 %collective-permute-done.7.refs_5_ = f32[192,128]{1,0:T(8,128)S(1)} collective-permute-done((f32[192,128]{1,0:T(8,128)S(1)}, f32[192,128]{1,0:T(8,128)S(1)}, u32[]{:S(2)}, u32[]{:S(2)}) %collective-permute-start.7) | collective-permute-done | bytes 98336 | tf_op jit(solution)/shard_map/ppermute | solution.py:382
  50.7 5.6 %settle.2 = (f32[192,128]{1,0:T(8,128)S(1)}, f32[192,128]{1,0:T(8,128)S(1)}, f32[192,128]{1,0:T(8,128)S(1)}, f32[192,128]{1,0:T(8,128)S(1)}, f32[192,128]{1,0:T(...) custom-call(f32[32,24,128]{2,1,0:T(8,128)S(1)} %get-tuple-element.40.anom_ref, ...), custom_call_target="tpu_custom_call" | custom-call | flops 25165824 | bytes 1572864 | tf_op jit(solution)/shard_map/settle/pallas_call | solution.py:321
  56.3 4.5 %settle.3 = f32[8,128,128]{2,1,0:T(8,128)} custom-call(f32[32,24,128]{2,1,0:T(8,128)S(1)} %get-tuple-element.40.anom_ref, f32[32,24,128]{2,1,0:T(8,128)S(1)} %get-tuple-element.29.incr_ref, f32[32,32,128]{2,1,0:T(8,128)S(1)} %get-tuple-element.30.loc_ref, f32[8,128,128]{2,1,0:T(8,128)S(1)} %all-to-all-done.1.refs_0_), custom_call_target="tpu_custom_call" | custom-call | flops 16777216 | bytes 1048576 | tf_op jit(solution)/shard_map/settle/pallas_call | solution.py:321
  60.7 4.6 %all-to-all-start.2 = ((f32[8,128,128]{2,1,0:T(8,128)}), f32[8,128,128]{2,1,0:T(8,128)S(1)}, u32[]{:S(2)}, u32[]{:S(2)}) async-start(f32[8,128,128]{2,1,0:T(8,128)} %settle.3), calls=%async_computation.2 | async-start | bytes 1048576 | tf_op jit(solution)/shard_map/all_to_all | solution.py:379
  65.4 2.0 %collective-permute-start.10 = (f32[192,128]{1,0:T(8,128)S(1)}, f32[192,128]{1,0:T(8,128)S(1)}, u32[]{:S(2)}, u32[]{:S(2)}) collective-permute-start(f32[192,128]{1,0:T(8,128)S(1)} %get-tuple-element.42), channel_id=1, source_target_pairs={{0,4},{4,0},{8,12},{12,8},{16,20},{20,16},{24,28},{28,24},{1,5},{5... | collective-permute-start | bytes 294920 | tf_op jit(solution)/shard_map/ppermute | solution.py:382
  67.4 1.5 %collective-permute-start.11 = (f32[192,128]{1,0:T(8,128)S(1)}, f32[192,128]{1,0:T(8,128)S(1)}, u32[]{:S(2)}, u32[]{:S(2)}) collective-permute-start(f32[192,128]{1,0:T(8,128)S(1)} %get-tuple-element.43), channel_id=1, source_target_pairs={{0,8},{4,12},{8,0},{12,4},{16,24},{20,28},{24,16},{28,20},{1,9},{5... | collective-permute-start | bytes 294920 | tf_op jit(solution)/shard_map/ppermute | solution.py:382
  69.1 2.7 %collective-permute-start.13 = (f32[192,128]{1,0:T(8,128)S(1)}, f32[192,128]{1,0:T(8,128)S(1)}, u32[]{:S(2)}, u32[]{:S(2)}) collective-permute-start(f32[192,128]{1,0:T(8,128)S(1)} %get-tuple-element.45), channel_id=1, source_target_pairs={{0,16},{4,20},{8,24},{12,28},{16,0},{20,4},{24,8},{28,12},{1,17},{... | collective-permute-start | bytes 294920 | tf_op jit(solution)/shard_map/ppermute | solution.py:382
  73.3 4.9 %collective-permute-start.15 = (f32[192,128]{1,0:T(8,128)S(1)}, f32[192,128]{1,0:T(8,128)S(1)}, u32[]{:S(2)}, u32[]{:S(2)}) collective-permute-start(f32[192,128]{1,0:T(8,128)S(1)} %get-tuple-element.47), channel_id=1, source_target_pairs={{0,24},{4,28},{8,16},{12,20},{16,8},{20,12},{24,0},{28,4},{1,25},{... | collective-permute-start | bytes 294920 | tf_op jit(solution)/shard_map/ppermute | solution.py:382
  78.2 3.7 %collective-permute-start.16 = (f32[192,128]{1,0:T(8,128)S(1)}, f32[192,128]{1,0:T(8,128)S(1)}, u32[]{:S(2)}, u32[]{:S(2)}) collective-permute-start(f32[192,128]{1,0:T(8,128)S(1)} %get-tuple-element.48), channel_id=1, source_target_pairs={{0,28},{4,24},{8,20},{12,16},{16,12},{20,8},{24,4},{28,0},{1,29},{... | collective-permute-start | bytes 294920 | tf_op jit(solution)/shard_map/ppermute | solution.py:382
  82.0 9.7 %collective-permute-done.13.refs_4_ = f32[192,128]{1,0:T(8,128)S(1)} collective-permute-done((f32[192,128]{1,0:T(8,128)S(1)}, f32[192,128]{1,0:T(8,128)S(1)}, u32[]{:S(2)}, u32[]{:S(2)}) %collective-permute-start.13) | collective-permute-done | bytes 98336 | tf_op jit(solution)/shard_map/ppermute | solution.py:382
  91.7 2.4 %collective-permute-done.14.refs_5_ = f32[192,128]{1,0:T(8,128)S(1)} collective-permute-done((f32[192,128]{1,0:T(8,128)S(1)}, f32[192,128]{1,0:T(8,128)S(1)}, u32[]{:S(2)}, u32[]{:S(2)}) %collective-permute-start.14) | collective-permute-done | bytes 98336 | tf_op jit(solution)/shard_map/ppermute | solution.py:382
  94.1 1.5 %assemble.2.refs_1_ = f32[2,5,64,512]{3,2,1,0:T(8,128)} custom-call(f32[192,128]{1,0:T(8,128)S(1)} %get-tuple-element.39.refs_0_, f32[192,128]{1,0:T(8,128)S(1)} %collective-permute-done.10.refs_1_, f32[192,128]{1,0:T(8,128)S(1)} %collective-permute-done.11.refs_2_, f32[192,128]{1,0:T(8,128)S(1)} %collective-permute-done.12.refs_3_, ...), custom_call_target="tpu_custom_call" | custom-call | bytes 1572864 | tf_op jit(solution)/shard_map/assemble/pallas_call | solution.py:363
  (28 shorter events, 3.8 us)
Async XLA Ops:
  0.0 38.8 %copy-start = (s32[2,16]{1,0:T(2,128)S(1)}, s32[2,16]{1,0:T(2,128)}, u32[]{:S(2)}) copy-start(s32[2,16]{1,0:T(2,128)} %cells_ref.1) | copy-start | bytes 388
  0.0 38.8 %copy-start.2 = (f32[2,16]{1,0:T(2,128)S(1)}, f32[2,16]{1,0:T(2,128)}, u32[]{:S(2)}) copy-start(f32[2,16]{1,0:T(2,128)} %errors_ref.1) | copy-start | bytes 388
  0.0 38.8 %copy-start.1 = (f32[2,16]{1,0:T(2,128)S(1)}, f32[2,16]{1,0:T(2,128)}, u32[]{:S(2)}) copy-start(f32[2,16]{1,0:T(2,128)} %values_ref.1) | copy-start | bytes 388
  18.9 37.3 %all-to-all-start.1 = ((f32[8,128,128]{2,1,0:T(8,128)}), f32[8,128,128]{2,1,0:T(8,128)S(1)}, u32[]{:S(2)}, u32[]{:S(2)}) async-start(f32[8,128,128]{2,1,0:T(8,128)} %get-tuple-element.41), calls=%async_computation.1 | async-start | bytes 1048576 | tf_op jit(solution)/shard_map/all_to_all | solution.py:379
  22.4 10.4 %collective-permute-start.3 = (f32[192,128]{1,0:T(8,128)S(1)}, f32[192,128]{1,0:T(8,128)S(1)}, u32[]{:S(2)}, u32[]{:S(2)}) collective-permute-start(f32[192,128]{1,0:T(8,128)S(1)} %get-tuple-element.32), channel_id=1, source_target_pairs={{0,4},{4,0},{8,12},{12,8},{16,20},{20,16},{24,28},{28,24},{1,5},{5... | collective-permute-start | bytes 294920 | tf_op jit(solution)/shard_map/ppermute | solution.py:382
  24.4 10.9 %collective-permute-start.4 = (f32[192,128]{1,0:T(8,128)S(1)}, f32[192,128]{1,0:T(8,128)S(1)}, u32[]{:S(2)}, u32[]{:S(2)}) collective-permute-start(f32[192,128]{1,0:T(8,128)S(1)} %get-tuple-element.33), channel_id=1, source_target_pairs={{0,8},{4,12},{8,0},{12,4},{16,24},{20,28},{24,16},{28,20},{1,9},{5... | collective-permute-start | bytes 294920 | tf_op jit(solution)/shard_map/ppermute | solution.py:382
  25.9 1.7 %collective-permute-start.2 = (f32[16,128]{1,0:T(8,128)S(1)}, f32[16,128]{1,0:T(8,128)S(1)}, u32[]{:S(2)}, u32[]{:S(2)}) collective-permute-start(f32[16,128]{1,0:T(8,128)S(1)} %bitcast.3), channel_id=1, source_target_pairs={{0,3},{1,0},{2,1},{3,2},{4,7},{5,4},{6,5},{7,6},{8,11},{9,8},{10,9... | collective-permute-start | bytes 24584 | tf_op jit(solution)/shard_map/ppermute | solution.py:400
  25.9 3.7 %collective-permute-start.1 = (f32[16,128]{1,0:T(8,128)S(1)}, f32[16,128]{1,0:T(8,128)S(1)}, u32[]{:S(2)}, u32[]{:S(2)}) collective-permute-start(f32[16,128]{1,0:T(8,128)S(1)} %bitcast.4), channel_id=1, source_target_pairs={{0,2},{1,3},{2,0},{3,1},{4,6},{5,7},{6,4},{7,5},{8,10},{9,11},{10,... | collective-permute-start | bytes 24584 | tf_op jit(solution)/shard_map/ppermute | solution.py:400
  27.4 4.6 %collective-permute-start = (f32[16,128]{1,0:T(8,128)S(1)}, f32[16,128]{1,0:T(8,128)S(1)}, u32[]{:S(2)}, u32[]{:S(2)}) collective-permute-start(f32[16,128]{1,0:T(8,128)S(1)} %bitcast.5), channel_id=1, source_target_pairs={{0,1},{1,2},{2,3},{3,0},{4,5},{5,6},{6,7},{7,4},{8,9},{9,10},{10,1... | collective-permute-start | bytes 24584 | tf_op jit(solution)/shard_map/ppermute | solution.py:400
  27.6 16.0 %collective-permute-start.5 = (f32[192,128]{1,0:T(8,128)S(1)}, f32[192,128]{1,0:T(8,128)S(1)}, u32[]{:S(2)}, u32[]{:S(2)}) collective-permute-start(f32[192,128]{1,0:T(8,128)S(1)} %get-tuple-element.34), channel_id=1, source_target_pairs={{0,12},{4,8},{8,4},{12,0},{16,28},{20,24},{24,20},{28,16},{1,13},{... | collective-permute-start | bytes 294920 | tf_op jit(solution)/shard_map/ppermute | solution.py:382
  29.6 17.9 %collective-permute-start.6 = (f32[192,128]{1,0:T(8,128)S(1)}, f32[192,128]{1,0:T(8,128)S(1)}, u32[]{:S(2)}, u32[]{:S(2)}) collective-permute-start(f32[192,128]{1,0:T(8,128)S(1)} %get-tuple-element.35), channel_id=1, source_target_pairs={{0,16},{4,20},{8,24},{12,28},{16,0},{20,4},{24,8},{28,12},{1,17},{... | collective-permute-start | bytes 294920 | tf_op jit(solution)/shard_map/ppermute | solution.py:382
  32.0 18.7 %collective-permute-start.7 = (f32[192,128]{1,0:T(8,128)S(1)}, f32[192,128]{1,0:T(8,128)S(1)}, u32[]{:S(2)}, u32[]{:S(2)}) collective-permute-start(f32[192,128]{1,0:T(8,128)S(1)} %get-tuple-element.36), channel_id=1, source_target_pairs={{0,20},{4,16},{8,28},{12,24},{16,4},{20,0},{24,12},{28,8},{1,21},{... | collective-permute-start | bytes 294920 | tf_op jit(solution)/shard_map/ppermute | solution.py:382
  32.9 17.8 %collective-permute-start.8 = (f32[192,128]{1,0:T(8,128)S(1)}, f32[192,128]{1,0:T(8,128)S(1)}, u32[]{:S(2)}, u32[]{:S(2)}) collective-permute-start(f32[192,128]{1,0:T(8,128)S(1)} %get-tuple-element.37), channel_id=1, source_target_pairs={{0,24},{4,28},{8,16},{12,20},{16,8},{20,12},{24,0},{28,4},{1,25},{... | collective-permute-start | bytes 294920 | tf_op jit(solution)/shard_map/ppermute | solution.py:382
  35.3 15.4 %collective-permute-start.9 = (f32[192,128]{1,0:T(8,128)S(1)}, f32[192,128]{1,0:T(8,128)S(1)}, u32[]{:S(2)}, u32[]{:S(2)}) collective-permute-start(f32[192,128]{1,0:T(8,128)S(1)} %get-tuple-element.38), channel_id=1, source_target_pairs={{0,28},{4,24},{8,20},{12,16},{16,12},{20,8},{24,4},{28,0},{1,29},{... | collective-permute-start | bytes 294920 | tf_op jit(solution)/shard_map/ppermute | solution.py:382
  60.7 34.9 %all-to-all-start.2 = ((f32[8,128,128]{2,1,0:T(8,128)}), f32[8,128,128]{2,1,0:T(8,128)S(1)}, u32[]{:S(2)}, u32[]{:S(2)}) async-start(f32[8,128,128]{2,1,0:T(8,128)} %settle.3), calls=%async_computation.2 | async-start | bytes 1048576 | tf_op jit(solution)/shard_map/all_to_all | solution.py:379
  65.4 7.9 %collective-permute-start.10 = (f32[192,128]{1,0:T(8,128)S(1)}, f32[192,128]{1,0:T(8,128)S(1)}, u32[]{:S(2)}, u32[]{:S(2)}) collective-permute-start(f32[192,128]{1,0:T(8,128)S(1)} %get-tuple-element.42), channel_id=1, source_target_pairs={{0,4},{4,0},{8,12},{12,8},{16,20},{20,16},{24,28},{28,24},{1,5},{5... | collective-permute-start | bytes 294920 | tf_op jit(solution)/shard_map/ppermute | solution.py:382
  67.4 10.8 %collective-permute-start.11 = (f32[192,128]{1,0:T(8,128)S(1)}, f32[192,128]{1,0:T(8,128)S(1)}, u32[]{:S(2)}, u32[]{:S(2)}) collective-permute-start(f32[192,128]{1,0:T(8,128)S(1)} %get-tuple-element.43), channel_id=1, source_target_pairs={{0,8},{4,12},{8,0},{12,4},{16,24},{20,28},{24,16},{28,20},{1,9},{5... | collective-permute-start | bytes 294920 | tf_op jit(solution)/shard_map/ppermute | solution.py:382
  68.9 13.1 %collective-permute-start.12 = (f32[192,128]{1,0:T(8,128)S(1)}, f32[192,128]{1,0:T(8,128)S(1)}, u32[]{:S(2)}, u32[]{:S(2)}) collective-permute-start(f32[192,128]{1,0:T(8,128)S(1)} %get-tuple-element.44), channel_id=1, source_target_pairs={{0,12},{4,8},{8,4},{12,0},{16,28},{20,24},{24,20},{28,16},{1,13},{... | collective-permute-start | bytes 294920 | tf_op jit(solution)/shard_map/ppermute | solution.py:382
  69.1 22.6 %collective-permute-start.13 = (f32[192,128]{1,0:T(8,128)S(1)}, f32[192,128]{1,0:T(8,128)S(1)}, u32[]{:S(2)}, u32[]{:S(2)}) collective-permute-start(f32[192,128]{1,0:T(8,128)S(1)} %get-tuple-element.45), channel_id=1, source_target_pairs={{0,16},{4,20},{8,24},{12,28},{16,0},{20,4},{24,8},{28,12},{1,17},{... | collective-permute-start | bytes 294920 | tf_op jit(solution)/shard_map/ppermute | solution.py:382
  71.8 22.3 %collective-permute-start.14 = (f32[192,128]{1,0:T(8,128)S(1)}, f32[192,128]{1,0:T(8,128)S(1)}, u32[]{:S(2)}, u32[]{:S(2)}) collective-permute-start(f32[192,128]{1,0:T(8,128)S(1)} %get-tuple-element.46), channel_id=1, source_target_pairs={{0,20},{4,16},{8,28},{12,24},{16,4},{20,0},{24,12},{28,8},{1,21},{... | collective-permute-start | bytes 294920 | tf_op jit(solution)/shard_map/ppermute | solution.py:382
  73.3 20.9 %collective-permute-start.15 = (f32[192,128]{1,0:T(8,128)S(1)}, f32[192,128]{1,0:T(8,128)S(1)}, u32[]{:S(2)}, u32[]{:S(2)}) collective-permute-start(f32[192,128]{1,0:T(8,128)S(1)} %get-tuple-element.47), channel_id=1, source_target_pairs={{0,24},{4,28},{8,16},{12,20},{16,8},{20,12},{24,0},{28,4},{1,25},{... | collective-permute-start | bytes 294920 | tf_op jit(solution)/shard_map/ppermute | solution.py:382
  78.2 15.9 %collective-permute-start.16 = (f32[192,128]{1,0:T(8,128)S(1)}, f32[192,128]{1,0:T(8,128)S(1)}, u32[]{:S(2)}, u32[]{:S(2)}) collective-permute-start(f32[192,128]{1,0:T(8,128)S(1)} %get-tuple-element.48), channel_id=1, source_target_pairs={{0,28},{4,24},{8,20},{12,16},{16,12},{20,8},{24,4},{28,0},{1,29},{... | collective-permute-start | bytes 294920 | tf_op jit(solution)/shard_map/ppermute | solution.py:382

commit v6 on v5

v6 whole, which is shorter than its diff:
```python
import functools

import jax
import jax.numpy as jnp
from jax import lax
from jax.experimental import pallas as pl
from jax.experimental.pallas import tpu as pltpu
from jax.sharding import PartitionSpec as P


STEPS = 2
LOC_HALF = 64
LANES = 128
GRANT = 24 * 1024 * 1024
TILE = 8
VMEM = pl.BlockSpec(memory_space=pltpu.VMEM)
SMEM = pl.BlockSpec(memory_space=pltpu.SMEM)


def cost(flops, nbytes):
    return pl.CostEstimate(flops=flops, bytes_accessed=nbytes, transcendentals=0)


def taper(row_gap, col_gap):
    scaled = jnp.sqrt(row_gap * row_gap + col_gap * col_gap) * (1.0 / LOC_HALF)
    inner = (
        ((-0.25 * scaled + 0.5) * scaled + 0.625) * scaled - 5.0 / 3.0
    ) * scaled * scaled + 1.0
    safe = jnp.maximum(scaled, 1.0)
    outer = (
        ((((scaled * (1.0 / 12.0) - 0.5) * scaled + 0.625) * scaled + 5.0 / 3.0) * scaled - 5.0)
        * scaled
        + 4.0
        - (2.0 / 3.0) / safe
    )
    return jnp.where(scaled <= 1.0, inner, jnp.where(scaled < 2.0, outer, 0.0))


def chunks_of(slab_dev):
    first = max(1, (2 * slab_dev) // 5)
    if slab_dev == 1:
        return ((0, 1, False),)
    return ((0, first, False), (first, slab_dev - first, True))


def row_col(cell, nx):
    if nx & (nx - 1):
        return cell // nx, cell % nx
    return lax.shift_right_logical(cell, nx.bit_length() - 1), cell & (nx - 1)


def place(ref, k):
    return ref[k // ref.shape[1], k % ref.shape[1]]


def params():
    return pltpu.CompilerParams(vmem_limit_bytes=GRANT)


def blocks_in(refs, n, whole):
    me = lax.axis_index("mem")
    return [(refs[0].at[me ^ j] if whole else refs[j], me ^ j) for j in range(n)]


def block_shapes(n, whole, rows):
    if whole:
        return [jax.ShapeDtypeStruct((n, rows, LANES), jnp.float32)]
    return [jax.ShapeDtypeStruct((rows, LANES), jnp.float32)] * n


def forecast_kernel(parts, n, cells_hbm, slabs_hbm, spread_hbm, x_hbm, cv_hbm, ch_hbm, *rest):
    outs = []
    for start, count, whole in parts:
        width = 1 if whole else n
        outs.append(blocks_in(rest[:width], n, whole))
        rest = rest[width:]
    x_buf, cv_buf, ch_buf, cells, slabs, spread, field, half, weights, picks, sem, small = rest
    slab_dev, mem_dev, ny, nx = x_buf.shape
    block = ny // n
    tiles = nx // LANES
    depth = block * tiles
    total = cells.shape[0] * cells.shape[1]

    def loads(s):
        return (
            pltpu.make_async_copy(x_hbm.at[:, s], x_buf.at[s], sem.at[0, s]),
            pltpu.make_async_copy(cv_hbm.at[s], cv_buf.at[s], sem.at[1, s]),
            pltpu.make_async_copy(ch_hbm.at[s], ch_buf.at[s], sem.at[2, s]),
        )

    lists = (
        pltpu.make_async_copy(spread_hbm, spread, small.at[0]),
        pltpu.make_async_copy(cells_hbm, cells, small.at[1]),
        pltpu.make_async_copy(slabs_hbm, slabs, small.at[2]),
    )
    for copy in lists:
        copy.start()
    for s in range(slab_dev):
        for copy in loads(s):
            copy.start()
    for copy in lists:
        copy.wait()
    sub = lax.broadcasted_iota(jnp.int32, (TILE, LANES), 0)
    lane = lax.broadcasted_iota(jnp.int32, (TILE, LANES), 1)
    east_edge, west_edge = lane == LANES - 1, lane == 0
    north_edge, south_edge = sub == TILE - 1, sub == 0
    high = ny // TILE

    def spot(r, t):
        return slice(t * ny + r * TILE, t * ny + (r + 1) * TILE)

    def advance(load, keep, store):
        known = {}

        def turned(r, t, by, axis):
            key = (r, t, by, axis)
            if key not in known:
                known[key] = pltpu.roll(load(r, t), by, axis)
            return known[key]

        def beyond(inside, r, t, by, axis, here):
            return turned(r, t, by, axis) if inside else here

        for r in range(high):
            for t in range(tiles):
                f = load(r, t)
                east = jnp.where(
                    east_edge,
                    beyond(t + 1 < tiles, r, t + 1, LANES - 1, 1, f),
                    turned(r, t, LANES - 1, 1),
                )
                west = jnp.where(
                    west_edge, beyond(t > 0, r, t - 1, 1, 1, f), turned(r, t, 1, 1)
                )
                north = jnp.where(
                    north_edge,
                    beyond(r + 1 < high, r + 1, t, TILE - 1, 0, f),
                    turned(r, t, TILE - 1, 0),
                )
                south = jnp.where(
                    south_edge, beyond(r > 0, r - 1, t, 1, 0, f), turned(r, t, 1, 0)
                )
                at = spot(r, t)
                store(
                    r,
                    t,
                    (keep * f + weights[0, at, :] * east)
                    + (weights[1, at, :] * west + weights[2, at, :] * north)
                    + weights[3, at, :] * south,
                )

    for (start, count, whole), blocks in zip(parts, outs):

        def one(s, carry):
            slab = start + s
            for copy in loads(slab):
                copy.wait()
            diffuse = spread[slab]
            keep = 1.0 - 4.0 * diffuse
            for r in range(high):
                for t in range(tiles):
                    tile = (slice(r * TILE, (r + 1) * TILE), slice(t * LANES, (t + 1) * LANES))
                    half_v, half_h = 0.5 * cv_buf[slab, *tile], 0.5 * ch_buf[slab, *tile]
                    weights[0, spot(r, t), :] = diffuse - half_v
                    weights[1, spot(r, t), :] = diffuse + half_v
                    weights[2, spot(r, t), :] = diffuse - half_h
                    weights[3, spot(r, t), :] = diffuse + half_h
            for m in range(mem_dev):
                level = slab * mem_dev + m

                def first(r, t):
                    return x_buf[
                        slab, m, r * TILE : (r + 1) * TILE, t * LANES : (t + 1) * LANES
                    ]

                def later(r, t):
                    return half[spot(r, t), :]

                def between(r, t, value):
                    half[spot(r, t), :] = value

                def final(r, t, value):
                    field[level, spot(r, t), :] = value

                for step in range(STEPS):
                    advance(
                        later if step else first, keep, between if step < STEPS - 1 else final
                    )
                at = pl.multiple_of((m * count + s) * depth, TILE)
                for ref, d in blocks:
                    for t in range(tiles):
                        row = pl.multiple_of(t * ny + d * block, block)
                        ref[pl.ds(at + t * block, block), :] = field[level, pl.ds(row, block), :]
            return carry

        lax.fori_loop(0, count, one, 0)

    lane = lax.broadcasted_iota(jnp.int32, (1, LANES), 1)
    for k in range(total):
        cell = place(cells, k)
        row, col = row_col(cell, nx)
        off = place(slabs, k) - lax.axis_index("lev") * slab_dev
        inside = (off >= 0) & (off < slab_dev)
        across, wanted = row_col(col, LANES)
        wanted = jnp.where(inside, wanted, LANES)
        off = jnp.where(inside, off, 0)
        for m in range(mem_dev):
            line = field[off * mem_dev + m, pl.ds(across * ny + row, 1), :]
            picks[m, pl.ds(k, 1), :] = jnp.where(lane == wanted, line, 0.0)
    diagonal = lax.broadcasted_iota(jnp.int32, (total, LANES), 0) == lax.broadcasted_iota(
        jnp.int32, (total, LANES), 1
    )
    values = []
    for m in range(mem_dev):
        value = jnp.sum(picks[m], axis=1, keepdims=True)
        values.append(jnp.sum(jnp.where(diagonal, value, 0.0), axis=0, keepdims=True))
    for j in range(n):
        seen = jnp.zeros((TILE, LANES), jnp.float32)
        for m in range(mem_dev):
            seen = jnp.where(sub == (j * mem_dev + m) % TILE, values[m], seen)
        outs[0][j][0][pl.ds(mem_dev * parts[0][1] * depth, TILE), :] = seen


def forecast(parts, n, cells, slabs, spread, x, cv, ch):
    mem_dev, slab_dev, ny, nx = x.shape
    depth = ny // n * nx // LANES
    shapes = []
    for i, (_, count, whole) in enumerate(parts):
        shapes.append(block_shapes(n, whole, mem_dev * count * depth + (0 if i else TILE)))
    outs = pl.pallas_call(
        functools.partial(forecast_kernel, parts, n),
        in_specs=[pl.BlockSpec(memory_space=pltpu.HBM)] * 6,
        out_specs=[VMEM for group in shapes for _ in group],
        out_shape=[shape for group in shapes for shape in group],
        scratch_shapes=[
            pltpu.VMEM((slab_dev, mem_dev, ny, nx), jnp.float32),
            pltpu.VMEM(cv.shape, jnp.float32),
            pltpu.VMEM(ch.shape, jnp.float32),
            pltpu.SMEM(cells.shape, jnp.int32),
            pltpu.SMEM(slabs.shape, jnp.int32),
            pltpu.SMEM(spread.shape, jnp.float32),
            pltpu.VMEM((slab_dev * mem_dev, ny * nx // LANES, LANES), jnp.float32),
            pltpu.VMEM((ny * nx // LANES, LANES), jnp.float32),
            pltpu.VMEM((4, ny * nx // LANES, LANES), jnp.float32),
            pltpu.VMEM((mem_dev, cells.size, LANES), jnp.float32),
            pltpu.SemaphoreType.DMA((3, slab_dev)),
            pltpu.SemaphoreType.DMA((3,)),
        ],
        cost_estimate=cost(60 * x.size, 4 * (2 * x.size + 2 * cv.size)),
        compiler_params=params(),
        name="forecast",
    )(*[pltpu.with_memory_space_constraint(a, pltpu.HBM) for a in (cells, slabs, spread, x, cv, ch)])
    sends = []
    for group in shapes:
        sends.append(list(outs[: len(group)]))
        outs = outs[len(group) :]
    return sends


def reach(cells, lists, nx, block, groups):
    total = cells.shape[0] * cells.shape[1]
    me = lax.axis_index("mem")
    for g in range(groups):
        count = jnp.int32(0)
        low_col = g * TILE // block * LANES
        high_col = (g * TILE + TILE - 1) // block * LANES + LANES - 1
        low_row = me * block + g * TILE % block
        high_row = low_row + min(block, TILE) - 1
        for k in range(total):
            row, col = row_col(place(cells, k), nx)
            down = jnp.maximum(jnp.maximum(low_row - row, row - high_row), 0)
            across = jnp.maximum(jnp.maximum(low_col - col, col - high_col), 0)
            lists[g, count] = jnp.int32(k)
            near = down * down + across * across < (2 * LOC_HALF) ** 2
            count = count + near.astype(jnp.int32)
        lists[g, count] = jnp.int32(total)
        lists[g, total + 1] = count


def settle_blocks(n, mem_dev, count, depth, lists, anom_ref, incr_ref, loc_ref, ins, outs):
    total = loc_ref.shape[0] - 1
    members = n * mem_dev
    group = max(g for g in range(1, count + 1) if count % g == 0 and (g == 1 or g * members <= 48))
    turns = count // group

    def spread(ref, k, m):
        return ref[k, pl.ds(m, TILE, stride=0), :]

    def part(i, carry):
        tile, slab = i // turns, i % turns * group
        at = tile * TILE

        def spot(m, g):
            row = ((m % mem_dev) * count + slab + g) * depth + at
            return m // mem_dev, pl.ds(pl.multiple_of(row, TILE), TILE)

        xs = []
        for m in range(members):
            for g in range(group):
                src, row = spot(m, g)
                xs.append(ins[src][0][row, :])

        def step(k, xs):
            terms = [[] for _ in range(group)]
            for m in range(members):
                a = spread(anom_ref, k, m)
                for g in range(group):
                    terms[g].append(a * xs[m * group + g])
            loc = loc_ref[k, pl.ds(pl.multiple_of(at, TILE), TILE), :]
            for g in range(group):
                while len(terms[g]) > 1:
                    odd = terms[g][len(terms[g]) // 2 * 2 :]
                    terms[g] = [a + b for a, b in zip(terms[g][::2], terms[g][1::2])] + odd
            sums = [terms[g][0] * loc for g in range(group)]
            new = []
            for m in range(members):
                b = spread(incr_ref, k, m)
                for g in range(group):
                    new.append(xs[m * group + g] + b * sums[g])
            return new

        def two(i, xs):
            return tuple(step(lists[tile, 2 * i + 1], step(lists[tile, 2 * i], list(xs))))

        xs = lax.fori_loop(
            0, lax.shift_right_logical(lists[tile, total + 1] + 1, 1), two, tuple(xs)
        )
        for m in range(members):
            for g in range(group):
                src, row = spot(m, g)
                outs[src][0][row, :] = xs[m * group + g]
        return carry

    lax.fori_loop(0, depth // TILE * turns, part, 0)


def plan_kernel(nx, block, n, mem_dev, count, lev, cells, values_ref, errors_ref, *refs):
    seen_refs, refs = refs[:lev], refs[lev:]
    ins, refs = blocks_in(refs[:n], n, False), refs[n:]
    anom_ref, incr_ref, loc_ref = refs[:3]
    outs, lists = blocks_in(refs[3 : 3 + n], n, False), refs[3 + n]
    total = cells.shape[0] * cells.shape[1]
    rows = seen_refs[0][...]
    for other in seen_refs[1:]:
        rows = rows + other[...]
    members = rows.shape[0]
    depth = loc_ref.shape[1]
    at = lax.broadcasted_iota(jnp.int32, (depth, LANES), 0)
    cell_row = (lax.axis_index("mem") * block + at % block).astype(jnp.float32)
    cell_col = (
        at // block * LANES + lax.broadcasted_iota(jnp.int32, (depth, LANES), 1)
    ).astype(jnp.float32)
    lane = lax.broadcasted_iota(jnp.int32, (1, LANES), 1)
    row_of = jnp.zeros((1, LANES), jnp.float32)
    col_of = jnp.zeros((1, LANES), jnp.float32)
    where = []
    for k in range(total):
        row, col = row_col(place(cells, k), nx)
        row, col = row.astype(jnp.float32), col.astype(jnp.float32)
        where.append((row, col))
        row_of = jnp.where(lane == k, row, row_of)
        col_of = jnp.where(lane == k, col, col_of)
    mean = jnp.sum(rows, axis=0, keepdims=True) * (1.0 / members)
    rows = rows - mean
    for k in range(total):
        loc_ref[k] = taper(cell_row - where[k][0], cell_col - where[k][1])
        loc = taper(row_of - where[k][0], col_of - where[k][1])
        anomaly = jnp.broadcast_to(rows[:, k : k + 1], rows.shape)
        ybar = jnp.broadcast_to(mean[:, k : k + 1], mean.shape)
        variance = jnp.sum(anomaly * anomaly, axis=0, keepdims=True) / (members - 1) + 1e-06
        shared = jnp.sum(rows * anomaly, axis=0, keepdims=True)
        error, value = place(errors_ref, k), place(values_ref, k)
        scale = 1.0 / ((members - 1) * variance)
        shift = (ybar * error + value * variance) / (variance + error) - ybar
        shrink = jnp.sqrt(error / (variance + error)) - 1.0
        anom_ref[k, 0:members, :] = anomaly * scale
        incr_ref[k, 0:members, :] = shift + shrink * anomaly
        weight = loc * shared * scale
        mean = mean + weight * shift
        rows = rows + (weight * shrink) * anomaly
    anom_ref[total] = jnp.zeros(anom_ref.shape[1:], jnp.float32)
    incr_ref[total] = jnp.zeros(incr_ref.shape[1:], jnp.float32)
    loc_ref[total] = jnp.zeros(loc_ref.shape[1:], jnp.float32)
    reach(cells, lists, nx, block, depth // TILE)
    settle_blocks(n, mem_dev, count, depth, lists, anom_ref, incr_ref, loc_ref, ins, outs)


def filter_plan(nx, block, mem_dev, count, cells, values, errors, seen, xs):
    members = seen[0].shape[0]
    n = len(xs)
    total = cells.size
    depth = block * nx // LANES
    table = jax.ShapeDtypeStruct((total + 1, members + TILE, LANES), jnp.float32)
    tapers = jax.ShapeDtypeStruct((total + 1, depth, LANES), jnp.float32)
    shapes = [table, table, tapers] + block_shapes(n, False, mem_dev * count * depth)
    got = pl.pallas_call(
        functools.partial(plan_kernel, nx, block, n, mem_dev, count, len(seen)),
        in_specs=[SMEM] * 3 + [VMEM] * (len(seen) + n),
        out_specs=[VMEM] * len(shapes),
        out_shape=shapes,
        scratch_shapes=[pltpu.SMEM((depth // TILE, total + 2), jnp.int32)],
        cost_estimate=cost(20_000_000, 4 * total * (2 * members + depth) * LANES),
        compiler_params=params(),
        name="filter_plan",
    )(cells, values, errors, *seen, *xs)
    return got[:3], list(got[3:])


def settle_kernel(nx, block, n, mem_dev, count, depth, whole, cells, anom, incr, loc, *refs):
    width = 1 if whole else n
    ins, outs = blocks_in(refs[:width], n, whole), blocks_in(refs[width:-1], n, False)
    lists = refs[-1]
    reach(cells, lists, nx, block, depth // TILE)
    settle_blocks(n, mem_dev, count, depth, lists, anom, incr, loc, ins, outs)


def settle(nx, block, n, mem_dev, count, whole, cells, tables, xs):
    depth = block * nx // LANES
    shapes = block_shapes(n, False, mem_dev * count * depth)
    size = n * mem_dev * count * depth * LANES
    return pl.pallas_call(
        functools.partial(settle_kernel, nx, block, n, mem_dev, count, depth, whole),
        in_specs=[SMEM] + [VMEM] * (3 + len(xs)),
        out_specs=[VMEM] * len(shapes),
        out_shape=shapes,
        scratch_shapes=[pltpu.SMEM((depth // TILE, cells.size + 2), jnp.int32)],
        cost_estimate=cost(4 * cells.size * size, 8 * size),
        compiler_params=params(),
        name="settle",
    )(cells, *tables, *xs)


def assemble_kernel(n, count, *refs):
    out_ref, turn = refs[-2], refs[-1]
    blocks = blocks_in(refs[:n], n, False)
    mem_dev, _, ny, nx = out_ref.shape
    block = ny // n
    tiles = nx // LANES
    depth = block * tiles
    slab = pl.program_id(0)
    for m in range(mem_dev):
        at = pl.multiple_of((m * count + slab) * depth, TILE)
        for t in range(tiles):
            lanes = slice(t * LANES, (t + 1) * LANES)
            lines = pl.ds(at + t * block, block)
            for j, (ref, d) in enumerate(blocks):
                if block % TILE == 0:
                    row = pl.multiple_of(d * block, block)
                    out_ref[m, 0, pl.ds(row, block), lanes] = ref[lines, :]
                else:
                    turn[pl.ds(j * block, block), :] = ref[lines, :]
            if block % TILE:
                for d, (_, j) in enumerate(blocks):
                    out_ref[m, 0, d * block : (d + 1) * block, lanes] = turn[
                        pl.ds(j * block, block), :
                    ]


def assemble(n, start, count, recv, shape, before):
    mem_dev, _, ny, nx = shape
    extra = [] if before is None else [before]
    return pl.pallas_call(
        functools.partial(assemble_kernel, n, count),
        grid=(count,),
        in_specs=[VMEM] * n + [pl.BlockSpec(memory_space=pl.ANY)] * len(extra),
        out_specs=pl.BlockSpec((mem_dev, 1, ny, nx), lambda s: (0, start + s, 0, 0)),
        out_shape=jax.ShapeDtypeStruct(shape, jnp.float32),
        scratch_shapes=[pltpu.VMEM((ny, LANES), jnp.float32)],
        input_output_aliases={} if before is None else {n: 0},
        cost_estimate=cost(0, 8 * n * recv[0].size),
        compiler_params=params(),
        name="assemble",
    )(*recv, *extra)


def exchange(blocks, n, whole):
    if whole:
        return [lax.all_to_all(blocks[0], "mem", split_axis=0, concat_axis=0, tiled=True)]
    got = {}
    for j in range(n - 1, 0, -1):
        got[j] = lax.ppermute(blocks[j], "mem", [(i, i ^ j) for i in range(n)])
    return blocks[:1] + [got[j] for j in range(1, n)]


def body(x, cv, ch, spread, obs_cells, obs_slabs, obs_values, obs_error):
    mem_dev, slab_dev, ny, nx = x.shape
    n, lev = lax.axis_size("mem"), lax.axis_size("lev")
    block = ny // n
    depth = block * nx // LANES
    parts = chunks_of(slab_dev)
    sends = forecast(parts, n, obs_cells, obs_slabs, spread, x, cv, ch)
    states = []
    for c, blocks in enumerate(sends):
        states.append(exchange(blocks, n, parts[c][2]))
    per = TILE // mem_dev
    seen = [s[mem_dev * parts[0][1] * depth :, :] for s in states[0]]
    seen = jnp.concatenate([sum(seen[g : g + per]) for g in range(0, n, per)])
    tiles = [seen] + [
        lax.ppermute(seen, "lev", [(i, (i + d) % lev) for i in range(lev)])
        for d in range(1, lev)
    ]
    result = None
    for c, ((start, count, whole), state) in enumerate(zip(parts, states)):
        if c == 0:
            tables, new = filter_plan(
                nx, block, mem_dev, count, obs_cells, obs_values, obs_error, tiles, state
            )
        else:
            new = settle(
                nx, block, n, mem_dev, count, whole, obs_cells, tables, state
            )
        back = exchange(list(new), n, False)
        result = assemble(n, start, count, back, x.shape, result)
    return result


def solution(mesh):
    in_specs = (
        P("mem", "lev", None, None),
        P("lev", None, None),
        P("lev", None, None),
        P("lev"),
        P(),
        P(),
        P(),
        P(),
    )
    out_specs = P("mem", "lev", None, None)
    return jax.shard_map(body, mesh=mesh, in_specs=in_specs, out_specs=out_specs, check_vma=False)
```

time: 97.3 us -> 93.7 us (0.963)
  blocking collectives: 13.8 us -> 0 us
  starting transfers between devices: 39.1 us -> 47.1 us
  waiting for transfers between devices: 21.2 us -> 27.5 us
  Pallas kernels: 22.3 us -> 18.8 us
    all_to_all x1 -> x0, blocking collectives: 13.8 us -> none  [body(): seen = lax.all_to_all(sends[-1][0], 'mem', 0, 0, tiled=True)]
    ppermute x14 -> x21, starting transfers between devices: 29.3 us -> 37.8 us  [exchange(): got[j] = lax.ppermute(blocks[j], 'mem', [(i, i ^ j) for i in range(n)])]
    ppermute x14 -> x21, waiting for transfers between devices: 19.3 us -> 24.5 us  [exchange(): got[j] = lax.ppermute(blocks[j], 'mem', [(i, i ^ j) for i in range(n)])]
    pallas_call x5 -> x4, Pallas kernels: 17.2 us -> 14.6 us  [the longest x1 7.48 us: filter_plan(): pl.pallas_call(functools.partial(plan_kernel, nx, block, n, mem_dev, coun...]
    ppermute x3, waiting for transfers between devices: 1.84 us -> 2.92 us  [body(): lax.ppermute(seen, 'lev', [(i, (i + d) % lev) for i in range(lev)])]
    all_to_all x2 -> x1, starting transfers between devices: 8.14 us -> 7.47 us  [exchange(): lax.all_to_all(blocks[0], 'mem', split_axis=0, concat_axis=0, tiled=True)]
  transfers between devices with their start and end apart: 19 -> 25, of which waited for: 6 -> 10; matrix products, arithmetic and copies ran while one was open for 0% -> 0% of each run, Pallas kernels for 12% -> 14%
where the time goes in v6:
time: 93.7 us; the launch traced here: 93.5 us
  starting transfers between devices  47.1 us (50%)
  waiting for transfers between devices  27.5 us (29%)
  Pallas kernels  18.8 us (20%)
    ppermute x21, starting transfers between devices, exchange(): got[j] = lax.ppermute(blocks[j], 'mem', [(i, i ^ j) for i in range(n)])  37.8 us
    ppermute x21, waiting for transfers between devices, exchange(): got[j] = lax.ppermute(blocks[j], 'mem', [(i, i ^ j) for i in range(n)])  24.5 us
    pallas_call x1, Pallas kernels, filter_plan(): pl.pallas_call(functools.partial(plan_kernel, nx, block, n, mem_dev, coun...  7.48 us
    all_to_all x1, starting transfers between devices, exchange(): lax.all_to_all(blocks[0], 'mem', split_axis=0, concat_axis=0, tiled=True)  7.47 us
    pallas_call x1, Pallas kernels, settle(): pl.pallas_call(functools.partial(settle_kernel, nx, block, n, mem_dev, co...  4.76 us
    pallas_call x1, Pallas kernels, forecast(): pl.pallas_call(functools.partial(forecast_kernel, parts, n), in_specs=[pl...  4.23 us
    ppermute x3, waiting for transfers between devices, body(): lax.ppermute(seen, 'lev', [(i, (i + d) % lev) for i in range(lev)])  2.92 us
    pallas_call x2, Pallas kernels, assemble(): pl.pallas_call(functools.partial(assemble_kernel, n, count), grid=(count,...  2.33 us
  transfers between devices with their start and end apart: 25, of which 10 were waited for; matrix products, arithmetic and copies ran while one was open for 0% of the time, Pallas kernels for 14%

profile of v6, /device:TPU:0, one launch (start us, length us, event | category | flops | bytes accessed | tf_op | source)
XLA Modules:
  0.0 93.5 jit_solution(3353929607605270722)
XLA Ops:
  0.0 4.2 %forecast.1 = (f32[136,128]{1,0:T(8,128)S(1)}, f32[136,128]{1,0:T(8,128)S(1)}, f32[136,128]{1,0:T(8,128)S(1)}, f32[136,128]{1,0:T(8,128)S(1)}, f32[136,128]{1,0:...) custom-call(s32[2,16]{1,0:T(2,128)} %cells.3, ...), custom_call_target="tpu_custom_call" | custom-call | flops 19660800 | bytes 3932160 | tf_op jit(solution)/shard_map/forecast/pallas_call | solution.py:230
  4.3 7.5 %all-to-all-start = ((f32[8,192,128]{2,1,0:T(8,128)}), f32[8,192,128]{2,1,0:T(8,128)S(1)}, u32[]{:S(2)}, u32[]{:S(2)}) async-start(f32[8,192,128]{2,1,0:T(8,128)} %get-tuple-element.44), calls=%async_computation | async-start | bytes 1572864 | tf_op jit(solution)/shard_map/all_to_all | solution.py:478
  11.8 2.0 %collective-permute-start = (f32[136,128]{1,0:T(8,128)S(1)}, f32[136,128]{1,0:T(8,128)S(1)}, u32[]{:S(2)}, u32[]{:S(2)}) collective-permute-start(f32[136,128]{1,0:T(8,128)S(1)} %get-tuple-element.34), channel_id=1, source_target_pairs={{0,4},{4,0},{8,12},{12,8},{16,20},{20,16},{24,28},{28,24},{1,5},{5... | collective-permute-start | bytes 208904 | tf_op jit(solution)/shard_map/ppermute | solution.py:481
  15.3 2.9 %collective-permute-start.3 = (f32[136,128]{1,0:T(8,128)S(1)}, f32[136,128]{1,0:T(8,128)S(1)}, u32[]{:S(2)}, u32[]{:S(2)}) collective-permute-start(f32[136,128]{1,0:T(8,128)S(1)} %get-tuple-element.37), channel_id=1, source_target_pairs={{0,16},{4,20},{8,24},{12,28},{16,0},{20,4},{24,8},{28,12},{1,17},{... | collective-permute-start | bytes 208904 | tf_op jit(solution)/shard_map/ppermute | solution.py:481
  20.6 2.4 %collective-permute-start.5 = (f32[136,128]{1,0:T(8,128)S(1)}, f32[136,128]{1,0:T(8,128)S(1)}, u32[]{:S(2)}, u32[]{:S(2)}) collective-permute-start(f32[136,128]{1,0:T(8,128)S(1)} %get-tuple-element.39), channel_id=1, source_target_pairs={{0,24},{4,28},{8,16},{12,20},{16,8},{20,12},{24,0},{28,4},{1,25},{... | collective-permute-start | bytes 208904 | tf_op jit(solution)/shard_map/ppermute | solution.py:481
  23.0 4.2 %collective-permute-done.1.refs_6_ = f32[136,128]{1,0:T(8,128)S(1)} collective-permute-done((f32[136,128]{1,0:T(8,128)S(1)}, f32[136,128]{1,0:T(8,128)S(1)}, u32[]{:S(2)}, u32[]{:S(2)}) %collective-permute-start.1) | collective-permute-done | bytes 69664 | tf_op jit(solution)/shard_map/ppermute | solution.py:481
  27.2 4.7 %collective-permute-start.6 = (f32[136,128]{1,0:T(8,128)S(1)}, f32[136,128]{1,0:T(8,128)S(1)}, u32[]{:S(2)}, u32[]{:S(2)}) collective-permute-start(f32[136,128]{1,0:T(8,128)S(1)} %get-tuple-element.40), channel_id=1, source_target_pairs={{0,28},{4,24},{8,20},{12,16},{16,12},{20,8},{24,4},{28,0},{1,29},{... | collective-permute-start | bytes 208904 | tf_op jit(solution)/shard_map/ppermute | solution.py:481
  31.9 8.8 %collective-permute-done.3.refs_8_ = f32[136,128]{1,0:T(8,128)S(1)} collective-permute-done((f32[136,128]{1,0:T(8,128)S(1)}, f32[136,128]{1,0:T(8,128)S(1)}, u32[]{:S(2)}, u32[]{:S(2)}) %collective-permute-start.3) | collective-permute-done | bytes 69664 | tf_op jit(solution)/shard_map/ppermute | solution.py:481
  40.7 2.0 %collective-permute-done.4.refs_9_ = f32[136,128]{1,0:T(8,128)S(1)} collective-permute-done((f32[136,128]{1,0:T(8,128)S(1)}, f32[136,128]{1,0:T(8,128)S(1)}, u32[]{:S(2)}, u32[]{:S(2)}) %collective-permute-start.4) | collective-permute-done | bytes 69664 | tf_op jit(solution)/shard_map/ppermute | solution.py:481
  42.8 1.6 %collective-permute-start.8 = (f32[16,128]{1,0:T(8,128)S(1)}, f32[16,128]{1,0:T(8,128)S(1)}, u32[]{:S(2)}, u32[]{:S(2)}) collective-permute-start(f32[16,128]{1,0:T(8,128)S(1)} %pad_maximum_fusion.refs_0_), channel_id=1, source_target_pairs={{0,2},{1,3},{2,0},{3,1},{4,6},{5,7},{6,4},{7,5},{8,10},{9,11},{10,... | collective-permute-start | bytes 24584 | tf_op jit(solution)/shard_map/ppermute | solution.py:499
  44.5 2.0 %collective-permute-done.8.refs_2_ = f32[16,128]{1,0:T(8,128)S(1)} collective-permute-done((f32[16,128]{1,0:T(8,128)S(1)}, f32[16,128]{1,0:T(8,128)S(1)}, u32[]{:S(2)}, u32[]{:S(2)}) %collective-permute-start.8) | collective-permute-done | bytes 8224 | tf_op jit(solution)/shard_map/ppermute | solution.py:499
  47.4 7.5 %filter_plan.1 = (f32[33,24,128]{2,1,0:T(8,128)S(1)}, f32[33,24,128]{2,1,0:T(8,128)S(1)}, f32[33,32,128]{2,1,0:T(8,128)S(1)}, f32[128,128]{1,0:T(8,128)S(1)}, f3...) custom-call(s32[2,16]{1,0:T(2,128)S(1)} %copy-done, ...), custom_call_target="tpu_custom_call" | custom-call | flops 20000000 | bytes 1048576 | tf_op jit(solution)/shard_map/filter_plan/pallas_call | solution.py:396
  56.0 2.2 %collective-permute-start.18 = (f32[128,128]{1,0:T(8,128)S(1)}, f32[128,128]{1,0:T(8,128)S(1)}, u32[]{:S(2)}, u32[]{:S(2)}) collective-permute-start(f32[128,128]{1,0:T(8,128)S(1)} %get-tuple-element.55), channel_id=1, source_target_pairs={{0,8},{4,12},{8,0},{12,4},{16,24},{20,28},{24,16},{28,20},{1,9},{5... | collective-permute-start | bytes 196616 | tf_op jit(solution)/shard_map/ppermute | solution.py:481
  59.0 2.2 %collective-permute-start.20 = (f32[128,128]{1,0:T(8,128)S(1)}, f32[128,128]{1,0:T(8,128)S(1)}, u32[]{:S(2)}, u32[]{:S(2)}) collective-permute-start(f32[128,128]{1,0:T(8,128)S(1)} %get-tuple-element.57), channel_id=1, source_target_pairs={{0,16},{4,20},{8,24},{12,28},{16,0},{20,4},{24,8},{28,12},{1,17},{... | collective-permute-start | bytes 196616 | tf_op jit(solution)/shard_map/ppermute | solution.py:481
  61.2 4.8 %settle.1 = (f32[192,128]{1,0:T(8,128)S(1)}, f32[192,128]{1,0:T(8,128)S(1)}, f32[192,128]{1,0:T(8,128)S(1)}, f32[192,128]{1,0:T(8,128)S(1)}, f32[192,128]{1,0:T(...) custom-call(s32[2,16]{1,0:T(2,128)S(1)} %copy-done, ...), custom_call_target="tpu_custom_call" | custom-call | flops 25165824 | bytes 1572864 | tf_op jit(solution)/shard_map/settle/pallas_call | solution.py:421
  66.6 3.6 %collective-permute-start.21 = (f32[128,128]{1,0:T(8,128)S(1)}, f32[128,128]{1,0:T(8,128)S(1)}, u32[]{:S(2)}, u32[]{:S(2)}) collective-permute-start(f32[128,128]{1,0:T(8,128)S(1)} %get-tuple-element.58), channel_id=1, source_target_pairs={{0,20},{4,16},{8,28},{12,24},{16,4},{20,0},{24,12},{28,8},{1,21},{... | collective-permute-start | bytes 196616 | tf_op jit(solution)/shard_map/ppermute | solution.py:481
  70.2 1.6 %collective-permute-start.22 = (f32[128,128]{1,0:T(8,128)S(1)}, f32[128,128]{1,0:T(8,128)S(1)}, u32[]{:S(2)}, u32[]{:S(2)}) collective-permute-start(f32[128,128]{1,0:T(8,128)S(1)} %get-tuple-element.59), channel_id=1, source_target_pairs={{0,24},{4,28},{8,16},{12,20},{16,8},{20,12},{24,0},{28,4},{1,25},{... | collective-permute-start | bytes 196616 | tf_op jit(solution)/shard_map/ppermute | solution.py:481
  71.9 2.2 %collective-permute-start.23 = (f32[128,128]{1,0:T(8,128)S(1)}, f32[128,128]{1,0:T(8,128)S(1)}, u32[]{:S(2)}, u32[]{:S(2)}) collective-permute-start(f32[128,128]{1,0:T(8,128)S(1)} %get-tuple-element.60), channel_id=1, source_target_pairs={{0,28},{4,24},{8,20},{12,16},{16,12},{20,8},{24,4},{28,0},{1,29},{... | collective-permute-start | bytes 196616 | tf_op jit(solution)/shard_map/ppermute | solution.py:481
  74.1 2.4 %collective-permute-start.12 = (f32[192,128]{1,0:T(8,128)S(1)}, f32[192,128]{1,0:T(8,128)S(1)}, u32[]{:S(2)}, u32[]{:S(2)}) collective-permute-start(f32[192,128]{1,0:T(8,128)S(1)} %get-tuple-element.48), channel_id=1, source_target_pairs={{0,12},{4,8},{8,4},{12,0},{16,28},{20,24},{24,20},{28,16},{1,13},{... | collective-permute-start | bytes 294920 | tf_op jit(solution)/shard_map/ppermute | solution.py:481
  77.9 1.7 %collective-permute-done.23.refs_7_ = f32[128,128]{1,0:T(8,128)S(1)} collective-permute-done((f32[128,128]{1,0:T(8,128)S(1)}, f32[128,128]{1,0:T(8,128)S(1)}, u32[]{:S(2)}, u32[]{:S(2)}) %collective-permute-start.23) | collective-permute-done | bytes 65568 | tf_op jit(solution)/shard_map/ppermute | solution.py:481
  79.6 2.8 %collective-permute-start.14 = (f32[192,128]{1,0:T(8,128)S(1)}, f32[192,128]{1,0:T(8,128)S(1)}, u32[]{:S(2)}, u32[]{:S(2)}) collective-permute-start(f32[192,128]{1,0:T(8,128)S(1)} %get-tuple-element.50), channel_id=1, source_target_pairs={{0,20},{4,16},{8,28},{12,24},{16,4},{20,0},{24,12},{28,8},{1,21},{... | collective-permute-start | bytes 294920 | tf_op jit(solution)/shard_map/ppermute | solution.py:481
  82.3 2.2 %collective-permute-start.15 = (f32[192,128]{1,0:T(8,128)S(1)}, f32[192,128]{1,0:T(8,128)S(1)}, u32[]{:S(2)}, u32[]{:S(2)}) collective-permute-start(f32[192,128]{1,0:T(8,128)S(1)} %get-tuple-element.51), channel_id=1, source_target_pairs={{0,24},{4,28},{8,16},{12,20},{16,8},{20,12},{24,0},{28,4},{1,25},{... | collective-permute-start | bytes 294920 | tf_op jit(solution)/shard_map/ppermute | solution.py:481
  85.6 4.6 %collective-permute-done.14.refs_5_ = f32[192,128]{1,0:T(8,128)S(1)} collective-permute-done((f32[192,128]{1,0:T(8,128)S(1)}, f32[192,128]{1,0:T(8,128)S(1)}, u32[]{:S(2)}, u32[]{:S(2)}) %collective-permute-start.14) | collective-permute-done | bytes 98336 | tf_op jit(solution)/shard_map/ppermute | solution.py:481
  90.2 1.7 %collective-permute-done.16.refs_7_ = f32[192,128]{1,0:T(8,128)S(1)} collective-permute-done((f32[192,128]{1,0:T(8,128)S(1)}, f32[192,128]{1,0:T(8,128)S(1)}, u32[]{:S(2)}, u32[]{:S(2)}) %collective-permute-start.16) | collective-permute-done | bytes 98336 | tf_op jit(solution)/shard_map/ppermute | solution.py:481
  (40 shorter events, 11.5 us)
Async XLA Ops:
  4.3 56.9 %all-to-all-start = ((f32[8,192,128]{2,1,0:T(8,128)}), f32[8,192,128]{2,1,0:T(8,128)S(1)}, u32[]{:S(2)}, u32[]{:S(2)}) async-start(f32[8,192,128]{2,1,0:T(8,128)} %get-tuple-element.44), calls=%async_computation | async-start | bytes 1572864 | tf_op jit(solution)/shard_map/all_to_all | solution.py:478
  11.8 8.8 %collective-permute-start = (f32[136,128]{1,0:T(8,128)S(1)}, f32[136,128]{1,0:T(8,128)S(1)}, u32[]{:S(2)}, u32[]{:S(2)}) collective-permute-start(f32[136,128]{1,0:T(8,128)S(1)} %get-tuple-element.34), channel_id=1, source_target_pairs={{0,4},{4,0},{8,12},{12,8},{16,20},{20,16},{24,28},{28,24},{1,5},{5... | collective-permute-start | bytes 208904 | tf_op jit(solution)/shard_map/ppermute | solution.py:481
  13.8 13.4 %collective-permute-start.1 = (f32[136,128]{1,0:T(8,128)S(1)}, f32[136,128]{1,0:T(8,128)S(1)}, u32[]{:S(2)}, u32[]{:S(2)}) collective-permute-start(f32[136,128]{1,0:T(8,128)S(1)} %get-tuple-element.35), channel_id=1, source_target_pairs={{0,8},{4,12},{8,0},{12,4},{16,24},{20,28},{24,16},{28,20},{1,9},{5... | collective-permute-start | bytes 208904 | tf_op jit(solution)/shard_map/ppermute | solution.py:481
  15.2 16.7 %collective-permute-start.2 = (f32[136,128]{1,0:T(8,128)S(1)}, f32[136,128]{1,0:T(8,128)S(1)}, u32[]{:S(2)}, u32[]{:S(2)}) collective-permute-start(f32[136,128]{1,0:T(8,128)S(1)} %get-tuple-element.36), channel_id=1, source_target_pairs={{0,12},{4,8},{8,4},{12,0},{16,28},{20,24},{24,20},{28,16},{1,13},{... | collective-permute-start | bytes 208904 | tf_op jit(solution)/shard_map/ppermute | solution.py:481
  15.3 25.5 %collective-permute-start.3 = (f32[136,128]{1,0:T(8,128)S(1)}, f32[136,128]{1,0:T(8,128)S(1)}, u32[]{:S(2)}, u32[]{:S(2)}) collective-permute-start(f32[136,128]{1,0:T(8,128)S(1)} %get-tuple-element.37), channel_id=1, source_target_pairs={{0,16},{4,20},{8,24},{12,28},{16,0},{20,4},{24,8},{28,12},{1,17},{... | collective-permute-start | bytes 208904 | tf_op jit(solution)/shard_map/ppermute | solution.py:481
  18.2 24.5 %collective-permute-start.4 = (f32[136,128]{1,0:T(8,128)S(1)}, f32[136,128]{1,0:T(8,128)S(1)}, u32[]{:S(2)}, u32[]{:S(2)}) collective-permute-start(f32[136,128]{1,0:T(8,128)S(1)} %get-tuple-element.38), channel_id=1, source_target_pairs={{0,20},{4,16},{8,28},{12,24},{16,4},{20,0},{24,12},{28,8},{1,21},{... | collective-permute-start | bytes 208904 | tf_op jit(solution)/shard_map/ppermute | solution.py:481
  20.6 22.1 %collective-permute-start.5 = (f32[136,128]{1,0:T(8,128)S(1)}, f32[136,128]{1,0:T(8,128)S(1)}, u32[]{:S(2)}, u32[]{:S(2)}) collective-permute-start(f32[136,128]{1,0:T(8,128)S(1)} %get-tuple-element.39), channel_id=1, source_target_pairs={{0,24},{4,28},{8,16},{12,20},{16,8},{20,12},{24,0},{28,4},{1,25},{... | collective-permute-start | bytes 208904 | tf_op jit(solution)/shard_map/ppermute | solution.py:481
  27.2 15.5 %collective-permute-start.6 = (f32[136,128]{1,0:T(8,128)S(1)}, f32[136,128]{1,0:T(8,128)S(1)}, u32[]{:S(2)}, u32[]{:S(2)}) collective-permute-start(f32[136,128]{1,0:T(8,128)S(1)} %get-tuple-element.40), channel_id=1, source_target_pairs={{0,28},{4,24},{8,20},{12,16},{16,12},{20,8},{24,4},{28,0},{1,29},{... | collective-permute-start | bytes 208904 | tf_op jit(solution)/shard_map/ppermute | solution.py:481
  42.8 3.7 %collective-permute-start.8 = (f32[16,128]{1,0:T(8,128)S(1)}, f32[16,128]{1,0:T(8,128)S(1)}, u32[]{:S(2)}, u32[]{:S(2)}) collective-permute-start(f32[16,128]{1,0:T(8,128)S(1)} %pad_maximum_fusion.refs_0_), channel_id=1, source_target_pairs={{0,2},{1,3},{2,0},{3,1},{4,6},{5,7},{6,4},{7,5},{8,10},{9,11},{10,... | collective-permute-start | bytes 24584 | tf_op jit(solution)/shard_map/ppermute | solution.py:499
  44.4 3.1 %collective-permute-start.7 = (f32[16,128]{1,0:T(8,128)S(1)}, f32[16,128]{1,0:T(8,128)S(1)}, u32[]{:S(2)}, u32[]{:S(2)}) collective-permute-start(f32[16,128]{1,0:T(8,128)S(1)} %pad_maximum_fusion.refs_0_), channel_id=1, source_target_pairs={{0,1},{1,2},{2,3},{3,0},{4,5},{5,6},{6,7},{7,4},{8,9},{9,10},{10,1... | collective-permute-start | bytes 24584 | tf_op jit(solution)/shard_map/ppermute | solution.py:499
  54.9 11.2 %collective-permute-start.17 = (f32[128,128]{1,0:T(8,128)S(1)}, f32[128,128]{1,0:T(8,128)S(1)}, u32[]{:S(2)}, u32[]{:S(2)}) collective-permute-start(f32[128,128]{1,0:T(8,128)S(1)} %get-tuple-element.54), channel_id=1, source_target_pairs={{0,4},{4,0},{8,12},{12,8},{16,20},{20,16},{24,28},{28,24},{1,5},{5... | collective-permute-start | bytes 196616 | tf_op jit(solution)/shard_map/ppermute | solution.py:481
  56.0 10.6 %collective-permute-start.18 = (f32[128,128]{1,0:T(8,128)S(1)}, f32[128,128]{1,0:T(8,128)S(1)}, u32[]{:S(2)}, u32[]{:S(2)}) collective-permute-start(f32[128,128]{1,0:T(8,128)S(1)} %get-tuple-element.55), channel_id=1, source_target_pairs={{0,8},{4,12},{8,0},{12,4},{16,24},{20,28},{24,16},{28,20},{1,9},{5... | collective-permute-start | bytes 196616 | tf_op jit(solution)/shard_map/ppermute | solution.py:481
  58.1 12.1 %collective-permute-start.19 = (f32[128,128]{1,0:T(8,128)S(1)}, f32[128,128]{1,0:T(8,128)S(1)}, u32[]{:S(2)}, u32[]{:S(2)}) collective-permute-start(f32[128,128]{1,0:T(8,128)S(1)} %get-tuple-element.56), channel_id=1, source_target_pairs={{0,12},{4,8},{8,4},{12,0},{16,28},{20,24},{24,20},{28,16},{1,13},{... | collective-permute-start | bytes 196616 | tf_op jit(solution)/shard_map/ppermute | solution.py:481
  59.0 12.9 %collective-permute-start.20 = (f32[128,128]{1,0:T(8,128)S(1)}, f32[128,128]{1,0:T(8,128)S(1)}, u32[]{:S(2)}, u32[]{:S(2)}) collective-permute-start(f32[128,128]{1,0:T(8,128)S(1)} %get-tuple-element.57), channel_id=1, source_target_pairs={{0,16},{4,20},{8,24},{12,28},{16,0},{20,4},{24,8},{28,12},{1,17},{... | collective-permute-start | bytes 196616 | tf_op jit(solution)/shard_map/ppermute | solution.py:481
  66.0 16.4 %collective-permute-start.10 = (f32[192,128]{1,0:T(8,128)S(1)}, f32[192,128]{1,0:T(8,128)S(1)}, u32[]{:S(2)}, u32[]{:S(2)}) collective-permute-start(f32[192,128]{1,0:T(8,128)S(1)} %get-tuple-element.46), channel_id=1, source_target_pairs={{0,4},{4,0},{8,12},{12,8},{16,20},{20,16},{24,28},{28,24},{1,5},{5... | collective-permute-start | bytes 294920 | tf_op jit(solution)/shard_map/ppermute | solution.py:481
  66.1 18.4 %collective-permute-start.11 = (f32[192,128]{1,0:T(8,128)S(1)}, f32[192,128]{1,0:T(8,128)S(1)}, u32[]{:S(2)}, u32[]{:S(2)}) collective-permute-start(f32[192,128]{1,0:T(8,128)S(1)} %get-tuple-element.47), channel_id=1, source_target_pairs={{0,8},{4,12},{8,0},{12,4},{16,24},{20,28},{24,16},{28,20},{1,9},{5... | collective-permute-start | bytes 294920 | tf_op jit(solution)/shard_map/ppermute | solution.py:481
  66.6 7.5 %collective-permute-start.21 = (f32[128,128]{1,0:T(8,128)S(1)}, f32[128,128]{1,0:T(8,128)S(1)}, u32[]{:S(2)}, u32[]{:S(2)}) collective-permute-start(f32[128,128]{1,0:T(8,128)S(1)} %get-tuple-element.58), channel_id=1, source_target_pairs={{0,20},{4,16},{8,28},{12,24},{16,4},{20,0},{24,12},{28,8},{1,21},{... | collective-permute-start | bytes 196616 | tf_op jit(solution)/shard_map/ppermute | solution.py:481
  70.2 6.9 %collective-permute-start.22 = (f32[128,128]{1,0:T(8,128)S(1)}, f32[128,128]{1,0:T(8,128)S(1)}, u32[]{:S(2)}, u32[]{:S(2)}) collective-permute-start(f32[128,128]{1,0:T(8,128)S(1)} %get-tuple-element.59), channel_id=1, source_target_pairs={{0,24},{4,28},{8,16},{12,20},{16,8},{20,12},{24,0},{28,4},{1,25},{... | collective-permute-start | bytes 196616 | tf_op jit(solution)/shard_map/ppermute | solution.py:481
  71.9 7.7 %collective-permute-start.23 = (f32[128,128]{1,0:T(8,128)S(1)}, f32[128,128]{1,0:T(8,128)S(1)}, u32[]{:S(2)}, u32[]{:S(2)}) collective-permute-start(f32[128,128]{1,0:T(8,128)S(1)} %get-tuple-element.60), channel_id=1, source_target_pairs={{0,28},{4,24},{8,20},{12,16},{16,12},{20,8},{24,4},{28,0},{1,29},{... | collective-permute-start | bytes 196616 | tf_op jit(solution)/shard_map/ppermute | solution.py:481
  74.1 11.5 %collective-permute-start.12 = (f32[192,128]{1,0:T(8,128)S(1)}, f32[192,128]{1,0:T(8,128)S(1)}, u32[]{:S(2)}, u32[]{:S(2)}) collective-permute-start(f32[192,128]{1,0:T(8,128)S(1)} %get-tuple-element.48), channel_id=1, source_target_pairs={{0,12},{4,8},{8,4},{12,0},{16,28},{20,24},{24,20},{28,16},{1,13},{... | collective-permute-start | bytes 294920 | tf_op jit(solution)/shard_map/ppermute | solution.py:481
  77.1 8.5 %collective-permute-start.13 = (f32[192,128]{1,0:T(8,128)S(1)}, f32[192,128]{1,0:T(8,128)S(1)}, u32[]{:S(2)}, u32[]{:S(2)}) collective-permute-start(f32[192,128]{1,0:T(8,128)S(1)} %get-tuple-element.49), channel_id=1, source_target_pairs={{0,16},{4,20},{8,24},{12,28},{16,0},{20,4},{24,8},{28,12},{1,17},{... | collective-permute-start | bytes 294920 | tf_op jit(solution)/shard_map/ppermute | solution.py:481
  79.6 10.7 %collective-permute-start.14 = (f32[192,128]{1,0:T(8,128)S(1)}, f32[192,128]{1,0:T(8,128)S(1)}, u32[]{:S(2)}, u32[]{:S(2)}) collective-permute-start(f32[192,128]{1,0:T(8,128)S(1)} %get-tuple-element.50), channel_id=1, source_target_pairs={{0,20},{4,16},{8,28},{12,24},{16,4},{20,0},{24,12},{28,8},{1,21},{... | collective-permute-start | bytes 294920 | tf_op jit(solution)/shard_map/ppermute | solution.py:481
  82.3 7.9 %collective-permute-start.15 = (f32[192,128]{1,0:T(8,128)S(1)}, f32[192,128]{1,0:T(8,128)S(1)}, u32[]{:S(2)}, u32[]{:S(2)}) collective-permute-start(f32[192,128]{1,0:T(8,128)S(1)} %get-tuple-element.51), channel_id=1, source_target_pairs={{0,24},{4,28},{8,16},{12,20},{16,8},{20,12},{24,0},{28,4},{1,25},{... | collective-permute-start | bytes 294920 | tf_op jit(solution)/shard_map/ppermute | solution.py:481
  84.6 7.4 %collective-permute-start.16 = (f32[192,128]{1,0:T(8,128)S(1)}, f32[192,128]{1,0:T(8,128)S(1)}, u32[]{:S(2)}, u32[]{:S(2)}) collective-permute-start(f32[192,128]{1,0:T(8,128)S(1)} %get-tuple-element.52), channel_id=1, source_target_pairs={{0,28},{4,24},{8,20},{12,16},{16,12},{20,8},{24,4},{28,0},{1,29},{... | collective-permute-start | bytes 294920 | tf_op jit(solution)/shard_map/ppermute | solution.py:481
  (4 other events, 131.3 us)

commit v7 on v6

--- a/solution.py
+++ b/solution.py
@@ -277,6 +277,62 @@
         lists[g, total + 1] = count
 
 
+def taper_kernel(nx, block, cells, values_ref, errors_ref, loc_ref, near_ref, meta_ref, out, lists, sem):
+    total = near_ref.shape[0]
+    depth = loc_ref.shape[1]
+    at = lax.broadcasted_iota(jnp.int32, (depth, LANES), 0)
+    cell_row = (lax.axis_index("mem") * block + at % block).astype(jnp.float32)
+    cell_col = (
+        at // block * LANES + lax.broadcasted_iota(jnp.int32, (depth, LANES), 1)
+    ).astype(jnp.float32)
+    lane = lax.broadcasted_iota(jnp.int32, (1, LANES), 1)
+    row_of = jnp.zeros((1, LANES), jnp.float32)
+    col_of = jnp.zeros((1, LANES), jnp.float32)
+    for k in range(total):
+        row, col = row_col(place(cells, k), nx)
+        row, col = row.astype(jnp.float32), col.astype(jnp.float32)
+        row_of = jnp.where(lane == k, row, row_of)
+        col_of = jnp.where(lane == k, col, col_of)
+        loc_ref[k] = taper(cell_row - row, cell_col - col)
+        meta_ref[k, 0:1, :] = jnp.full((1, LANES), place(errors_ref, k), jnp.float32)
+        meta_ref[k, 1:2, :] = jnp.full((1, LANES), place(values_ref, k), jnp.float32)
+    loc_ref[total] = jnp.zeros((depth, LANES), jnp.float32)
+    reach(cells, lists, nx, block, depth // TILE)
+    copy = pltpu.make_async_copy(lists, out, sem)
+    copy.start()
+    diagonal = lax.broadcasted_iota(jnp.int32, (total, LANES), 0) == lax.broadcasted_iota(
+        jnp.int32, (total, LANES), 1
+    )
+    own_row = jnp.sum(jnp.where(diagonal, row_of, 0.0), axis=1, keepdims=True)
+    own_col = jnp.sum(jnp.where(diagonal, col_of, 0.0), axis=1, keepdims=True)
+    near_ref[...] = taper(row_of - own_row, col_of - own_col)
+    copy.wait()
+
+
+def list_shape(depth):
+    return (-(-depth // TILE // TILE) * TILE, LANES)
+
+
+def taper_tables(nx, block, cells, values, errors):
+    total = cells.size
+    depth = block * nx // LANES
+    return pl.pallas_call(
+        functools.partial(taper_kernel, nx, block),
+        in_specs=[SMEM] * 3,
+        out_specs=[VMEM] * 4,
+        out_shape=[
+            jax.ShapeDtypeStruct((total + 1, depth, LANES), jnp.float32),
+            jax.ShapeDtypeStruct((total, LANES), jnp.float32),
+            jax.ShapeDtypeStruct((total, TILE, LANES), jnp.float32),
+            jax.ShapeDtypeStruct(list_shape(depth), jnp.int32),
+        ],
+        scratch_shapes=[pltpu.SMEM(list_shape(depth), jnp.int32), pltpu.SemaphoreType.DMA(())],
+        cost_estimate=cost(60 * total * depth * LANES, 4 * total * depth * LANES),
+        compiler_params=params(),
+        name="taper_tables",
+    )(cells, values, errors)
+
+
 def settle_blocks(n, mem_dev, count, depth, lists, anom_ref, incr_ref, loc_ref, ins, outs):
     total = loc_ref.shape[0] - 1
     members = n * mem_dev
@@ -334,100 +390,85 @@
     lax.fori_loop(0, depth // TILE * turns, part, 0)
 
 
-def plan_kernel(nx, block, n, mem_dev, count, lev, cells, values_ref, errors_ref, *refs):
+def plan_kernel(n, mem_dev, count, lev, loc_ref, near_ref, meta_ref, lists_ref, *refs):
     seen_refs, refs = refs[:lev], refs[lev:]
     ins, refs = blocks_in(refs[:n], n, False), refs[n:]
-    anom_ref, incr_ref, loc_ref = refs[:3]
-    outs, lists = blocks_in(refs[3 : 3 + n], n, False), refs[3 + n]
-    total = cells.shape[0] * cells.shape[1]
+    anom_ref, incr_ref = refs[:2]
+    outs = blocks_in(refs[2 : 2 + n], n, False)
+    lists, sem = refs[2 + n :]
+    copy = pltpu.make_async_copy(lists_ref, lists, sem)
+    copy.start()
+    total, depth = near_ref.shape[0], loc_ref.shape[1]
     rows = seen_refs[0][...]
     for other in seen_refs[1:]:
         rows = rows + other[...]
     members = rows.shape[0]
-    depth = loc_ref.shape[1]
-    at = lax.broadcasted_iota(jnp.int32, (depth, LANES), 0)
-    cell_row = (lax.axis_index("mem") * block + at % block).astype(jnp.float32)
-    cell_col = (
-        at // block * LANES + lax.broadcasted_iota(jnp.int32, (depth, LANES), 1)
-    ).astype(jnp.float32)
-    lane = lax.broadcasted_iota(jnp.int32, (1, LANES), 1)
-    row_of = jnp.zeros((1, LANES), jnp.float32)
-    col_of = jnp.zeros((1, LANES), jnp.float32)
-    where = []
-    for k in range(total):
-        row, col = row_col(place(cells, k), nx)
-        row, col = row.astype(jnp.float32), col.astype(jnp.float32)
-        where.append((row, col))
-        row_of = jnp.where(lane == k, row, row_of)
-        col_of = jnp.where(lane == k, col, col_of)
     mean = jnp.sum(rows, axis=0, keepdims=True) * (1.0 / members)
     rows = rows - mean
     for k in range(total):
-        loc_ref[k] = taper(cell_row - where[k][0], cell_col - where[k][1])
-        loc = taper(row_of - where[k][0], col_of - where[k][1])
+        error, value = meta_ref[k, 0:1, :], meta_ref[k, 1:2, :]
         anomaly = jnp.broadcast_to(rows[:, k : k + 1], rows.shape)
         ybar = jnp.broadcast_to(mean[:, k : k + 1], mean.shape)
         variance = jnp.sum(anomaly * anomaly, axis=0, keepdims=True) / (members - 1) + 1e-06
         shared = jnp.sum(rows * anomaly, axis=0, keepdims=True)
-        error, value = place(errors_ref, k), place(values_ref, k)
         scale = 1.0 / ((members - 1) * variance)
         shift = (ybar * error + value * variance) / (variance + error) - ybar
         shrink = jnp.sqrt(error / (variance + error)) - 1.0
         anom_ref[k, 0:members, :] = anomaly * scale
         incr_ref[k, 0:members, :] = shift + shrink * anomaly
-        weight = loc * shared * scale
+        weight = near_ref[k : k + 1, :] * shared * scale
         mean = mean + weight * shift
         rows = rows + (weight * shrink) * anomaly
     anom_ref[total] = jnp.zeros(anom_ref.shape[1:], jnp.float32)
     incr_ref[total] = jnp.zeros(incr_ref.shape[1:], jnp.float32)
-    loc_ref[total] = jnp.zeros(loc_ref.shape[1:], jnp.float32)
-    reach(cells, lists, nx, block, depth // TILE)
+    copy.wait()
     settle_blocks(n, mem_dev, count, depth, lists, anom_ref, incr_ref, loc_ref, ins, outs)
 
 
-def filter_plan(nx, block, mem_dev, count, cells, values, errors, seen, xs):
+def filter_plan(mem_dev, count, places, seen, xs):
     members = seen[0].shape[0]
     n = len(xs)
-    total = cells.size
-    depth = block * nx // LANES
+    total, depth = places[1].shape[0], places[0].shape[1]
     table = jax.ShapeDtypeStruct((total + 1, members + TILE, LANES), jnp.float32)
-    tapers = jax.ShapeDtypeStruct((total + 1, depth, LANES), jnp.float32)
-    shapes = [table, table, tapers] + block_shapes(n, False, mem_dev * count * depth)
+    shapes = [table, table] + block_shapes(n, False, mem_dev * count * depth)
     got = pl.pallas_call(
-        functools.partial(plan_kernel, nx, block, n, mem_dev, count, len(seen)),
-        in_specs=[SMEM] * 3 + [VMEM] * (len(seen) + n),
+        functools.partial(plan_kernel, n, mem_dev, count, len(seen)),
+        in_specs=[VMEM] * (4 + len(seen) + n),
         out_specs=[VMEM] * len(shapes),
         out_shape=shapes,
-        scratch_shapes=[pltpu.SMEM((depth // TILE, total + 2), jnp.int32)],
+        scratch_shapes=[pltpu.SMEM(list_shape(depth), jnp.int32), pltpu.SemaphoreType.DMA(())],
         cost_estimate=cost(20_000_000, 4 * total * (2 * members + depth) * LANES),
         compiler_params=params(),
         name="filter_plan",
-    )(cells, values, errors, *seen, *xs)
-    return got[:3], list(got[3:])
-
-
-def settle_kernel(nx, block, n, mem_dev, count, depth, whole, cells, anom, incr, loc, *refs):
+    )(*places, *seen, *xs)
+    return got[:2], list(got[2:])
+
+
+def settle_kernel(n, mem_dev, count, depth, whole, lists_ref, anom, incr, loc, *refs):
     width = 1 if whole else n
-    ins, outs = blocks_in(refs[:width], n, whole), blocks_in(refs[width:-1], n, False)
-    lists = refs[-1]
-    reach(cells, lists, nx, block, depth // TILE)
+    ins, outs = blocks_in(refs[:width], n, whole), blocks_in(refs[width:-2], n, False)
+    lists, sem = refs[-2:]
+    copy = pltpu.make_async_copy(lists_ref, lists, sem)
+    copy.start()
+    copy.wait()
     settle_blocks(n, mem_dev, count, depth, lists, anom, incr, loc, ins, outs)
 
 
-def settle(nx, block, n, mem_dev, count, whole, cells, tables, xs):
-    depth = block * nx // LANES
+def settle(n, mem_dev, count, whole, places, tables, xs):
+    loc, lists = places[0], places[3]
+    depth = loc.shape[1]
     shapes = block_shapes(n, False, mem_dev * count * depth)
     size = n * mem_dev * count * depth * LANES
     return pl.pallas_call(
-        functools.partial(settle_kernel, nx, block, n, mem_dev, count, depth, whole),
-        in_specs=[SMEM] + [VMEM] * (3 + len(xs)),
+        functools.partial(settle_kernel, n, mem_dev, count, depth, whole),
+        in_specs=[VMEM] * (4 + len(xs)),
         out_specs=[VMEM] * len(shapes),
         out_shape=shapes,
-        scratch_shapes=[pltpu.SMEM((depth // TILE, cells.size + 2), jnp.int32)],
-        cost_estimate=cost(4 * cells.size * size, 8 * size),
+        scratch_shapes=[pltpu.SMEM(list_shape(depth), jnp.int32), pltpu.SemaphoreType.DMA(())],
+        cost_estimate=cost(4 * loc.shape[0] * size, 8 * size),
         compiler_params=params(),
         name="settle",
-    )(cells, *tables, *xs)
+    )(lists, *tables, loc, *xs)
 
 
 def assemble_kernel(n, count, *refs):
@@ -473,11 +514,15 @@
     )(*recv, *extra)
 
 
+def order_of(n):
+    return list(range(n // 2, n)) + list(range(n // 2 - 1, 0, -1))
+
+
 def exchange(blocks, n, whole):
     if whole:
         return [lax.all_to_all(blocks[0], "mem", split_axis=0, concat_axis=0, tiled=True)]
     got = {}
-    for j in range(n - 1, 0, -1):
+    for j in order_of(n):
         got[j] = lax.ppermute(blocks[j], "mem", [(i, i ^ j) for i in range(n)])
     return blocks[:1] + [got[j] for j in range(1, n)]
 
@@ -499,16 +544,13 @@
         lax.ppermute(seen, "lev", [(i, (i + d) % lev) for i in range(lev)])
         for d in range(1, lev)
     ]
+    places = taper_tables(nx, block, obs_cells, obs_values, obs_error)
     result = None
     for c, ((start, count, whole), state) in enumerate(zip(parts, states)):
         if c == 0:
-            tables, new = filter_plan(
-                nx, block, mem_dev, count, obs_cells, obs_values, obs_error, tiles, state
-            )
+            tables, new = filter_plan(mem_dev, count, places, tiles, state)
         else:
-            new = settle(
-                nx, block, n, mem_dev, count, whole, obs_cells, tables, state
-            )
+            new = settle(n, mem_dev, count, whole, places, tables, state)
         back = exchange(list(new), n, False)
         result = assemble(n, start, count, back, x.shape, result)
     return result

time: 93.7 us -> 92.8 us (level)
  waiting for transfers between devices: 27.5 us -> 24.5 us
  starting transfers between devices: 47.1 us -> 48.9 us
    ppermute x3, waiting for transfers between devices: 2.92 us -> 0.07 us  [body(): lax.ppermute(seen, 'lev', [(i, (i + d) % lev) for i in range(lev)])]
    ppermute x21, starting transfers between devices: 37.8 us -> 39.7 us  [exchange(): got[j] = lax.ppermute(blocks[j], 'mem', [(i, i ^ j) for i in range(n)])]
    pallas_call x2 -> x3, Pallas kernels: 12.2 us -> 12.4 us  [the longest x1 5.69 us: filter_plan(): pl.pallas_call(functools.partial(plan_kernel, n, mem_dev, count, len(seen...]
  transfers between devices with their start and end apart: 25 -> 25, of which waited for: 10 -> 9; matrix products, arithmetic and copies ran while one was open for 0% -> 0% of each run, Pallas kernels for 14% -> 14%
where the time goes in v7:
time: 92.8 us; the launch traced here: 92.6 us
  starting transfers between devices  48.9 us (53%)
  waiting for transfers between devices  24.5 us (26%)
  Pallas kernels  19 us (20%)
    ppermute x21, starting transfers between devices, exchange(): got[j] = lax.ppermute(blocks[j], 'mem', [(i, i ^ j) for i in range(n)])  39.7 us
    ppermute x21, waiting for transfers between devices, exchange(): got[j] = lax.ppermute(blocks[j], 'mem', [(i, i ^ j) for i in range(n)])  24.5 us
    all_to_all x1, starting transfers between devices, exchange(): lax.all_to_all(blocks[0], 'mem', split_axis=0, concat_axis=0, tiled=True)  7.47 us
    pallas_call x1, Pallas kernels, filter_plan(): pl.pallas_call(functools.partial(plan_kernel, n, mem_dev, count, len(seen...  5.69 us
    pallas_call x1, Pallas kernels, forecast(): pl.pallas_call(functools.partial(forecast_kernel, parts, n), in_specs=[pl...  4.23 us
    pallas_call x1, Pallas kernels, settle(): pl.pallas_call(functools.partial(settle_kernel, n, mem_dev, count, depth,...  3.86 us
    pallas_call x1, Pallas kernels, taper_tables(): pl.pallas_call(functools.partial(taper_kernel, nx, block), in_specs=[SMEM...  2.83 us
    pallas_call x2, Pallas kernels, assemble(): pl.pallas_call(functools.partial(assemble_kernel, n, count), grid=(count,...  2.36 us
  transfers between devices with their start and end apart: 25, of which 9 were waited for; matrix products, arithmetic and copies ran while one was open for 0% of the time, Pallas kernels for 14%

profile of v7, /device:TPU:0, one launch (start us, length us, event | category | flops | bytes accessed | tf_op | source)
XLA Modules:
  0.0 92.6 jit_solution(5077086107487993743)
XLA Ops:
  0.0 4.2 %forecast.1 = (f32[136,128]{1,0:T(8,128)S(1)}, f32[136,128]{1,0:T(8,128)S(1)}, f32[136,128]{1,0:T(8,128)S(1)}, f32[136,128]{1,0:T(8,128)S(1)}, f32[136,128]{1,0:...) custom-call(s32[2,16]{1,0:T(2,128)} %cells_hbm.1, ...), custom_call_target="tpu_custom_call" | custom-call | flops 19660800 | bytes 3932160 | tf_op jit(solution)/shard_map/forecast/pallas_call | solution.py:230
  4.3 7.5 %all-to-all-start = ((f32[8,192,128]{2,1,0:T(8,128)}), f32[8,192,128]{2,1,0:T(8,128)S(1)}, u32[]{:S(2)}, u32[]{:S(2)}) async-start(f32[8,192,128]{2,1,0:T(8,128)} %get-tuple-element.50), calls=%async_computation | async-start | bytes 1572864 | tf_op jit(solution)/shard_map/all_to_all | solution.py:523
  11.8 2.0 %collective-permute-start = (f32[136,128]{1,0:T(8,128)S(1)}, f32[136,128]{1,0:T(8,128)S(1)}, u32[]{:S(2)}, u32[]{:S(2)}) collective-permute-start(f32[136,128]{1,0:T(8,128)S(1)} %get-tuple-element.41), channel_id=1, source_target_pairs={{0,4},{4,0},{8,12},{12,8},{16,20},{20,16},{24,28},{28,24},{1,5},{5... | collective-permute-start | bytes 208904 | tf_op jit(solution)/shard_map/ppermute | solution.py:526
  15.3 2.9 %collective-permute-start.3 = (f32[136,128]{1,0:T(8,128)S(1)}, f32[136,128]{1,0:T(8,128)S(1)}, u32[]{:S(2)}, u32[]{:S(2)}) collective-permute-start(f32[136,128]{1,0:T(8,128)S(1)} %get-tuple-element.44), channel_id=1, source_target_pairs={{0,16},{4,20},{8,24},{12,28},{16,0},{20,4},{24,8},{28,12},{1,17},{... | collective-permute-start | bytes 208904 | tf_op jit(solution)/shard_map/ppermute | solution.py:526
  20.6 2.4 %collective-permute-start.5 = (f32[136,128]{1,0:T(8,128)S(1)}, f32[136,128]{1,0:T(8,128)S(1)}, u32[]{:S(2)}, u32[]{:S(2)}) collective-permute-start(f32[136,128]{1,0:T(8,128)S(1)} %get-tuple-element.46), channel_id=1, source_target_pairs={{0,24},{4,28},{8,16},{12,20},{16,8},{20,12},{24,0},{28,4},{1,25},{... | collective-permute-start | bytes 208904 | tf_op jit(solution)/shard_map/ppermute | solution.py:526
  23.0 4.2 %collective-permute-done.1.refs_6_ = f32[136,128]{1,0:T(8,128)S(1)} collective-permute-done((f32[136,128]{1,0:T(8,128)S(1)}, f32[136,128]{1,0:T(8,128)S(1)}, u32[]{:S(2)}, u32[]{:S(2)}) %collective-permute-start.1) | collective-permute-done | bytes 69664 | tf_op jit(solution)/shard_map/ppermute | solution.py:526
  27.2 4.7 %collective-permute-start.6 = (f32[136,128]{1,0:T(8,128)S(1)}, f32[136,128]{1,0:T(8,128)S(1)}, u32[]{:S(2)}, u32[]{:S(2)}) collective-permute-start(f32[136,128]{1,0:T(8,128)S(1)} %get-tuple-element.47), channel_id=1, source_target_pairs={{0,28},{4,24},{8,20},{12,16},{16,12},{20,8},{24,4},{28,0},{1,29},{... | collective-permute-start | bytes 208904 | tf_op jit(solution)/shard_map/ppermute | solution.py:526
  31.9 8.8 %collective-permute-done.3.refs_8_ = f32[136,128]{1,0:T(8,128)S(1)} collective-permute-done((f32[136,128]{1,0:T(8,128)S(1)}, f32[136,128]{1,0:T(8,128)S(1)}, u32[]{:S(2)}, u32[]{:S(2)}) %collective-permute-start.3) | collective-permute-done | bytes 69664 | tf_op jit(solution)/shard_map/ppermute | solution.py:526
  40.7 2.0 %collective-permute-done.4.refs_9_ = f32[136,128]{1,0:T(8,128)S(1)} collective-permute-done((f32[136,128]{1,0:T(8,128)S(1)}, f32[136,128]{1,0:T(8,128)S(1)}, u32[]{:S(2)}, u32[]{:S(2)}) %collective-permute-start.4) | collective-permute-done | bytes 69664 | tf_op jit(solution)/shard_map/ppermute | solution.py:526
  42.8 1.6 %collective-permute-start.8 = (f32[16,128]{1,0:T(8,128)S(1)}, f32[16,128]{1,0:T(8,128)S(1)}, u32[]{:S(2)}, u32[]{:S(2)}) collective-permute-start(f32[16,128]{1,0:T(8,128)S(1)} %pad_maximum_fusion.refs_0_), channel_id=1, source_target_pairs={{0,2},{1,3},{2,0},{3,1},{4,6},{5,7},{6,4},{7,5},{8,10},{9,11},{10,... | collective-permute-start | bytes 24584 | tf_op jit(solution)/shard_map/ppermute | solution.py:544
  44.5 2.8 %taper_tables.1 = (f32[33,32,128]{2,1,0:T(8,128)S(1)}, f32[32,128]{1,0:T(8,128)S(1)}, f32[32,8,128]{2,1,0:T(8,128)S(1)}, s32[8,128]{1,0:T(8,128)S(1)}) custom-call(s32[2,16]{1,0:T(2,128)S(1)} %copy-done, f32[2,16]{1,0:T(2,128)S(1)} %copy-done.1, f32[2,16]{1,0:T(2,128)S(1)} %copy-done.2), custom_call_target="tpu_custom_call" | custom-call | flops 7864320 | bytes 524288 | tf_op jit(solution)/shard_map/taper_tables/pallas_call | solution.py:319
  47.4 5.7 %filter_plan.1 = (f32[33,24,128]{2,1,0:T(8,128)S(1)}, f32[33,24,128]{2,1,0:T(8,128)S(1)}, f32[128,128]{1,0:T(8,128)S(1)}, f32[128,128]{1,0:T(8,128)S(1)}, f32[12...) custom-call(f32[33,32,128]{2,1,0:T(8,128)S(1)} %get-tuple-element.37, ...), custom_call_target="tpu_custom_call" | custom-call | flops 20000000 | bytes 1048576 | tf_op jit(solution)/shard_map/filter_plan/pallas_call | solution.py:434
  54.2 2.2 %collective-permute-start.18 = (f32[128,128]{1,0:T(8,128)S(1)}, f32[128,128]{1,0:T(8,128)S(1)}, u32[]{:S(2)}, u32[]{:S(2)}) collective-permute-start(f32[128,128]{1,0:T(8,128)S(1)} %get-tuple-element.61), channel_id=1, source_target_pairs={{0,8},{4,12},{8,0},{12,4},{16,24},{20,28},{24,16},{28,20},{1,9},{5... | collective-permute-start | bytes 196616 | tf_op jit(solution)/shard_map/ppermute | solution.py:526
  57.2 2.2 %collective-permute-start.20 = (f32[128,128]{1,0:T(8,128)S(1)}, f32[128,128]{1,0:T(8,128)S(1)}, u32[]{:S(2)}, u32[]{:S(2)}) collective-permute-start(f32[128,128]{1,0:T(8,128)S(1)} %get-tuple-element.63), channel_id=1, source_target_pairs={{0,16},{4,20},{8,24},{12,28},{16,0},{20,4},{24,8},{28,12},{1,17},{... | collective-permute-start | bytes 196616 | tf_op jit(solution)/shard_map/ppermute | solution.py:526
  59.4 3.9 %settle.1 = (f32[192,128]{1,0:T(8,128)S(1)}, f32[192,128]{1,0:T(8,128)S(1)}, f32[192,128]{1,0:T(8,128)S(1)}, f32[192,128]{1,0:T(8,128)S(1)}, f32[192,128]{1,0:T(...) custom-call(s32[8,128]{1,0:T(8,128)S(1)} %get-tuple-element.36.lists_ref, ...), custom_call_target="tpu_custom_call" | custom-call | flops 25952256 | bytes 1572864 | tf_op jit(solution)/shard_map/settle/pallas_call | solution.py:462
  63.9 3.6 %collective-permute-start.21 = (f32[128,128]{1,0:T(8,128)S(1)}, f32[128,128]{1,0:T(8,128)S(1)}, u32[]{:S(2)}, u32[]{:S(2)}) collective-permute-start(f32[128,128]{1,0:T(8,128)S(1)} %get-tuple-element.64), channel_id=1, source_target_pairs={{0,20},{4,16},{8,28},{12,24},{16,4},{20,0},{24,12},{28,8},{1,21},{... | collective-permute-start | bytes 196616 | tf_op jit(solution)/shard_map/ppermute | solution.py:526
  67.5 1.6 %collective-permute-start.22 = (f32[128,128]{1,0:T(8,128)S(1)}, f32[128,128]{1,0:T(8,128)S(1)}, u32[]{:S(2)}, u32[]{:S(2)}) collective-permute-start(f32[128,128]{1,0:T(8,128)S(1)} %get-tuple-element.65), channel_id=1, source_target_pairs={{0,24},{4,28},{8,16},{12,20},{16,8},{20,12},{24,0},{28,4},{1,25},{... | collective-permute-start | bytes 196616 | tf_op jit(solution)/shard_map/ppermute | solution.py:526
  69.2 2.3 %collective-permute-start.23 = (f32[128,128]{1,0:T(8,128)S(1)}, f32[128,128]{1,0:T(8,128)S(1)}, u32[]{:S(2)}, u32[]{:S(2)}) collective-permute-start(f32[128,128]{1,0:T(8,128)S(1)} %get-tuple-element.66), channel_id=1, source_target_pairs={{0,28},{4,24},{8,20},{12,16},{16,12},{20,8},{24,4},{28,0},{1,29},{... | collective-permute-start | bytes 196616 | tf_op jit(solution)/shard_map/ppermute | solution.py:526
  74.3 3.5 %collective-permute-start.13 = (f32[192,128]{1,0:T(8,128)S(1)}, f32[192,128]{1,0:T(8,128)S(1)}, u32[]{:S(2)}, u32[]{:S(2)}) collective-permute-start(f32[192,128]{1,0:T(8,128)S(1)} %get-tuple-element.55), channel_id=1, source_target_pairs={{0,16},{4,20},{8,24},{12,28},{16,0},{20,4},{24,8},{28,12},{1,17},{... | collective-permute-start | bytes 294920 | tf_op jit(solution)/shard_map/ppermute | solution.py:526
  77.9 2.8 %collective-permute-start.14 = (f32[192,128]{1,0:T(8,128)S(1)}, f32[192,128]{1,0:T(8,128)S(1)}, u32[]{:S(2)}, u32[]{:S(2)}) collective-permute-start(f32[192,128]{1,0:T(8,128)S(1)} %get-tuple-element.56), channel_id=1, source_target_pairs={{0,20},{4,16},{8,28},{12,24},{16,4},{20,0},{24,12},{28,8},{1,21},{... | collective-permute-start | bytes 294920 | tf_op jit(solution)/shard_map/ppermute | solution.py:526
  80.7 1.9 %collective-permute-start.15 = (f32[192,128]{1,0:T(8,128)S(1)}, f32[192,128]{1,0:T(8,128)S(1)}, u32[]{:S(2)}, u32[]{:S(2)}) collective-permute-start(f32[192,128]{1,0:T(8,128)S(1)} %get-tuple-element.57), channel_id=1, source_target_pairs={{0,24},{4,28},{8,16},{12,20},{16,8},{20,12},{24,0},{28,4},{1,25},{... | collective-permute-start | bytes 294920 | tf_op jit(solution)/shard_map/ppermute | solution.py:526
  84.9 4.0 %collective-permute-done.13.refs_4_ = f32[192,128]{1,0:T(8,128)S(1)} collective-permute-done((f32[192,128]{1,0:T(8,128)S(1)}, f32[192,128]{1,0:T(8,128)S(1)}, u32[]{:S(2)}, u32[]{:S(2)}) %collective-permute-start.13) | collective-permute-done | bytes 98336 | tf_op jit(solution)/shard_map/ppermute | solution.py:526
  88.9 2.1 %collective-permute-done.14.refs_5_ = f32[192,128]{1,0:T(8,128)S(1)} collective-permute-done((f32[192,128]{1,0:T(8,128)S(1)}, f32[192,128]{1,0:T(8,128)S(1)}, u32[]{:S(2)}, u32[]{:S(2)}) %collective-permute-start.14) | collective-permute-done | bytes 98336 | tf_op jit(solution)/shard_map/ppermute | solution.py:526
  91.0 1.5 %assemble.3 = f32[2,5,64,512]{3,2,1,0:T(8,128)} custom-call(f32[192,128]{1,0:T(8,128)S(1)} %get-tuple-element.51.refs_0_, f32[192,128]{1,0:T(8,128)S(1)} %collective-permute-done.10.refs_1_, f32[192,128]{1,0:T(8,128)S(1)} %collective-permute-done.11.refs_2_, f32[192,128]{1,0:T(8,128)S(1)} %collective-permute-done.12.refs_3_, ...), custom_call_target="tpu_custom_call", output_to_operand_aliasing={{}: (8, {})} | custom-call | bytes 1572864 | tf_op jit(solution)/shard_map/assemble/pallas_call | solution.py:503
  (41 shorter events, 11.9 us)
Async XLA Ops:
  4.3 55.1 %all-to-all-start = ((f32[8,192,128]{2,1,0:T(8,128)}), f32[8,192,128]{2,1,0:T(8,128)S(1)}, u32[]{:S(2)}, u32[]{:S(2)}) async-start(f32[8,192,128]{2,1,0:T(8,128)} %get-tuple-element.50), calls=%async_computation | async-start | bytes 1572864 | tf_op jit(solution)/shard_map/all_to_all | solution.py:523
  11.8 8.8 %collective-permute-start = (f32[136,128]{1,0:T(8,128)S(1)}, f32[136,128]{1,0:T(8,128)S(1)}, u32[]{:S(2)}, u32[]{:S(2)}) collective-permute-start(f32[136,128]{1,0:T(8,128)S(1)} %get-tuple-element.41), channel_id=1, source_target_pairs={{0,4},{4,0},{8,12},{12,8},{16,20},{20,16},{24,28},{28,24},{1,5},{5... | collective-permute-start | bytes 208904 | tf_op jit(solution)/shard_map/ppermute | solution.py:526
  13.8 13.4 %collective-permute-start.1 = (f32[136,128]{1,0:T(8,128)S(1)}, f32[136,128]{1,0:T(8,128)S(1)}, u32[]{:S(2)}, u32[]{:S(2)}) collective-permute-start(f32[136,128]{1,0:T(8,128)S(1)} %get-tuple-element.42), channel_id=1, source_target_pairs={{0,8},{4,12},{8,0},{12,4},{16,24},{20,28},{24,16},{28,20},{1,9},{5... | collective-permute-start | bytes 208904 | tf_op jit(solution)/shard_map/ppermute | solution.py:526
  15.2 16.7 %collective-permute-start.2 = (f32[136,128]{1,0:T(8,128)S(1)}, f32[136,128]{1,0:T(8,128)S(1)}, u32[]{:S(2)}, u32[]{:S(2)}) collective-permute-start(f32[136,128]{1,0:T(8,128)S(1)} %get-tuple-element.43), channel_id=1, source_target_pairs={{0,12},{4,8},{8,4},{12,0},{16,28},{20,24},{24,20},{28,16},{1,13},{... | collective-permute-start | bytes 208904 | tf_op jit(solution)/shard_map/ppermute | solution.py:526
  15.3 25.5 %collective-permute-start.3 = (f32[136,128]{1,0:T(8,128)S(1)}, f32[136,128]{1,0:T(8,128)S(1)}, u32[]{:S(2)}, u32[]{:S(2)}) collective-permute-start(f32[136,128]{1,0:T(8,128)S(1)} %get-tuple-element.44), channel_id=1, source_target_pairs={{0,16},{4,20},{8,24},{12,28},{16,0},{20,4},{24,8},{28,12},{1,17},{... | collective-permute-start | bytes 208904 | tf_op jit(solution)/shard_map/ppermute | solution.py:526
  18.2 24.5 %collective-permute-start.4 = (f32[136,128]{1,0:T(8,128)S(1)}, f32[136,128]{1,0:T(8,128)S(1)}, u32[]{:S(2)}, u32[]{:S(2)}) collective-permute-start(f32[136,128]{1,0:T(8,128)S(1)} %get-tuple-element.45), channel_id=1, source_target_pairs={{0,20},{4,16},{8,28},{12,24},{16,4},{20,0},{24,12},{28,8},{1,21},{... | collective-permute-start | bytes 208904 | tf_op jit(solution)/shard_map/ppermute | solution.py:526
  20.6 22.1 %collective-permute-start.5 = (f32[136,128]{1,0:T(8,128)S(1)}, f32[136,128]{1,0:T(8,128)S(1)}, u32[]{:S(2)}, u32[]{:S(2)}) collective-permute-start(f32[136,128]{1,0:T(8,128)S(1)} %get-tuple-element.46), channel_id=1, source_target_pairs={{0,24},{4,28},{8,16},{12,20},{16,8},{20,12},{24,0},{28,4},{1,25},{... | collective-permute-start | bytes 208904 | tf_op jit(solution)/shard_map/ppermute | solution.py:526
  27.2 15.5 %collective-permute-start.6 = (f32[136,128]{1,0:T(8,128)S(1)}, f32[136,128]{1,0:T(8,128)S(1)}, u32[]{:S(2)}, u32[]{:S(2)}) collective-permute-start(f32[136,128]{1,0:T(8,128)S(1)} %get-tuple-element.47), channel_id=1, source_target_pairs={{0,28},{4,24},{8,20},{12,16},{16,12},{20,8},{24,4},{28,0},{1,29},{... | collective-permute-start | bytes 208904 | tf_op jit(solution)/shard_map/ppermute | solution.py:526
  42.7 4.6 %collective-permute-start.9 = (f32[16,128]{1,0:T(8,128)S(1)}, f32[16,128]{1,0:T(8,128)S(1)}, u32[]{:S(2)}, u32[]{:S(2)}) collective-permute-start(f32[16,128]{1,0:T(8,128)S(1)} %pad_maximum_fusion.refs_0_), channel_id=1, source_target_pairs={{0,3},{1,0},{2,1},{3,2},{4,7},{5,4},{6,5},{7,6},{8,11},{9,8},{10,9... | collective-permute-start | bytes 24584 | tf_op jit(solution)/shard_map/ppermute | solution.py:544
  42.8 4.6 %collective-permute-start.8 = (f32[16,128]{1,0:T(8,128)S(1)}, f32[16,128]{1,0:T(8,128)S(1)}, u32[]{:S(2)}, u32[]{:S(2)}) collective-permute-start(f32[16,128]{1,0:T(8,128)S(1)} %pad_maximum_fusion.refs_0_), channel_id=1, source_target_pairs={{0,2},{1,3},{2,0},{3,1},{4,6},{5,7},{6,4},{7,5},{8,10},{9,11},{10,... | collective-permute-start | bytes 24584 | tf_op jit(solution)/shard_map/ppermute | solution.py:544
  53.1 10.3 %collective-permute-start.17 = (f32[128,128]{1,0:T(8,128)S(1)}, f32[128,128]{1,0:T(8,128)S(1)}, u32[]{:S(2)}, u32[]{:S(2)}) collective-permute-start(f32[128,128]{1,0:T(8,128)S(1)} %get-tuple-element.60), channel_id=1, source_target_pairs={{0,4},{4,0},{8,12},{12,8},{16,20},{20,16},{24,28},{28,24},{1,5},{5... | collective-permute-start | bytes 196616 | tf_op jit(solution)/shard_map/ppermute | solution.py:526
  54.2 9.7 %collective-permute-start.18 = (f32[128,128]{1,0:T(8,128)S(1)}, f32[128,128]{1,0:T(8,128)S(1)}, u32[]{:S(2)}, u32[]{:S(2)}) collective-permute-start(f32[128,128]{1,0:T(8,128)S(1)} %get-tuple-element.61), channel_id=1, source_target_pairs={{0,8},{4,12},{8,0},{12,4},{16,24},{20,28},{24,16},{28,20},{1,9},{5... | collective-permute-start | bytes 196616 | tf_op jit(solution)/shard_map/ppermute | solution.py:526
  56.3 11.2 %collective-permute-start.19 = (f32[128,128]{1,0:T(8,128)S(1)}, f32[128,128]{1,0:T(8,128)S(1)}, u32[]{:S(2)}, u32[]{:S(2)}) collective-permute-start(f32[128,128]{1,0:T(8,128)S(1)} %get-tuple-element.62), channel_id=1, source_target_pairs={{0,12},{4,8},{8,4},{12,0},{16,28},{20,24},{24,20},{28,16},{1,13},{... | collective-permute-start | bytes 196616 | tf_op jit(solution)/shard_map/ppermute | solution.py:526
  57.2 12.0 %collective-permute-start.20 = (f32[128,128]{1,0:T(8,128)S(1)}, f32[128,128]{1,0:T(8,128)S(1)}, u32[]{:S(2)}, u32[]{:S(2)}) collective-permute-start(f32[128,128]{1,0:T(8,128)S(1)} %get-tuple-element.63), channel_id=1, source_target_pairs={{0,16},{4,20},{8,24},{12,28},{16,0},{20,4},{24,8},{28,12},{1,17},{... | collective-permute-start | bytes 196616 | tf_op jit(solution)/shard_map/ppermute | solution.py:526
  63.2 17.4 %collective-permute-start.10 = (f32[192,128]{1,0:T(8,128)S(1)}, f32[192,128]{1,0:T(8,128)S(1)}, u32[]{:S(2)}, u32[]{:S(2)}) collective-permute-start(f32[192,128]{1,0:T(8,128)S(1)} %get-tuple-element.52), channel_id=1, source_target_pairs={{0,4},{4,0},{8,12},{12,8},{16,20},{20,16},{24,28},{28,24},{1,5},{5... | collective-permute-start | bytes 294920 | tf_op jit(solution)/shard_map/ppermute | solution.py:526
  63.4 19.2 %collective-permute-start.11 = (f32[192,128]{1,0:T(8,128)S(1)}, f32[192,128]{1,0:T(8,128)S(1)}, u32[]{:S(2)}, u32[]{:S(2)}) collective-permute-start(f32[192,128]{1,0:T(8,128)S(1)} %get-tuple-element.53), channel_id=1, source_target_pairs={{0,8},{4,12},{8,0},{12,4},{16,24},{20,28},{24,16},{28,20},{1,9},{5... | collective-permute-start | bytes 294920 | tf_op jit(solution)/shard_map/ppermute | solution.py:526
  63.9 8.8 %collective-permute-start.21 = (f32[128,128]{1,0:T(8,128)S(1)}, f32[128,128]{1,0:T(8,128)S(1)}, u32[]{:S(2)}, u32[]{:S(2)}) collective-permute-start(f32[128,128]{1,0:T(8,128)S(1)} %get-tuple-element.64), channel_id=1, source_target_pairs={{0,20},{4,16},{8,28},{12,24},{16,4},{20,0},{24,12},{28,8},{1,21},{... | collective-permute-start | bytes 196616 | tf_op jit(solution)/shard_map/ppermute | solution.py:526
  67.5 6.8 %collective-permute-start.22 = (f32[128,128]{1,0:T(8,128)S(1)}, f32[128,128]{1,0:T(8,128)S(1)}, u32[]{:S(2)}, u32[]{:S(2)}) collective-permute-start(f32[128,128]{1,0:T(8,128)S(1)} %get-tuple-element.65), channel_id=1, source_target_pairs={{0,24},{4,28},{8,16},{12,20},{16,8},{20,12},{24,0},{28,4},{1,25},{... | collective-permute-start | bytes 196616 | tf_op jit(solution)/shard_map/ppermute | solution.py:526
  69.2 8.7 %collective-permute-start.23 = (f32[128,128]{1,0:T(8,128)S(1)}, f32[128,128]{1,0:T(8,128)S(1)}, u32[]{:S(2)}, u32[]{:S(2)}) collective-permute-start(f32[128,128]{1,0:T(8,128)S(1)} %get-tuple-element.66), channel_id=1, source_target_pairs={{0,28},{4,24},{8,20},{12,16},{16,12},{20,8},{24,4},{28,0},{1,29},{... | collective-permute-start | bytes 196616 | tf_op jit(solution)/shard_map/ppermute | solution.py:526
  72.7 12.2 %collective-permute-start.12 = (f32[192,128]{1,0:T(8,128)S(1)}, f32[192,128]{1,0:T(8,128)S(1)}, u32[]{:S(2)}, u32[]{:S(2)}) collective-permute-start(f32[192,128]{1,0:T(8,128)S(1)} %get-tuple-element.54), channel_id=1, source_target_pairs={{0,12},{4,8},{8,4},{12,0},{16,28},{20,24},{24,20},{28,16},{1,13},{... | collective-permute-start | bytes 294920 | tf_op jit(solution)/shard_map/ppermute | solution.py:526
  74.3 14.6 %collective-permute-start.13 = (f32[192,128]{1,0:T(8,128)S(1)}, f32[192,128]{1,0:T(8,128)S(1)}, u32[]{:S(2)}, u32[]{:S(2)}) collective-permute-start(f32[192,128]{1,0:T(8,128)S(1)} %get-tuple-element.55), channel_id=1, source_target_pairs={{0,16},{4,20},{8,24},{12,28},{16,0},{20,4},{24,8},{28,12},{1,17},{... | collective-permute-start | bytes 294920 | tf_op jit(solution)/shard_map/ppermute | solution.py:526
  77.9 13.1 %collective-permute-start.14 = (f32[192,128]{1,0:T(8,128)S(1)}, f32[192,128]{1,0:T(8,128)S(1)}, u32[]{:S(2)}, u32[]{:S(2)}) collective-permute-start(f32[192,128]{1,0:T(8,128)S(1)} %get-tuple-element.56), channel_id=1, source_target_pairs={{0,20},{4,16},{8,28},{12,24},{16,4},{20,0},{24,12},{28,8},{1,21},{... | collective-permute-start | bytes 294920 | tf_op jit(solution)/shard_map/ppermute | solution.py:526
  80.7 10.3 %collective-permute-start.15 = (f32[192,128]{1,0:T(8,128)S(1)}, f32[192,128]{1,0:T(8,128)S(1)}, u32[]{:S(2)}, u32[]{:S(2)}) collective-permute-start(f32[192,128]{1,0:T(8,128)S(1)} %get-tuple-element.57), channel_id=1, source_target_pairs={{0,24},{4,28},{8,16},{12,20},{16,8},{20,12},{24,0},{28,4},{1,25},{... | collective-permute-start | bytes 294920 | tf_op jit(solution)/shard_map/ppermute | solution.py:526
  82.6 8.4 %collective-permute-start.16 = (f32[192,128]{1,0:T(8,128)S(1)}, f32[192,128]{1,0:T(8,128)S(1)}, u32[]{:S(2)}, u32[]{:S(2)}) collective-permute-start(f32[192,128]{1,0:T(8,128)S(1)} %get-tuple-element.58), channel_id=1, source_target_pairs={{0,28},{4,24},{8,20},{12,16},{16,12},{20,8},{24,4},{28,0},{1,29},{... | collective-permute-start | bytes 294920 | tf_op jit(solution)/shard_map/ppermute | solution.py:526
  (4 other events, 123.8 us)

commit v8 on v7

--- a/solution.py
+++ b/solution.py
@@ -75,18 +75,24 @@
         outs.append(blocks_in(rest[:width], n, whole))
         rest = rest[width:]
     x_buf, cv_buf, ch_buf, cells, slabs, spread, field, half, weights, picks, sem, small = rest
-    slab_dev, mem_dev, ny, nx = x_buf.shape
+    slab_dev, mem_dev, tiles = x_buf.shape[:3]
+    ny, nx = x_buf.shape[3] - 2 * TILE, tiles * LANES
     block = ny // n
-    tiles = nx // LANES
     depth = block * tiles
     total = cells.shape[0] * cells.shape[1]
 
     def loads(s):
-        return (
-            pltpu.make_async_copy(x_hbm.at[:, s], x_buf.at[s], sem.at[0, s]),
-            pltpu.make_async_copy(cv_hbm.at[s], cv_buf.at[s], sem.at[1, s]),
-            pltpu.make_async_copy(ch_hbm.at[s], ch_buf.at[s], sem.at[2, s]),
-        )
+        return [
+            pltpu.make_async_copy(cv_hbm.at[s], cv_buf.at[s], sem.at[tiles, s]),
+            pltpu.make_async_copy(ch_hbm.at[s], ch_buf.at[s], sem.at[tiles + 1, s]),
+        ] + [
+            pltpu.make_async_copy(
+                x_hbm.at[:, s, :, t * LANES : (t + 1) * LANES],
+                x_buf.at[s, :, t, TILE : TILE + ny, :],
+                sem.at[t, s],
+            )
+            for t in range(tiles)
+        ]
 
     lists = (
         pltpu.make_async_copy(spread_hbm, spread, small.at[0]),
@@ -103,50 +109,27 @@
     sub = lax.broadcasted_iota(jnp.int32, (TILE, LANES), 0)
     lane = lax.broadcasted_iota(jnp.int32, (TILE, LANES), 1)
     east_edge, west_edge = lane == LANES - 1, lane == 0
-    north_edge, south_edge = sub == TILE - 1, sub == 0
     high = ny // TILE
 
     def spot(r, t):
         return slice(t * ny + r * TILE, t * ny + (r + 1) * TILE)
 
     def advance(load, keep, store):
-        known = {}
-
-        def turned(r, t, by, axis):
-            key = (r, t, by, axis)
-            if key not in known:
-                known[key] = pltpu.roll(load(r, t), by, axis)
-            return known[key]
-
-        def beyond(inside, r, t, by, axis, here):
-            return turned(r, t, by, axis) if inside else here
-
         for r in range(high):
-            for t in range(tiles):
-                f = load(r, t)
-                east = jnp.where(
-                    east_edge,
-                    beyond(t + 1 < tiles, r, t + 1, LANES - 1, 1, f),
-                    turned(r, t, LANES - 1, 1),
-                )
-                west = jnp.where(
-                    west_edge, beyond(t > 0, r, t - 1, 1, 1, f), turned(r, t, 1, 1)
-                )
-                north = jnp.where(
-                    north_edge,
-                    beyond(r + 1 < high, r + 1, t, TILE - 1, 0, f),
-                    turned(r, t, TILE - 1, 0),
-                )
-                south = jnp.where(
-                    south_edge, beyond(r > 0, r - 1, t, 1, 0, f), turned(r, t, 1, 0)
-                )
+            row = TILE + r * TILE
+            centre = [load(t, row) for t in range(tiles)]
+            ahead = [pltpu.roll(f, LANES - 1, 1) for f in centre]
+            behind = [pltpu.roll(f, 1, 1) for f in centre]
+            for t, f in enumerate(centre):
+                east = jnp.where(east_edge, ahead[t + 1] if t + 1 < tiles else f, ahead[t])
+                west = jnp.where(west_edge, behind[t - 1] if t else f, behind[t])
                 at = spot(r, t)
                 store(
                     r,
                     t,
                     (keep * f + weights[0, at, :] * east)
-                    + (weights[1, at, :] * west + weights[2, at, :] * north)
-                    + weights[3, at, :] * south,
+                    + (weights[1, at, :] * west + weights[2, at, :] * load(t, row + 1))
+                    + weights[3, at, :] * load(t, row - 1),
                 )
 
     for (start, count, whole), blocks in zip(parts, outs):
@@ -168,16 +151,25 @@
             for m in range(mem_dev):
                 level = slab * mem_dev + m
 
-                def first(r, t):
-                    return x_buf[
-                        slab, m, r * TILE : (r + 1) * TILE, t * LANES : (t + 1) * LANES
+                for t in range(tiles):
+                    x_buf[slab, m, t, TILE - 1 : TILE, :] = x_buf[slab, m, t, TILE : TILE + 1, :]
+                    x_buf[slab, m, t, TILE + ny : TILE + ny + 1, :] = x_buf[
+                        slab, m, t, TILE + ny - 1 : TILE + ny, :
                     ]
 
-                def later(r, t):
-                    return half[spot(r, t), :]
+                def first(t, row):
+                    return x_buf[slab, m, t, row : row + TILE, :]
+
+                def later(t, row):
+                    return half[m, t, row : row + TILE, :]
 
                 def between(r, t, value):
-                    half[spot(r, t), :] = value
+                    row = TILE + r * TILE
+                    half[m, t, row : row + TILE, :] = value
+                    if r == 0:
+                        half[m, t, TILE - 1 : TILE, :] = value[0:1, :]
+                    if r == high - 1:
+                        half[m, t, TILE + ny : TILE + ny + 1, :] = value[TILE - 1 : TILE, :]
 
                 def final(r, t, value):
                     field[level, spot(r, t), :] = value
@@ -233,17 +225,17 @@
         out_specs=[VMEM for group in shapes for _ in group],
         out_shape=[shape for group in shapes for shape in group],
         scratch_shapes=[
-            pltpu.VMEM((slab_dev, mem_dev, ny, nx), jnp.float32),
+            pltpu.VMEM((slab_dev, mem_dev, nx // LANES, ny + 2 * TILE, LANES), jnp.float32),
             pltpu.VMEM(cv.shape, jnp.float32),
             pltpu.VMEM(ch.shape, jnp.float32),
             pltpu.SMEM(cells.shape, jnp.int32),
             pltpu.SMEM(slabs.shape, jnp.int32),
             pltpu.SMEM(spread.shape, jnp.float32),
             pltpu.VMEM((slab_dev * mem_dev, ny * nx // LANES, LANES), jnp.float32),
-            pltpu.VMEM((ny * nx // LANES, LANES), jnp.float32),
+            pltpu.VMEM((mem_dev, nx // LANES, ny + 2 * TILE, LANES), jnp.float32),
             pltpu.VMEM((4, ny * nx // LANES, LANES), jnp.float32),
             pltpu.VMEM((mem_dev, cells.size, LANES), jnp.float32),
-            pltpu.SemaphoreType.DMA((3, slab_dev)),
+            pltpu.SemaphoreType.DMA((2 + nx // LANES, slab_dev)),
             pltpu.SemaphoreType.DMA((3,)),
         ],
         cost_estimate=cost(60 * x.size, 4 * (2 * x.size + 2 * cv.size)),
@@ -471,42 +463,54 @@
     )(lists, *tables, loc, *xs)
 
 
-def assemble_kernel(n, count, *refs):
-    out_ref, turn = refs[-2], refs[-1]
+def assemble_kernel(n, start, count, *refs):
+    out_ref, stage, turn, sem = refs[-4:]
     blocks = blocks_in(refs[:n], n, False)
     mem_dev, _, ny, nx = out_ref.shape
     block = ny // n
     tiles = nx // LANES
     depth = block * tiles
-    slab = pl.program_id(0)
-    for m in range(mem_dev):
-        at = pl.multiple_of((m * count + slab) * depth, TILE)
-        for t in range(tiles):
-            lanes = slice(t * LANES, (t + 1) * LANES)
-            lines = pl.ds(at + t * block, block)
-            for j, (ref, d) in enumerate(blocks):
-                if block % TILE == 0:
-                    row = pl.multiple_of(d * block, block)
-                    out_ref[m, 0, pl.ds(row, block), lanes] = ref[lines, :]
-                else:
-                    turn[pl.ds(j * block, block), :] = ref[lines, :]
-            if block % TILE:
-                for d, (_, j) in enumerate(blocks):
-                    out_ref[m, 0, d * block : (d + 1) * block, lanes] = turn[
-                        pl.ds(j * block, block), :
-                    ]
+    copies = []
+    for slab in range(count):
+        for m in range(mem_dev):
+            at = (m * count + slab) * depth
+            for t in range(tiles):
+                lanes = slice(t * LANES, (t + 1) * LANES)
+                lines = slice(at + t * block, at + (t + 1) * block)
+                for j, (ref, d) in enumerate(blocks):
+                    if block % TILE == 0:
+                        row = pl.multiple_of(d * block, block)
+                        stage[m, slab, pl.ds(row, block), lanes] = ref[lines, :]
+                    else:
+                        turn[j * block : (j + 1) * block, :] = ref[lines, :]
+                if block % TILE:
+                    for d, (_, j) in enumerate(blocks):
+                        stage[m, slab, d * block : (d + 1) * block, lanes] = turn[
+                            pl.ds(j * block, block), :
+                        ]
+        copies.append(
+            pltpu.make_async_copy(
+                stage.at[:, slab], out_ref.at[:, start + slab], sem.at[slab]
+            )
+        )
+        copies[-1].start()
+    for copy in copies:
+        copy.wait()
 
 
 def assemble(n, start, count, recv, shape, before):
     mem_dev, _, ny, nx = shape
     extra = [] if before is None else [before]
     return pl.pallas_call(
-        functools.partial(assemble_kernel, n, count),
-        grid=(count,),
+        functools.partial(assemble_kernel, n, start, count),
         in_specs=[VMEM] * n + [pl.BlockSpec(memory_space=pl.ANY)] * len(extra),
-        out_specs=pl.BlockSpec((mem_dev, 1, ny, nx), lambda s: (0, start + s, 0, 0)),
+        out_specs=pl.BlockSpec(memory_space=pl.ANY),
         out_shape=jax.ShapeDtypeStruct(shape, jnp.float32),
-        scratch_shapes=[pltpu.VMEM((ny, LANES), jnp.float32)],
+        scratch_shapes=[
+            pltpu.VMEM((mem_dev, count, ny, nx), jnp.float32),
+            pltpu.VMEM((ny, LANES), jnp.float32),
+            pltpu.SemaphoreType.DMA((count,)),
+        ],
         input_output_aliases={} if before is None else {n: 0},
         cost_estimate=cost(0, 8 * n * recv[0].size),
         compiler_params=params(),
@@ -514,15 +518,16 @@
     )(*recv, *extra)
 
 
-def order_of(n):
-    return list(range(n // 2, n)) + list(range(n // 2 - 1, 0, -1))
-
-
-def exchange(blocks, n, whole):
+def order_of(n, near_first=False):
+    far, near = list(range(n // 2, n)), list(range(n // 2 - 1, 0, -1))
+    return near + far if near_first else far + near
+
+
+def exchange(blocks, n, whole, near_first=False):
     if whole:
         return [lax.all_to_all(blocks[0], "mem", split_axis=0, concat_axis=0, tiled=True)]
     got = {}
-    for j in order_of(n):
+    for j in order_of(n, near_first):
         got[j] = lax.ppermute(blocks[j], "mem", [(i, i ^ j) for i in range(n)])
     return blocks[:1] + [got[j] for j in range(1, n)]
 
@@ -551,7 +556,7 @@
             tables, new = filter_plan(mem_dev, count, places, tiles, state)
         else:
             new = settle(n, mem_dev, count, whole, places, tables, state)
-        back = exchange(list(new), n, False)
+        back = exchange(list(new), n, False, near_first=c == 0)
         result = assemble(n, start, count, back, x.shape, result)
     return result
 

time: 92.8 us -> 92.4 us (level)
  no operation moved by 1% of the time
where the time goes in v8:
time: 92.4 us; the launch traced here: 92.2 us
  starting transfers between devices  48.9 us (53%)
  waiting for transfers between devices  24.5 us (27%)
  Pallas kernels  18.6 us (20%)
    ppermute x21, starting transfers between devices, exchange(): got[j] = lax.ppermute(blocks[j], 'mem', [(i, i ^ j) for i in range(n)])  39.7 us
    ppermute x21, waiting for transfers between devices, exchange(): got[j] = lax.ppermute(blocks[j], 'mem', [(i, i ^ j) for i in range(n)])  24.4 us
    all_to_all x1, starting transfers between devices, exchange(): lax.all_to_all(blocks[0], 'mem', split_axis=0, concat_axis=0, tiled=True)  7.47 us
    pallas_call x1, Pallas kernels, filter_plan(): pl.pallas_call(functools.partial(plan_kernel, n, mem_dev, count, len(seen...  5.69 us
    pallas_call x1, Pallas kernels, forecast(): pl.pallas_call(functools.partial(forecast_kernel, parts, n), in_specs=[pl...  4.46 us
    pallas_call x1, Pallas kernels, settle(): pl.pallas_call(functools.partial(settle_kernel, n, mem_dev, count, depth,...  3.86 us
    pallas_call x1, Pallas kernels, taper_tables(): pl.pallas_call(functools.partial(taper_kernel, nx, block), in_specs=[SMEM...  2.83 us
  transfers between devices with their start and end apart: 25, of which 9 were waited for; matrix products, arithmetic and copies ran while one was open for 0% of the time, Pallas kernels for 14%

profile of v8, /device:TPU:0, one launch (start us, length us, event | category | flops | bytes accessed | tf_op | source)
XLA Modules:
  0.0 92.2 jit_solution(12389426461432052832)
XLA Ops:
  0.0 4.5 %forecast.1 = (f32[136,128]{1,0:T(8,128)S(1)}, f32[136,128]{1,0:T(8,128)S(1)}, f32[136,128]{1,0:T(8,128)S(1)}, f32[136,128]{1,0:T(8,128)S(1)}, f32[136,128]{1,0:...) custom-call(s32[2,16]{1,0:T(2,128)} %cells_hbm.1, ...), custom_call_target="tpu_custom_call" | custom-call | flops 19660800 | bytes 3932160 | tf_op jit(solution)/shard_map/forecast/pallas_call | solution.py:222
  4.5 7.5 %all-to-all-start = ((f32[8,192,128]{2,1,0:T(8,128)}), f32[8,192,128]{2,1,0:T(8,128)S(1)}, u32[]{:S(2)}, u32[]{:S(2)}) async-start(f32[8,192,128]{2,1,0:T(8,128)} %get-tuple-element.50), calls=%async_computation | async-start | bytes 1572864 | tf_op jit(solution)/shard_map/all_to_all | solution.py:528
  12.0 2.0 %collective-permute-start = (f32[136,128]{1,0:T(8,128)S(1)}, f32[136,128]{1,0:T(8,128)S(1)}, u32[]{:S(2)}, u32[]{:S(2)}) collective-permute-start(f32[136,128]{1,0:T(8,128)S(1)} %get-tuple-element.41), channel_id=1, source_target_pairs={{0,4},{4,0},{8,12},{12,8},{16,20},{20,16},{24,28},{28,24},{1,5},{5... | collective-permute-start | bytes 208904 | tf_op jit(solution)/shard_map/ppermute | solution.py:531
  14.0 1.5 %collective-permute-start.1 = (f32[136,128]{1,0:T(8,128)S(1)}, f32[136,128]{1,0:T(8,128)S(1)}, u32[]{:S(2)}, u32[]{:S(2)}) collective-permute-start(f32[136,128]{1,0:T(8,128)S(1)} %get-tuple-element.42), channel_id=1, source_target_pairs={{0,8},{4,12},{8,0},{12,4},{16,24},{20,28},{24,16},{28,20},{1,9},{5... | collective-permute-start | bytes 208904 | tf_op jit(solution)/shard_map/ppermute | solution.py:531
  15.5 2.9 %collective-permute-start.3 = (f32[136,128]{1,0:T(8,128)S(1)}, f32[136,128]{1,0:T(8,128)S(1)}, u32[]{:S(2)}, u32[]{:S(2)}) collective-permute-start(f32[136,128]{1,0:T(8,128)S(1)} %get-tuple-element.44), channel_id=1, source_target_pairs={{0,16},{4,20},{8,24},{12,28},{16,0},{20,4},{24,8},{28,12},{1,17},{... | collective-permute-start | bytes 208904 | tf_op jit(solution)/shard_map/ppermute | solution.py:531
  20.8 2.4 %collective-permute-start.5 = (f32[136,128]{1,0:T(8,128)S(1)}, f32[136,128]{1,0:T(8,128)S(1)}, u32[]{:S(2)}, u32[]{:S(2)}) collective-permute-start(f32[136,128]{1,0:T(8,128)S(1)} %get-tuple-element.46), channel_id=1, source_target_pairs={{0,24},{4,28},{8,16},{12,20},{16,8},{20,12},{24,0},{28,4},{1,25},{... | collective-permute-start | bytes 208904 | tf_op jit(solution)/shard_map/ppermute | solution.py:531
  23.2 4.2 %collective-permute-done.1.refs_6_ = f32[136,128]{1,0:T(8,128)S(1)} collective-permute-done((f32[136,128]{1,0:T(8,128)S(1)}, f32[136,128]{1,0:T(8,128)S(1)}, u32[]{:S(2)}, u32[]{:S(2)}) %collective-permute-start.1) | collective-permute-done | bytes 69664 | tf_op jit(solution)/shard_map/ppermute | solution.py:531
  27.4 4.7 %collective-permute-start.6 = (f32[136,128]{1,0:T(8,128)S(1)}, f32[136,128]{1,0:T(8,128)S(1)}, u32[]{:S(2)}, u32[]{:S(2)}) collective-permute-start(f32[136,128]{1,0:T(8,128)S(1)} %get-tuple-element.47), channel_id=1, source_target_pairs={{0,28},{4,24},{8,20},{12,16},{16,12},{20,8},{24,4},{28,0},{1,29},{... | collective-permute-start | bytes 208904 | tf_op jit(solution)/shard_map/ppermute | solution.py:531
  32.1 8.8 %collective-permute-done.3.refs_8_ = f32[136,128]{1,0:T(8,128)S(1)} collective-permute-done((f32[136,128]{1,0:T(8,128)S(1)}, f32[136,128]{1,0:T(8,128)S(1)}, u32[]{:S(2)}, u32[]{:S(2)}) %collective-permute-start.3) | collective-permute-done | bytes 69664 | tf_op jit(solution)/shard_map/ppermute | solution.py:531
  40.9 2.0 %collective-permute-done.4.refs_9_ = f32[136,128]{1,0:T(8,128)S(1)} collective-permute-done((f32[136,128]{1,0:T(8,128)S(1)}, f32[136,128]{1,0:T(8,128)S(1)}, u32[]{:S(2)}, u32[]{:S(2)}) %collective-permute-start.4) | collective-permute-done | bytes 69664 | tf_op jit(solution)/shard_map/ppermute | solution.py:531
  43.0 1.6 %collective-permute-start.8 = (f32[16,128]{1,0:T(8,128)S(1)}, f32[16,128]{1,0:T(8,128)S(1)}, u32[]{:S(2)}, u32[]{:S(2)}) collective-permute-start(f32[16,128]{1,0:T(8,128)S(1)} %pad_maximum_fusion.refs_0_), channel_id=1, source_target_pairs={{0,2},{1,3},{2,0},{3,1},{4,6},{5,7},{6,4},{7,5},{8,10},{9,11},{10,... | collective-permute-start | bytes 24584 | tf_op jit(solution)/shard_map/ppermute | solution.py:549
  44.7 2.8 %taper_tables.1 = (f32[33,32,128]{2,1,0:T(8,128)S(1)}, f32[32,128]{1,0:T(8,128)S(1)}, f32[32,8,128]{2,1,0:T(8,128)S(1)}, s32[8,128]{1,0:T(8,128)S(1)}) custom-call(s32[2,16]{1,0:T(2,128)S(1)} %copy-done, f32[2,16]{1,0:T(2,128)S(1)} %copy-done.1, f32[2,16]{1,0:T(2,128)S(1)} %copy-done.2), custom_call_target="tpu_custom_call" | custom-call | flops 7864320 | bytes 524288 | tf_op jit(solution)/shard_map/taper_tables/pallas_call | solution.py:311
  47.7 5.7 %filter_plan.1 = (f32[33,24,128]{2,1,0:T(8,128)S(1)}, f32[33,24,128]{2,1,0:T(8,128)S(1)}, f32[128,128]{1,0:T(8,128)S(1)}, f32[128,128]{1,0:T(8,128)S(1)}, f32[12...) custom-call(f32[33,32,128]{2,1,0:T(8,128)S(1)} %get-tuple-element.37, ...), custom_call_target="tpu_custom_call" | custom-call | flops 20000000 | bytes 1048576 | tf_op jit(solution)/shard_map/filter_plan/pallas_call | solution.py:426
  54.4 2.2 %collective-permute-start.18 = (f32[128,128]{1,0:T(8,128)S(1)}, f32[128,128]{1,0:T(8,128)S(1)}, u32[]{:S(2)}, u32[]{:S(2)}) collective-permute-start(f32[128,128]{1,0:T(8,128)S(1)} %get-tuple-element.61), channel_id=1, source_target_pairs={{0,8},{4,12},{8,0},{12,4},{16,24},{20,28},{24,16},{28,20},{1,9},{5... | collective-permute-start | bytes 196616 | tf_op jit(solution)/shard_map/ppermute | solution.py:531
  57.4 2.2 %collective-permute-start.20 = (f32[128,128]{1,0:T(8,128)S(1)}, f32[128,128]{1,0:T(8,128)S(1)}, u32[]{:S(2)}, u32[]{:S(2)}) collective-permute-start(f32[128,128]{1,0:T(8,128)S(1)} %get-tuple-element.63), channel_id=1, source_target_pairs={{0,16},{4,20},{8,24},{12,28},{16,0},{20,4},{24,8},{28,12},{1,17},{... | collective-permute-start | bytes 196616 | tf_op jit(solution)/shard_map/ppermute | solution.py:531
  59.6 3.9 %settle.1 = (f32[192,128]{1,0:T(8,128)S(1)}, f32[192,128]{1,0:T(8,128)S(1)}, f32[192,128]{1,0:T(8,128)S(1)}, f32[192,128]{1,0:T(8,128)S(1)}, f32[192,128]{1,0:T(...) custom-call(s32[8,128]{1,0:T(8,128)S(1)} %get-tuple-element.36.lists_ref, ...), custom_call_target="tpu_custom_call" | custom-call | flops 25952256 | bytes 1572864 | tf_op jit(solution)/shard_map/settle/pallas_call | solution.py:454
  64.1 3.6 %collective-permute-start.21 = (f32[128,128]{1,0:T(8,128)S(1)}, f32[128,128]{1,0:T(8,128)S(1)}, u32[]{:S(2)}, u32[]{:S(2)}) collective-permute-start(f32[128,128]{1,0:T(8,128)S(1)} %get-tuple-element.64), channel_id=1, source_target_pairs={{0,20},{4,16},{8,28},{12,24},{16,4},{20,0},{24,12},{28,8},{1,21},{... | collective-permute-start | bytes 196616 | tf_op jit(solution)/shard_map/ppermute | solution.py:531
  67.7 1.6 %collective-permute-start.22 = (f32[128,128]{1,0:T(8,128)S(1)}, f32[128,128]{1,0:T(8,128)S(1)}, u32[]{:S(2)}, u32[]{:S(2)}) collective-permute-start(f32[128,128]{1,0:T(8,128)S(1)} %get-tuple-element.65), channel_id=1, source_target_pairs={{0,24},{4,28},{8,16},{12,20},{16,8},{20,12},{24,0},{28,4},{1,25},{... | collective-permute-start | bytes 196616 | tf_op jit(solution)/shard_map/ppermute | solution.py:531
  69.4 2.3 %collective-permute-start.23 = (f32[128,128]{1,0:T(8,128)S(1)}, f32[128,128]{1,0:T(8,128)S(1)}, u32[]{:S(2)}, u32[]{:S(2)}) collective-permute-start(f32[128,128]{1,0:T(8,128)S(1)} %get-tuple-element.66), channel_id=1, source_target_pairs={{0,28},{4,24},{8,20},{12,16},{16,12},{20,8},{24,4},{28,0},{1,29},{... | collective-permute-start | bytes 196616 | tf_op jit(solution)/shard_map/ppermute | solution.py:531
  74.6 3.5 %collective-permute-start.13 = (f32[192,128]{1,0:T(8,128)S(1)}, f32[192,128]{1,0:T(8,128)S(1)}, u32[]{:S(2)}, u32[]{:S(2)}) collective-permute-start(f32[192,128]{1,0:T(8,128)S(1)} %get-tuple-element.55), channel_id=1, source_target_pairs={{0,16},{4,20},{8,24},{12,28},{16,0},{20,4},{24,8},{28,12},{1,17},{... | collective-permute-start | bytes 294920 | tf_op jit(solution)/shard_map/ppermute | solution.py:531
  78.1 2.8 %collective-permute-start.14 = (f32[192,128]{1,0:T(8,128)S(1)}, f32[192,128]{1,0:T(8,128)S(1)}, u32[]{:S(2)}, u32[]{:S(2)}) collective-permute-start(f32[192,128]{1,0:T(8,128)S(1)} %get-tuple-element.56), channel_id=1, source_target_pairs={{0,20},{4,16},{8,28},{12,24},{16,4},{20,0},{24,12},{28,8},{1,21},{... | collective-permute-start | bytes 294920 | tf_op jit(solution)/shard_map/ppermute | solution.py:531
  80.9 1.9 %collective-permute-start.15 = (f32[192,128]{1,0:T(8,128)S(1)}, f32[192,128]{1,0:T(8,128)S(1)}, u32[]{:S(2)}, u32[]{:S(2)}) collective-permute-start(f32[192,128]{1,0:T(8,128)S(1)} %get-tuple-element.57), channel_id=1, source_target_pairs={{0,24},{4,28},{8,16},{12,20},{16,8},{20,12},{24,0},{28,4},{1,25},{... | collective-permute-start | bytes 294920 | tf_op jit(solution)/shard_map/ppermute | solution.py:531
  85.1 4.0 %collective-permute-done.13.refs_4_ = f32[192,128]{1,0:T(8,128)S(1)} collective-permute-done((f32[192,128]{1,0:T(8,128)S(1)}, f32[192,128]{1,0:T(8,128)S(1)}, u32[]{:S(2)}, u32[]{:S(2)}) %collective-permute-start.13) | collective-permute-done | bytes 98336 | tf_op jit(solution)/shard_map/ppermute | solution.py:531
  89.1 2.1 %collective-permute-done.14.refs_5_ = f32[192,128]{1,0:T(8,128)S(1)} collective-permute-done((f32[192,128]{1,0:T(8,128)S(1)}, f32[192,128]{1,0:T(8,128)S(1)}, u32[]{:S(2)}, u32[]{:S(2)}) %collective-permute-start.14) | collective-permute-done | bytes 98336 | tf_op jit(solution)/shard_map/ppermute | solution.py:531
  (41 shorter events, 11.4 us)
Async XLA Ops:
  4.5 55.1 %all-to-all-start = ((f32[8,192,128]{2,1,0:T(8,128)}), f32[8,192,128]{2,1,0:T(8,128)S(1)}, u32[]{:S(2)}, u32[]{:S(2)}) async-start(f32[8,192,128]{2,1,0:T(8,128)} %get-tuple-element.50), calls=%async_computation | async-start | bytes 1572864 | tf_op jit(solution)/shard_map/all_to_all | solution.py:528
  12.0 8.8 %collective-permute-start = (f32[136,128]{1,0:T(8,128)S(1)}, f32[136,128]{1,0:T(8,128)S(1)}, u32[]{:S(2)}, u32[]{:S(2)}) collective-permute-start(f32[136,128]{1,0:T(8,128)S(1)} %get-tuple-element.41), channel_id=1, source_target_pairs={{0,4},{4,0},{8,12},{12,8},{16,20},{20,16},{24,28},{28,24},{1,5},{5... | collective-permute-start | bytes 208904 | tf_op jit(solution)/shard_map/ppermute | solution.py:531
  14.0 13.4 %collective-permute-start.1 = (f32[136,128]{1,0:T(8,128)S(1)}, f32[136,128]{1,0:T(8,128)S(1)}, u32[]{:S(2)}, u32[]{:S(2)}) collective-permute-start(f32[136,128]{1,0:T(8,128)S(1)} %get-tuple-element.42), channel_id=1, source_target_pairs={{0,8},{4,12},{8,0},{12,4},{16,24},{20,28},{24,16},{28,20},{1,9},{5... | collective-permute-start | bytes 208904 | tf_op jit(solution)/shard_map/ppermute | solution.py:531
  15.5 16.7 %collective-permute-start.2 = (f32[136,128]{1,0:T(8,128)S(1)}, f32[136,128]{1,0:T(8,128)S(1)}, u32[]{:S(2)}, u32[]{:S(2)}) collective-permute-start(f32[136,128]{1,0:T(8,128)S(1)} %get-tuple-element.43), channel_id=1, source_target_pairs={{0,12},{4,8},{8,4},{12,0},{16,28},{20,24},{24,20},{28,16},{1,13},{... | collective-permute-start | bytes 208904 | tf_op jit(solution)/shard_map/ppermute | solution.py:531
  15.5 25.5 %collective-permute-start.3 = (f32[136,128]{1,0:T(8,128)S(1)}, f32[136,128]{1,0:T(8,128)S(1)}, u32[]{:S(2)}, u32[]{:S(2)}) collective-permute-start(f32[136,128]{1,0:T(8,128)S(1)} %get-tuple-element.44), channel_id=1, source_target_pairs={{0,16},{4,20},{8,24},{12,28},{16,0},{20,4},{24,8},{28,12},{1,17},{... | collective-permute-start | bytes 208904 | tf_op jit(solution)/shard_map/ppermute | solution.py:531
  18.4 24.5 %collective-permute-start.4 = (f32[136,128]{1,0:T(8,128)S(1)}, f32[136,128]{1,0:T(8,128)S(1)}, u32[]{:S(2)}, u32[]{:S(2)}) collective-permute-start(f32[136,128]{1,0:T(8,128)S(1)} %get-tuple-element.45), channel_id=1, source_target_pairs={{0,20},{4,16},{8,28},{12,24},{16,4},{20,0},{24,12},{28,8},{1,21},{... | collective-permute-start | bytes 208904 | tf_op jit(solution)/shard_map/ppermute | solution.py:531
  20.8 22.1 %collective-permute-start.5 = (f32[136,128]{1,0:T(8,128)S(1)}, f32[136,128]{1,0:T(8,128)S(1)}, u32[]{:S(2)}, u32[]{:S(2)}) collective-permute-start(f32[136,128]{1,0:T(8,128)S(1)} %get-tuple-element.46), channel_id=1, source_target_pairs={{0,24},{4,28},{8,16},{12,20},{16,8},{20,12},{24,0},{28,4},{1,25},{... | collective-permute-start | bytes 208904 | tf_op jit(solution)/shard_map/ppermute | solution.py:531
  27.4 15.5 %collective-permute-start.6 = (f32[136,128]{1,0:T(8,128)S(1)}, f32[136,128]{1,0:T(8,128)S(1)}, u32[]{:S(2)}, u32[]{:S(2)}) collective-permute-start(f32[136,128]{1,0:T(8,128)S(1)} %get-tuple-element.47), channel_id=1, source_target_pairs={{0,28},{4,24},{8,20},{12,16},{16,12},{20,8},{24,4},{28,0},{1,29},{... | collective-permute-start | bytes 208904 | tf_op jit(solution)/shard_map/ppermute | solution.py:531
  43.0 4.6 %collective-permute-start.9 = (f32[16,128]{1,0:T(8,128)S(1)}, f32[16,128]{1,0:T(8,128)S(1)}, u32[]{:S(2)}, u32[]{:S(2)}) collective-permute-start(f32[16,128]{1,0:T(8,128)S(1)} %pad_maximum_fusion.refs_0_), channel_id=1, source_target_pairs={{0,3},{1,0},{2,1},{3,2},{4,7},{5,4},{6,5},{7,6},{8,11},{9,8},{10,9... | collective-permute-start | bytes 24584 | tf_op jit(solution)/shard_map/ppermute | solution.py:549
  43.0 4.6 %collective-permute-start.8 = (f32[16,128]{1,0:T(8,128)S(1)}, f32[16,128]{1,0:T(8,128)S(1)}, u32[]{:S(2)}, u32[]{:S(2)}) collective-permute-start(f32[16,128]{1,0:T(8,128)S(1)} %pad_maximum_fusion.refs_0_), channel_id=1, source_target_pairs={{0,2},{1,3},{2,0},{3,1},{4,6},{5,7},{6,4},{7,5},{8,10},{9,11},{10,... | collective-permute-start | bytes 24584 | tf_op jit(solution)/shard_map/ppermute | solution.py:549
  53.3 10.3 %collective-permute-start.17 = (f32[128,128]{1,0:T(8,128)S(1)}, f32[128,128]{1,0:T(8,128)S(1)}, u32[]{:S(2)}, u32[]{:S(2)}) collective-permute-start(f32[128,128]{1,0:T(8,128)S(1)} %get-tuple-element.60), channel_id=1, source_target_pairs={{0,4},{4,0},{8,12},{12,8},{16,20},{20,16},{24,28},{28,24},{1,5},{5... | collective-permute-start | bytes 196616 | tf_op jit(solution)/shard_map/ppermute | solution.py:531
  54.4 9.7 %collective-permute-start.18 = (f32[128,128]{1,0:T(8,128)S(1)}, f32[128,128]{1,0:T(8,128)S(1)}, u32[]{:S(2)}, u32[]{:S(2)}) collective-permute-start(f32[128,128]{1,0:T(8,128)S(1)} %get-tuple-element.61), channel_id=1, source_target_pairs={{0,8},{4,12},{8,0},{12,4},{16,24},{20,28},{24,16},{28,20},{1,9},{5... | collective-permute-start | bytes 196616 | tf_op jit(solution)/shard_map/ppermute | solution.py:531
  56.6 11.2 %collective-permute-start.19 = (f32[128,128]{1,0:T(8,128)S(1)}, f32[128,128]{1,0:T(8,128)S(1)}, u32[]{:S(2)}, u32[]{:S(2)}) collective-permute-start(f32[128,128]{1,0:T(8,128)S(1)} %get-tuple-element.62), channel_id=1, source_target_pairs={{0,12},{4,8},{8,4},{12,0},{16,28},{20,24},{24,20},{28,16},{1,13},{... | collective-permute-start | bytes 196616 | tf_op jit(solution)/shard_map/ppermute | solution.py:531
  57.4 12.0 %collective-permute-start.20 = (f32[128,128]{1,0:T(8,128)S(1)}, f32[128,128]{1,0:T(8,128)S(1)}, u32[]{:S(2)}, u32[]{:S(2)}) collective-permute-start(f32[128,128]{1,0:T(8,128)S(1)} %get-tuple-element.63), channel_id=1, source_target_pairs={{0,16},{4,20},{8,24},{12,28},{16,0},{20,4},{24,8},{28,12},{1,17},{... | collective-permute-start | bytes 196616 | tf_op jit(solution)/shard_map/ppermute | solution.py:531
  63.5 17.4 %collective-permute-start.10 = (f32[192,128]{1,0:T(8,128)S(1)}, f32[192,128]{1,0:T(8,128)S(1)}, u32[]{:S(2)}, u32[]{:S(2)}) collective-permute-start(f32[192,128]{1,0:T(8,128)S(1)} %get-tuple-element.52), channel_id=1, source_target_pairs={{0,4},{4,0},{8,12},{12,8},{16,20},{20,16},{24,28},{28,24},{1,5},{5... | collective-permute-start | bytes 294920 | tf_op jit(solution)/shard_map/ppermute | solution.py:531
  63.6 19.2 %collective-permute-start.11 = (f32[192,128]{1,0:T(8,128)S(1)}, f32[192,128]{1,0:T(8,128)S(1)}, u32[]{:S(2)}, u32[]{:S(2)}) collective-permute-start(f32[192,128]{1,0:T(8,128)S(1)} %get-tuple-element.53), channel_id=1, source_target_pairs={{0,8},{4,12},{8,0},{12,4},{16,24},{20,28},{24,16},{28,20},{1,9},{5... | collective-permute-start | bytes 294920 | tf_op jit(solution)/shard_map/ppermute | solution.py:531
  64.1 8.8 %collective-permute-start.21 = (f32[128,128]{1,0:T(8,128)S(1)}, f32[128,128]{1,0:T(8,128)S(1)}, u32[]{:S(2)}, u32[]{:S(2)}) collective-permute-start(f32[128,128]{1,0:T(8,128)S(1)} %get-tuple-element.64), channel_id=1, source_target_pairs={{0,20},{4,16},{8,28},{12,24},{16,4},{20,0},{24,12},{28,8},{1,21},{... | collective-permute-start | bytes 196616 | tf_op jit(solution)/shard_map/ppermute | solution.py:531
  67.7 6.8 %collective-permute-start.22 = (f32[128,128]{1,0:T(8,128)S(1)}, f32[128,128]{1,0:T(8,128)S(1)}, u32[]{:S(2)}, u32[]{:S(2)}) collective-permute-start(f32[128,128]{1,0:T(8,128)S(1)} %get-tuple-element.65), channel_id=1, source_target_pairs={{0,24},{4,28},{8,16},{12,20},{16,8},{20,12},{24,0},{28,4},{1,25},{... | collective-permute-start | bytes 196616 | tf_op jit(solution)/shard_map/ppermute | solution.py:531
  69.4 8.7 %collective-permute-start.23 = (f32[128,128]{1,0:T(8,128)S(1)}, f32[128,128]{1,0:T(8,128)S(1)}, u32[]{:S(2)}, u32[]{:S(2)}) collective-permute-start(f32[128,128]{1,0:T(8,128)S(1)} %get-tuple-element.66), channel_id=1, source_target_pairs={{0,28},{4,24},{8,20},{12,16},{16,12},{20,8},{24,4},{28,0},{1,29},{... | collective-permute-start | bytes 196616 | tf_op jit(solution)/shard_map/ppermute | solution.py:531
  72.9 12.2 %collective-permute-start.12 = (f32[192,128]{1,0:T(8,128)S(1)}, f32[192,128]{1,0:T(8,128)S(1)}, u32[]{:S(2)}, u32[]{:S(2)}) collective-permute-start(f32[192,128]{1,0:T(8,128)S(1)} %get-tuple-element.54), channel_id=1, source_target_pairs={{0,12},{4,8},{8,4},{12,0},{16,28},{20,24},{24,20},{28,16},{1,13},{... | collective-permute-start | bytes 294920 | tf_op jit(solution)/shard_map/ppermute | solution.py:531
  74.6 14.6 %collective-permute-start.13 = (f32[192,128]{1,0:T(8,128)S(1)}, f32[192,128]{1,0:T(8,128)S(1)}, u32[]{:S(2)}, u32[]{:S(2)}) collective-permute-start(f32[192,128]{1,0:T(8,128)S(1)} %get-tuple-element.55), channel_id=1, source_target_pairs={{0,16},{4,20},{8,24},{12,28},{16,0},{20,4},{24,8},{28,12},{1,17},{... | collective-permute-start | bytes 294920 | tf_op jit(solution)/shard_map/ppermute | solution.py:531
  78.1 13.1 %collective-permute-start.14 = (f32[192,128]{1,0:T(8,128)S(1)}, f32[192,128]{1,0:T(8,128)S(1)}, u32[]{:S(2)}, u32[]{:S(2)}) collective-permute-start(f32[192,128]{1,0:T(8,128)S(1)} %get-tuple-element.56), channel_id=1, source_target_pairs={{0,20},{4,16},{8,28},{12,24},{16,4},{20,0},{24,12},{28,8},{1,21},{... | collective-permute-start | bytes 294920 | tf_op jit(solution)/shard_map/ppermute | solution.py:531
  80.9 10.3 %collective-permute-start.15 = (f32[192,128]{1,0:T(8,128)S(1)}, f32[192,128]{1,0:T(8,128)S(1)}, u32[]{:S(2)}, u32[]{:S(2)}) collective-permute-start(f32[192,128]{1,0:T(8,128)S(1)} %get-tuple-element.57), channel_id=1, source_target_pairs={{0,24},{4,28},{8,16},{12,20},{16,8},{20,12},{24,0},{28,4},{1,25},{... | collective-permute-start | bytes 294920 | tf_op jit(solution)/shard_map/ppermute | solution.py:531
  82.8 8.4 %collective-permute-start.16 = (f32[192,128]{1,0:T(8,128)S(1)}, f32[192,128]{1,0:T(8,128)S(1)}, u32[]{:S(2)}, u32[]{:S(2)}) collective-permute-start(f32[192,128]{1,0:T(8,128)S(1)} %get-tuple-element.58), channel_id=1, source_target_pairs={{0,28},{4,24},{8,20},{12,16},{16,12},{20,8},{24,4},{28,0},{1,29},{... | collective-permute-start | bytes 294920 | tf_op jit(solution)/shard_map/ppermute | solution.py:531
  (4 other events, 123.8 us)

commit v9 on v8

--- a/solution.py
+++ b/solution.py
@@ -74,7 +74,8 @@
         width = 1 if whole else n
         outs.append(blocks_in(rest[:width], n, whole))
         rest = rest[width:]
-    x_buf, cv_buf, ch_buf, cells, slabs, spread, field, half, weights, picks, sem, small = rest
+    x_buf, cv_buf, ch_buf, cells, slabs, spread, spots, field, half, weights, picks = rest[:-2]
+    sem, small = rest[-2:]
     slab_dev, mem_dev, tiles = x_buf.shape[:3]
     ny, nx = x_buf.shape[3] - 2 * TILE, tiles * LANES
     block = ny // n
@@ -106,6 +107,14 @@
             copy.start()
     for copy in lists:
         copy.wait()
+    for k in range(total):
+        row, col = row_col(place(cells, k), nx)
+        across, wanted = row_col(col, LANES)
+        off = place(slabs, k) - lax.axis_index("lev") * slab_dev
+        inside = (off >= 0) & (off < slab_dev)
+        spots[0, k] = jnp.where(inside, off, 0) * mem_dev
+        spots[1, k] = across * ny + row
+        spots[2, k] = jnp.where(inside, wanted, LANES)
     sub = lax.broadcasted_iota(jnp.int32, (TILE, LANES), 0)
     lane = lax.broadcasted_iota(jnp.int32, (TILE, LANES), 1)
     east_edge, west_edge = lane == LANES - 1, lane == 0
@@ -117,20 +126,28 @@
     def advance(load, keep, store):
         for r in range(high):
             row = TILE + r * TILE
-            centre = [load(t, row) for t in range(tiles)]
-            ahead = [pltpu.roll(f, LANES - 1, 1) for f in centre]
-            behind = [pltpu.roll(f, 1, 1) for f in centre]
-            for t, f in enumerate(centre):
-                east = jnp.where(east_edge, ahead[t + 1] if t + 1 < tiles else f, ahead[t])
-                west = jnp.where(west_edge, behind[t - 1] if t else f, behind[t])
+            ahead, behind = {}, {}
+            for m in range(mem_dev):
+                for t in range(tiles):
+                    f = load(m, t, row)
+                    ahead[m, t] = pltpu.roll(f, LANES - 1, 1)
+                    behind[m, t] = pltpu.roll(f, 1, 1)
+            for t in range(tiles):
                 at = spot(r, t)
-                store(
-                    r,
-                    t,
-                    (keep * f + weights[0, at, :] * east)
-                    + (weights[1, at, :] * west + weights[2, at, :] * load(t, row + 1))
-                    + weights[3, at, :] * load(t, row - 1),
-                )
+                east_w, west_w = weights[0, at, :], weights[1, at, :]
+                north_w, south_w = weights[2, at, :], weights[3, at, :]
+                for m in range(mem_dev):
+                    f = load(m, t, row)
+                    east = jnp.where(east_edge, ahead.get((m, t + 1), f), ahead[m, t])
+                    west = jnp.where(west_edge, behind.get((m, t - 1), f), behind[m, t])
+                    store(
+                        m,
+                        r,
+                        t,
+                        (keep * f + east_w * east)
+                        + (west_w * west + north_w * load(m, t, row + 1))
+                        + south_w * load(m, t, row - 1),
+                    )
 
     for (start, count, whole), blocks in zip(parts, outs):
 
@@ -149,56 +166,50 @@
                     weights[2, spot(r, t), :] = diffuse - half_h
                     weights[3, spot(r, t), :] = diffuse + half_h
             for m in range(mem_dev):
-                level = slab * mem_dev + m
-
                 for t in range(tiles):
                     x_buf[slab, m, t, TILE - 1 : TILE, :] = x_buf[slab, m, t, TILE : TILE + 1, :]
                     x_buf[slab, m, t, TILE + ny : TILE + ny + 1, :] = x_buf[
                         slab, m, t, TILE + ny - 1 : TILE + ny, :
                     ]
 
-                def first(t, row):
-                    return x_buf[slab, m, t, row : row + TILE, :]
-
-                def later(t, row):
-                    return half[m, t, row : row + TILE, :]
-
-                def between(r, t, value):
-                    row = TILE + r * TILE
-                    half[m, t, row : row + TILE, :] = value
-                    if r == 0:
-                        half[m, t, TILE - 1 : TILE, :] = value[0:1, :]
-                    if r == high - 1:
-                        half[m, t, TILE + ny : TILE + ny + 1, :] = value[TILE - 1 : TILE, :]
-
-                def final(r, t, value):
-                    field[level, spot(r, t), :] = value
-
-                for step in range(STEPS):
-                    advance(
-                        later if step else first, keep, between if step < STEPS - 1 else final
-                    )
+            def first(m, t, row):
+                return x_buf[slab, m, t, row : row + TILE, :]
+
+            def later(m, t, row):
+                return half[m, t, row : row + TILE, :]
+
+            def between(m, r, t, value):
+                row = TILE + r * TILE
+                half[m, t, row : row + TILE, :] = value
+                if r == 0:
+                    half[m, t, TILE - 1 : TILE, :] = value[0:1, :]
+                if r == high - 1:
+                    half[m, t, TILE + ny : TILE + ny + 1, :] = value[TILE - 1 : TILE, :]
+
+            def final(m, r, t, value):
+                field[slab * mem_dev + m, spot(r, t), :] = value
+
+            for step in range(STEPS):
+                load, store = later if step else first, between if step < STEPS - 1 else final
+                advance(load, keep, store)
+            for m in range(mem_dev):
                 at = pl.multiple_of((m * count + s) * depth, TILE)
                 for ref, d in blocks:
                     for t in range(tiles):
                         row = pl.multiple_of(t * ny + d * block, block)
-                        ref[pl.ds(at + t * block, block), :] = field[level, pl.ds(row, block), :]
+                        ref[pl.ds(at + t * block, block), :] = field[
+                            slab * mem_dev + m, pl.ds(row, block), :
+                        ]
             return carry
 
         lax.fori_loop(0, count, one, 0)
 
-    lane = lax.broadcasted_iota(jnp.int32, (1, LANES), 1)
+    line_lane = lax.broadcasted_iota(jnp.int32, (1, LANES), 1)
     for k in range(total):
-        cell = place(cells, k)
-        row, col = row_col(cell, nx)
-        off = place(slabs, k) - lax.axis_index("lev") * slab_dev
-        inside = (off >= 0) & (off < slab_dev)
-        across, wanted = row_col(col, LANES)
-        wanted = jnp.where(inside, wanted, LANES)
-        off = jnp.where(inside, off, 0)
+        level, row, wanted = spots[0, k], spots[1, k], spots[2, k]
         for m in range(mem_dev):
-            line = field[off * mem_dev + m, pl.ds(across * ny + row, 1), :]
-            picks[m, pl.ds(k, 1), :] = jnp.where(lane == wanted, line, 0.0)
+            line = field[level + m, pl.ds(row, 1), :]
+            picks[m, pl.ds(k, 1), :] = jnp.where(line_lane == wanted, line, 0.0)
     diagonal = lax.broadcasted_iota(jnp.int32, (total, LANES), 0) == lax.broadcasted_iota(
         jnp.int32, (total, LANES), 1
     )
@@ -231,6 +242,7 @@
             pltpu.SMEM(cells.shape, jnp.int32),
             pltpu.SMEM(slabs.shape, jnp.int32),
             pltpu.SMEM(spread.shape, jnp.float32),
+            pltpu.SMEM((3, cells.size), jnp.int32),
             pltpu.VMEM((slab_dev * mem_dev, ny * nx // LANES, LANES), jnp.float32),
             pltpu.VMEM((mem_dev, nx // LANES, ny + 2 * TILE, LANES), jnp.float32),
             pltpu.VMEM((4, ny * nx // LANES, LANES), jnp.float32),
@@ -519,8 +531,10 @@
 
 
 def order_of(n, near_first=False):
-    far, near = list(range(n // 2, n)), list(range(n // 2 - 1, 0, -1))
-    return near + far if near_first else far + near
+    far, near = list(range(n // 2, n)), list(range(2, n // 2)) + [1]
+    if near_first:
+        return near + far
+    return [j for pair in zip(far, near) for j in pair] + far[len(near) :]
 
 
 def exchange(blocks, n, whole, near_first=False):

time: 92.4 us -> 92.2 us (level)
  no operation moved by 1% of the time
where the time goes in v9:
time: 92.2 us; the launch traced here: 92 us
  starting transfers between devices  48.9 us (53%)
  waiting for transfers between devices  24.5 us (27%)
  Pallas kernels  18.4 us (20%)
    ppermute x21, starting transfers between devices, exchange(): got[j] = lax.ppermute(blocks[j], 'mem', [(i, i ^ j) for i in range(n)])  39.7 us
    ppermute x21, waiting for transfers between devices, exchange(): got[j] = lax.ppermute(blocks[j], 'mem', [(i, i ^ j) for i in range(n)])  24.4 us
    all_to_all x1, starting transfers between devices, exchange(): lax.all_to_all(blocks[0], 'mem', split_axis=0, concat_axis=0, tiled=True)  7.45 us
    pallas_call x1, Pallas kernels, filter_plan(): pl.pallas_call(functools.partial(plan_kernel, n, mem_dev, count, len(seen...  5.69 us
    pallas_call x1, Pallas kernels, forecast(): pl.pallas_call(functools.partial(forecast_kernel, parts, n), in_specs=[pl...  4.25 us
    pallas_call x1, Pallas kernels, settle(): pl.pallas_call(functools.partial(settle_kernel, n, mem_dev, count, depth,...  3.86 us
    pallas_call x1, Pallas kernels, taper_tables(): pl.pallas_call(functools.partial(taper_kernel, nx, block), in_specs=[SMEM...  2.83 us
  transfers between devices with their start and end apart: 25, of which 9 were waited for; matrix products, arithmetic and copies ran while one was open for 0% of the time, Pallas kernels for 14%

profile of v9, /device:TPU:0, one launch (start us, length us, event | category | flops | bytes accessed | tf_op | source)
XLA Modules:
  0.0 92.0 jit_solution(5836910159814288263)
XLA Ops:
  0.0 4.3 %forecast.1 = (f32[136,128]{1,0:T(8,128)S(1)}, f32[136,128]{1,0:T(8,128)S(1)}, f32[136,128]{1,0:T(8,128)S(1)}, f32[136,128]{1,0:T(8,128)S(1)}, f32[136,128]{1,0:...) custom-call(s32[2,16]{1,0:T(2,128)} %cells_hbm.1, ...), custom_call_target="tpu_custom_call" | custom-call | flops 19660800 | bytes 3932160 | tf_op jit(solution)/shard_map/forecast/pallas_call | solution.py:233
  4.3 7.5 %all-to-all-start = ((f32[8,192,128]{2,1,0:T(8,128)}), f32[8,192,128]{2,1,0:T(8,128)S(1)}, u32[]{:S(2)}, u32[]{:S(2)}) async-start(f32[8,192,128]{2,1,0:T(8,128)} %get-tuple-element.50), calls=%async_computation | async-start | bytes 1572864 | tf_op jit(solution)/shard_map/all_to_all | solution.py:542
  11.7 2.0 %collective-permute-start = (f32[136,128]{1,0:T(8,128)S(1)}, f32[136,128]{1,0:T(8,128)S(1)}, u32[]{:S(2)}, u32[]{:S(2)}) collective-permute-start(f32[136,128]{1,0:T(8,128)S(1)} %get-tuple-element.41), channel_id=1, source_target_pairs={{0,4},{4,0},{8,12},{12,8},{16,20},{20,16},{24,28},{28,24},{1,5},{5... | collective-permute-start | bytes 208904 | tf_op jit(solution)/shard_map/ppermute | solution.py:545
  13.8 1.5 %collective-permute-start.1 = (f32[136,128]{1,0:T(8,128)S(1)}, f32[136,128]{1,0:T(8,128)S(1)}, u32[]{:S(2)}, u32[]{:S(2)}) collective-permute-start(f32[136,128]{1,0:T(8,128)S(1)} %get-tuple-element.42), channel_id=1, source_target_pairs={{0,8},{4,12},{8,0},{12,4},{16,24},{20,28},{24,16},{28,20},{1,9},{5... | collective-permute-start | bytes 208904 | tf_op jit(solution)/shard_map/ppermute | solution.py:545
  15.3 2.9 %collective-permute-start.3 = (f32[136,128]{1,0:T(8,128)S(1)}, f32[136,128]{1,0:T(8,128)S(1)}, u32[]{:S(2)}, u32[]{:S(2)}) collective-permute-start(f32[136,128]{1,0:T(8,128)S(1)} %get-tuple-element.44), channel_id=1, source_target_pairs={{0,16},{4,20},{8,24},{12,28},{16,0},{20,4},{24,8},{28,12},{1,17},{... | collective-permute-start | bytes 208904 | tf_op jit(solution)/shard_map/ppermute | solution.py:545
  20.6 2.4 %collective-permute-start.5 = (f32[136,128]{1,0:T(8,128)S(1)}, f32[136,128]{1,0:T(8,128)S(1)}, u32[]{:S(2)}, u32[]{:S(2)}) collective-permute-start(f32[136,128]{1,0:T(8,128)S(1)} %get-tuple-element.46), channel_id=1, source_target_pairs={{0,24},{4,28},{8,16},{12,20},{16,8},{20,12},{24,0},{28,4},{1,25},{... | collective-permute-start | bytes 208904 | tf_op jit(solution)/shard_map/ppermute | solution.py:545
  23.0 4.2 %collective-permute-done.1.refs_6_ = f32[136,128]{1,0:T(8,128)S(1)} collective-permute-done((f32[136,128]{1,0:T(8,128)S(1)}, f32[136,128]{1,0:T(8,128)S(1)}, u32[]{:S(2)}, u32[]{:S(2)}) %collective-permute-start.1) | collective-permute-done | bytes 69664 | tf_op jit(solution)/shard_map/ppermute | solution.py:545
  27.2 4.7 %collective-permute-start.6 = (f32[136,128]{1,0:T(8,128)S(1)}, f32[136,128]{1,0:T(8,128)S(1)}, u32[]{:S(2)}, u32[]{:S(2)}) collective-permute-start(f32[136,128]{1,0:T(8,128)S(1)} %get-tuple-element.47), channel_id=1, source_target_pairs={{0,28},{4,24},{8,20},{12,16},{16,12},{20,8},{24,4},{28,0},{1,29},{... | collective-permute-start | bytes 208904 | tf_op jit(solution)/shard_map/ppermute | solution.py:545
  31.9 8.8 %collective-permute-done.3.refs_8_ = f32[136,128]{1,0:T(8,128)S(1)} collective-permute-done((f32[136,128]{1,0:T(8,128)S(1)}, f32[136,128]{1,0:T(8,128)S(1)}, u32[]{:S(2)}, u32[]{:S(2)}) %collective-permute-start.3) | collective-permute-done | bytes 69664 | tf_op jit(solution)/shard_map/ppermute | solution.py:545
  40.7 2.0 %collective-permute-done.4.refs_9_ = f32[136,128]{1,0:T(8,128)S(1)} collective-permute-done((f32[136,128]{1,0:T(8,128)S(1)}, f32[136,128]{1,0:T(8,128)S(1)}, u32[]{:S(2)}, u32[]{:S(2)}) %collective-permute-start.4) | collective-permute-done | bytes 69664 | tf_op jit(solution)/shard_map/ppermute | solution.py:545
  42.8 1.6 %collective-permute-start.8 = (f32[16,128]{1,0:T(8,128)S(1)}, f32[16,128]{1,0:T(8,128)S(1)}, u32[]{:S(2)}, u32[]{:S(2)}) collective-permute-start(f32[16,128]{1,0:T(8,128)S(1)} %pad_maximum_fusion.refs_0_), channel_id=1, source_target_pairs={{0,2},{1,3},{2,0},{3,1},{4,6},{5,7},{6,4},{7,5},{8,10},{9,11},{10,... | collective-permute-start | bytes 24584 | tf_op jit(solution)/shard_map/ppermute | solution.py:563
  44.5 2.8 %taper_tables.1 = (f32[33,32,128]{2,1,0:T(8,128)S(1)}, f32[32,128]{1,0:T(8,128)S(1)}, f32[32,8,128]{2,1,0:T(8,128)S(1)}, s32[8,128]{1,0:T(8,128)S(1)}) custom-call(s32[2,16]{1,0:T(2,128)S(1)} %copy-done, f32[2,16]{1,0:T(2,128)S(1)} %copy-done.1, f32[2,16]{1,0:T(2,128)S(1)} %copy-done.2), custom_call_target="tpu_custom_call" | custom-call | flops 7864320 | bytes 524288 | tf_op jit(solution)/shard_map/taper_tables/pallas_call | solution.py:323
  47.4 5.7 %filter_plan.1 = (f32[33,24,128]{2,1,0:T(8,128)S(1)}, f32[33,24,128]{2,1,0:T(8,128)S(1)}, f32[128,128]{1,0:T(8,128)S(1)}, f32[128,128]{1,0:T(8,128)S(1)}, f32[12...) custom-call(f32[33,32,128]{2,1,0:T(8,128)S(1)} %get-tuple-element.37, ...), custom_call_target="tpu_custom_call" | custom-call | flops 20000000 | bytes 1048576 | tf_op jit(solution)/shard_map/filter_plan/pallas_call | solution.py:438
  54.2 2.2 %collective-permute-start.18 = (f32[128,128]{1,0:T(8,128)S(1)}, f32[128,128]{1,0:T(8,128)S(1)}, u32[]{:S(2)}, u32[]{:S(2)}) collective-permute-start(f32[128,128]{1,0:T(8,128)S(1)} %get-tuple-element.61), channel_id=1, source_target_pairs={{0,8},{4,12},{8,0},{12,4},{16,24},{20,28},{24,16},{28,20},{1,9},{5... | collective-permute-start | bytes 196616 | tf_op jit(solution)/shard_map/ppermute | solution.py:545
  57.2 2.2 %collective-permute-start.20 = (f32[128,128]{1,0:T(8,128)S(1)}, f32[128,128]{1,0:T(8,128)S(1)}, u32[]{:S(2)}, u32[]{:S(2)}) collective-permute-start(f32[128,128]{1,0:T(8,128)S(1)} %get-tuple-element.63), channel_id=1, source_target_pairs={{0,16},{4,20},{8,24},{12,28},{16,0},{20,4},{24,8},{28,12},{1,17},{... | collective-permute-start | bytes 196616 | tf_op jit(solution)/shard_map/ppermute | solution.py:545
  59.4 3.9 %settle.1 = (f32[192,128]{1,0:T(8,128)S(1)}, f32[192,128]{1,0:T(8,128)S(1)}, f32[192,128]{1,0:T(8,128)S(1)}, f32[192,128]{1,0:T(8,128)S(1)}, f32[192,128]{1,0:T(...) custom-call(s32[8,128]{1,0:T(8,128)S(1)} %get-tuple-element.36.lists_ref, ...), custom_call_target="tpu_custom_call" | custom-call | flops 25952256 | bytes 1572864 | tf_op jit(solution)/shard_map/settle/pallas_call | solution.py:466
  63.9 3.6 %collective-permute-start.21 = (f32[128,128]{1,0:T(8,128)S(1)}, f32[128,128]{1,0:T(8,128)S(1)}, u32[]{:S(2)}, u32[]{:S(2)}) collective-permute-start(f32[128,128]{1,0:T(8,128)S(1)} %get-tuple-element.64), channel_id=1, source_target_pairs={{0,20},{4,16},{8,28},{12,24},{16,4},{20,0},{24,12},{28,8},{1,21},{... | collective-permute-start | bytes 196616 | tf_op jit(solution)/shard_map/ppermute | solution.py:545
  67.5 1.6 %collective-permute-start.22 = (f32[128,128]{1,0:T(8,128)S(1)}, f32[128,128]{1,0:T(8,128)S(1)}, u32[]{:S(2)}, u32[]{:S(2)}) collective-permute-start(f32[128,128]{1,0:T(8,128)S(1)} %get-tuple-element.65), channel_id=1, source_target_pairs={{0,24},{4,28},{8,16},{12,20},{16,8},{20,12},{24,0},{28,4},{1,25},{... | collective-permute-start | bytes 196616 | tf_op jit(solution)/shard_map/ppermute | solution.py:545
  69.2 2.3 %collective-permute-start.23 = (f32[128,128]{1,0:T(8,128)S(1)}, f32[128,128]{1,0:T(8,128)S(1)}, u32[]{:S(2)}, u32[]{:S(2)}) collective-permute-start(f32[128,128]{1,0:T(8,128)S(1)} %get-tuple-element.66), channel_id=1, source_target_pairs={{0,28},{4,24},{8,20},{12,16},{16,12},{20,8},{24,4},{28,0},{1,29},{... | collective-permute-start | bytes 196616 | tf_op jit(solution)/shard_map/ppermute | solution.py:545
  74.3 3.5 %collective-permute-start.13 = (f32[192,128]{1,0:T(8,128)S(1)}, f32[192,128]{1,0:T(8,128)S(1)}, u32[]{:S(2)}, u32[]{:S(2)}) collective-permute-start(f32[192,128]{1,0:T(8,128)S(1)} %get-tuple-element.55), channel_id=1, source_target_pairs={{0,16},{4,20},{8,24},{12,28},{16,0},{20,4},{24,8},{28,12},{1,17},{... | collective-permute-start | bytes 294920 | tf_op jit(solution)/shard_map/ppermute | solution.py:545
  77.9 2.8 %collective-permute-start.14 = (f32[192,128]{1,0:T(8,128)S(1)}, f32[192,128]{1,0:T(8,128)S(1)}, u32[]{:S(2)}, u32[]{:S(2)}) collective-permute-start(f32[192,128]{1,0:T(8,128)S(1)} %get-tuple-element.56), channel_id=1, source_target_pairs={{0,20},{4,16},{8,28},{12,24},{16,4},{20,0},{24,12},{28,8},{1,21},{... | collective-permute-start | bytes 294920 | tf_op jit(solution)/shard_map/ppermute | solution.py:545
  80.7 1.9 %collective-permute-start.15 = (f32[192,128]{1,0:T(8,128)S(1)}, f32[192,128]{1,0:T(8,128)S(1)}, u32[]{:S(2)}, u32[]{:S(2)}) collective-permute-start(f32[192,128]{1,0:T(8,128)S(1)} %get-tuple-element.57), channel_id=1, source_target_pairs={{0,24},{4,28},{8,16},{12,20},{16,8},{20,12},{24,0},{28,4},{1,25},{... | collective-permute-start | bytes 294920 | tf_op jit(solution)/shard_map/ppermute | solution.py:545
  84.9 4.0 %collective-permute-done.13.refs_4_ = f32[192,128]{1,0:T(8,128)S(1)} collective-permute-done((f32[192,128]{1,0:T(8,128)S(1)}, f32[192,128]{1,0:T(8,128)S(1)}, u32[]{:S(2)}, u32[]{:S(2)}) %collective-permute-start.13) | collective-permute-done | bytes 98336 | tf_op jit(solution)/shard_map/ppermute | solution.py:545
  88.9 2.1 %collective-permute-done.14.refs_5_ = f32[192,128]{1,0:T(8,128)S(1)} collective-permute-done((f32[192,128]{1,0:T(8,128)S(1)}, f32[192,128]{1,0:T(8,128)S(1)}, u32[]{:S(2)}, u32[]{:S(2)}) %collective-permute-start.14) | collective-permute-done | bytes 98336 | tf_op jit(solution)/shard_map/ppermute | solution.py:545
  (41 shorter events, 11.4 us)
Async XLA Ops:
  4.3 55.1 %all-to-all-start = ((f32[8,192,128]{2,1,0:T(8,128)}), f32[8,192,128]{2,1,0:T(8,128)S(1)}, u32[]{:S(2)}, u32[]{:S(2)}) async-start(f32[8,192,128]{2,1,0:T(8,128)} %get-tuple-element.50), calls=%async_computation | async-start | bytes 1572864 | tf_op jit(solution)/shard_map/all_to_all | solution.py:542
  11.7 8.8 %collective-permute-start = (f32[136,128]{1,0:T(8,128)S(1)}, f32[136,128]{1,0:T(8,128)S(1)}, u32[]{:S(2)}, u32[]{:S(2)}) collective-permute-start(f32[136,128]{1,0:T(8,128)S(1)} %get-tuple-element.41), channel_id=1, source_target_pairs={{0,4},{4,0},{8,12},{12,8},{16,20},{20,16},{24,28},{28,24},{1,5},{5... | collective-permute-start | bytes 208904 | tf_op jit(solution)/shard_map/ppermute | solution.py:545
  13.8 13.4 %collective-permute-start.1 = (f32[136,128]{1,0:T(8,128)S(1)}, f32[136,128]{1,0:T(8,128)S(1)}, u32[]{:S(2)}, u32[]{:S(2)}) collective-permute-start(f32[136,128]{1,0:T(8,128)S(1)} %get-tuple-element.42), channel_id=1, source_target_pairs={{0,8},{4,12},{8,0},{12,4},{16,24},{20,28},{24,16},{28,20},{1,9},{5... | collective-permute-start | bytes 208904 | tf_op jit(solution)/shard_map/ppermute | solution.py:545
  15.2 16.7 %collective-permute-start.2 = (f32[136,128]{1,0:T(8,128)S(1)}, f32[136,128]{1,0:T(8,128)S(1)}, u32[]{:S(2)}, u32[]{:S(2)}) collective-permute-start(f32[136,128]{1,0:T(8,128)S(1)} %get-tuple-element.43), channel_id=1, source_target_pairs={{0,12},{4,8},{8,4},{12,0},{16,28},{20,24},{24,20},{28,16},{1,13},{... | collective-permute-start | bytes 208904 | tf_op jit(solution)/shard_map/ppermute | solution.py:545
  15.3 25.5 %collective-permute-start.3 = (f32[136,128]{1,0:T(8,128)S(1)}, f32[136,128]{1,0:T(8,128)S(1)}, u32[]{:S(2)}, u32[]{:S(2)}) collective-permute-start(f32[136,128]{1,0:T(8,128)S(1)} %get-tuple-element.44), channel_id=1, source_target_pairs={{0,16},{4,20},{8,24},{12,28},{16,0},{20,4},{24,8},{28,12},{1,17},{... | collective-permute-start | bytes 208904 | tf_op jit(solution)/shard_map/ppermute | solution.py:545
  18.2 24.5 %collective-permute-start.4 = (f32[136,128]{1,0:T(8,128)S(1)}, f32[136,128]{1,0:T(8,128)S(1)}, u32[]{:S(2)}, u32[]{:S(2)}) collective-permute-start(f32[136,128]{1,0:T(8,128)S(1)} %get-tuple-element.45), channel_id=1, source_target_pairs={{0,20},{4,16},{8,28},{12,24},{16,4},{20,0},{24,12},{28,8},{1,21},{... | collective-permute-start | bytes 208904 | tf_op jit(solution)/shard_map/ppermute | solution.py:545
  20.6 22.1 %collective-permute-start.5 = (f32[136,128]{1,0:T(8,128)S(1)}, f32[136,128]{1,0:T(8,128)S(1)}, u32[]{:S(2)}, u32[]{:S(2)}) collective-permute-start(f32[136,128]{1,0:T(8,128)S(1)} %get-tuple-element.46), channel_id=1, source_target_pairs={{0,24},{4,28},{8,16},{12,20},{16,8},{20,12},{24,0},{28,4},{1,25},{... | collective-permute-start | bytes 208904 | tf_op jit(solution)/shard_map/ppermute | solution.py:545
  27.2 15.5 %collective-permute-start.6 = (f32[136,128]{1,0:T(8,128)S(1)}, f32[136,128]{1,0:T(8,128)S(1)}, u32[]{:S(2)}, u32[]{:S(2)}) collective-permute-start(f32[136,128]{1,0:T(8,128)S(1)} %get-tuple-element.47), channel_id=1, source_target_pairs={{0,28},{4,24},{8,20},{12,16},{16,12},{20,8},{24,4},{28,0},{1,29},{... | collective-permute-start | bytes 208904 | tf_op jit(solution)/shard_map/ppermute | solution.py:545
  42.7 4.6 %collective-permute-start.9 = (f32[16,128]{1,0:T(8,128)S(1)}, f32[16,128]{1,0:T(8,128)S(1)}, u32[]{:S(2)}, u32[]{:S(2)}) collective-permute-start(f32[16,128]{1,0:T(8,128)S(1)} %pad_maximum_fusion.refs_0_), channel_id=1, source_target_pairs={{0,3},{1,0},{2,1},{3,2},{4,7},{5,4},{6,5},{7,6},{8,11},{9,8},{10,9... | collective-permute-start | bytes 24584 | tf_op jit(solution)/shard_map/ppermute | solution.py:563
  42.8 4.6 %collective-permute-start.8 = (f32[16,128]{1,0:T(8,128)S(1)}, f32[16,128]{1,0:T(8,128)S(1)}, u32[]{:S(2)}, u32[]{:S(2)}) collective-permute-start(f32[16,128]{1,0:T(8,128)S(1)} %pad_maximum_fusion.refs_0_), channel_id=1, source_target_pairs={{0,2},{1,3},{2,0},{3,1},{4,6},{5,7},{6,4},{7,5},{8,10},{9,11},{10,... | collective-permute-start | bytes 24584 | tf_op jit(solution)/shard_map/ppermute | solution.py:563
  53.1 10.3 %collective-permute-start.17 = (f32[128,128]{1,0:T(8,128)S(1)}, f32[128,128]{1,0:T(8,128)S(1)}, u32[]{:S(2)}, u32[]{:S(2)}) collective-permute-start(f32[128,128]{1,0:T(8,128)S(1)} %get-tuple-element.60), channel_id=1, source_target_pairs={{0,4},{4,0},{8,12},{12,8},{16,20},{20,16},{24,28},{28,24},{1,5},{5... | collective-permute-start | bytes 196616 | tf_op jit(solution)/shard_map/ppermute | solution.py:545
  54.2 9.7 %collective-permute-start.18 = (f32[128,128]{1,0:T(8,128)S(1)}, f32[128,128]{1,0:T(8,128)S(1)}, u32[]{:S(2)}, u32[]{:S(2)}) collective-permute-start(f32[128,128]{1,0:T(8,128)S(1)} %get-tuple-element.61), channel_id=1, source_target_pairs={{0,8},{4,12},{8,0},{12,4},{16,24},{20,28},{24,16},{28,20},{1,9},{5... | collective-permute-start | bytes 196616 | tf_op jit(solution)/shard_map/ppermute | solution.py:545
  56.3 11.2 %collective-permute-start.19 = (f32[128,128]{1,0:T(8,128)S(1)}, f32[128,128]{1,0:T(8,128)S(1)}, u32[]{:S(2)}, u32[]{:S(2)}) collective-permute-start(f32[128,128]{1,0:T(8,128)S(1)} %get-tuple-element.62), channel_id=1, source_target_pairs={{0,12},{4,8},{8,4},{12,0},{16,28},{20,24},{24,20},{28,16},{1,13},{... | collective-permute-start | bytes 196616 | tf_op jit(solution)/shard_map/ppermute | solution.py:545
  57.2 12.0 %collective-permute-start.20 = (f32[128,128]{1,0:T(8,128)S(1)}, f32[128,128]{1,0:T(8,128)S(1)}, u32[]{:S(2)}, u32[]{:S(2)}) collective-permute-start(f32[128,128]{1,0:T(8,128)S(1)} %get-tuple-element.63), channel_id=1, source_target_pairs={{0,16},{4,20},{8,24},{12,28},{16,0},{20,4},{24,8},{28,12},{1,17},{... | collective-permute-start | bytes 196616 | tf_op jit(solution)/shard_map/ppermute | solution.py:545
  63.2 17.4 %collective-permute-start.10 = (f32[192,128]{1,0:T(8,128)S(1)}, f32[192,128]{1,0:T(8,128)S(1)}, u32[]{:S(2)}, u32[]{:S(2)}) collective-permute-start(f32[192,128]{1,0:T(8,128)S(1)} %get-tuple-element.52), channel_id=1, source_target_pairs={{0,4},{4,0},{8,12},{12,8},{16,20},{20,16},{24,28},{28,24},{1,5},{5... | collective-permute-start | bytes 294920 | tf_op jit(solution)/shard_map/ppermute | solution.py:545
  63.4 19.2 %collective-permute-start.11 = (f32[192,128]{1,0:T(8,128)S(1)}, f32[192,128]{1,0:T(8,128)S(1)}, u32[]{:S(2)}, u32[]{:S(2)}) collective-permute-start(f32[192,128]{1,0:T(8,128)S(1)} %get-tuple-element.53), channel_id=1, source_target_pairs={{0,8},{4,12},{8,0},{12,4},{16,24},{20,28},{24,16},{28,20},{1,9},{5... | collective-permute-start | bytes 294920 | tf_op jit(solution)/shard_map/ppermute | solution.py:545
  63.9 8.8 %collective-permute-start.21 = (f32[128,128]{1,0:T(8,128)S(1)}, f32[128,128]{1,0:T(8,128)S(1)}, u32[]{:S(2)}, u32[]{:S(2)}) collective-permute-start(f32[128,128]{1,0:T(8,128)S(1)} %get-tuple-element.64), channel_id=1, source_target_pairs={{0,20},{4,16},{8,28},{12,24},{16,4},{20,0},{24,12},{28,8},{1,21},{... | collective-permute-start | bytes 196616 | tf_op jit(solution)/shard_map/ppermute | solution.py:545
  67.5 6.8 %collective-permute-start.22 = (f32[128,128]{1,0:T(8,128)S(1)}, f32[128,128]{1,0:T(8,128)S(1)}, u32[]{:S(2)}, u32[]{:S(2)}) collective-permute-start(f32[128,128]{1,0:T(8,128)S(1)} %get-tuple-element.65), channel_id=1, source_target_pairs={{0,24},{4,28},{8,16},{12,20},{16,8},{20,12},{24,0},{28,4},{1,25},{... | collective-permute-start | bytes 196616 | tf_op jit(solution)/shard_map/ppermute | solution.py:545
  69.2 8.7 %collective-permute-start.23 = (f32[128,128]{1,0:T(8,128)S(1)}, f32[128,128]{1,0:T(8,128)S(1)}, u32[]{:S(2)}, u32[]{:S(2)}) collective-permute-start(f32[128,128]{1,0:T(8,128)S(1)} %get-tuple-element.66), channel_id=1, source_target_pairs={{0,28},{4,24},{8,20},{12,16},{16,12},{20,8},{24,4},{28,0},{1,29},{... | collective-permute-start | bytes 196616 | tf_op jit(solution)/shard_map/ppermute | solution.py:545
  72.7 12.2 %collective-permute-start.12 = (f32[192,128]{1,0:T(8,128)S(1)}, f32[192,128]{1,0:T(8,128)S(1)}, u32[]{:S(2)}, u32[]{:S(2)}) collective-permute-start(f32[192,128]{1,0:T(8,128)S(1)} %get-tuple-element.54), channel_id=1, source_target_pairs={{0,12},{4,8},{8,4},{12,0},{16,28},{20,24},{24,20},{28,16},{1,13},{... | collective-permute-start | bytes 294920 | tf_op jit(solution)/shard_map/ppermute | solution.py:545
  74.3 14.6 %collective-permute-start.13 = (f32[192,128]{1,0:T(8,128)S(1)}, f32[192,128]{1,0:T(8,128)S(1)}, u32[]{:S(2)}, u32[]{:S(2)}) collective-permute-start(f32[192,128]{1,0:T(8,128)S(1)} %get-tuple-element.55), channel_id=1, source_target_pairs={{0,16},{4,20},{8,24},{12,28},{16,0},{20,4},{24,8},{28,12},{1,17},{... | collective-permute-start | bytes 294920 | tf_op jit(solution)/shard_map/ppermute | solution.py:545
  77.9 13.1 %collective-permute-start.14 = (f32[192,128]{1,0:T(8,128)S(1)}, f32[192,128]{1,0:T(8,128)S(1)}, u32[]{:S(2)}, u32[]{:S(2)}) collective-permute-start(f32[192,128]{1,0:T(8,128)S(1)} %get-tuple-element.56), channel_id=1, source_target_pairs={{0,20},{4,16},{8,28},{12,24},{16,4},{20,0},{24,12},{28,8},{1,21},{... | collective-permute-start | bytes 294920 | tf_op jit(solution)/shard_map/ppermute | solution.py:545
  80.7 10.3 %collective-permute-start.15 = (f32[192,128]{1,0:T(8,128)S(1)}, f32[192,128]{1,0:T(8,128)S(1)}, u32[]{:S(2)}, u32[]{:S(2)}) collective-permute-start(f32[192,128]{1,0:T(8,128)S(1)} %get-tuple-element.57), channel_id=1, source_target_pairs={{0,24},{4,28},{8,16},{12,20},{16,8},{20,12},{24,0},{28,4},{1,25},{... | collective-permute-start | bytes 294920 | tf_op jit(solution)/shard_map/ppermute | solution.py:545
  82.6 8.4 %collective-permute-start.16 = (f32[192,128]{1,0:T(8,128)S(1)}, f32[192,128]{1,0:T(8,128)S(1)}, u32[]{:S(2)}, u32[]{:S(2)}) collective-permute-start(f32[192,128]{1,0:T(8,128)S(1)} %get-tuple-element.58), channel_id=1, source_target_pairs={{0,28},{4,24},{8,20},{12,16},{16,12},{20,8},{24,4},{28,0},{1,29},{... | collective-permute-start | bytes 294920 | tf_op jit(solution)/shard_map/ppermute | solution.py:545
  (4 other events, 123.8 us)
